TPU v7x, 32 devices: a whole 2x2x4 slice. The times are simulated.
32 devices in a mesh: dp: 4 (over z), row: 2 (over x), col: 4 (over y, core).
Axes of the slice: x: 2, y: 2, z: 4, core: 2. Of those that a mesh axis runs over, the one named last changes fastest.
Arguments:
- block_input: bfloat16 [8192, 768], P(('dp', 'col'), 'row'), may hold values from -6 to 6
- w_qkv: bfloat16 [768, 2304], P('row', 'col'), may hold values from -0.21875 to 0.21875
- b_qkv: float32 [2304], P('col'), may hold values from -3 to 3
- w_in: bfloat16 [768, 3072], P('row', 'col'), may hold values from -0.21875 to 0.21875
- b_in: float32 [3072], P('col'), may hold values from -3 to 3
- w_dense: bfloat16 [768, 768], P('col', 'row'), may hold values from -1.75 to 1.75
- b_dense: float32 [768], P('row'), may hold values from -3 to 3
- w_out: bfloat16 [3072, 768], P('col', 'row'), may hold values from -0.109375 to 0.109375
- b_out: float32 [768], P('row'), may hold values from -3 to 3
- ln_attn_gain: float32 [768], P('row'), may hold values from 0.1 to 1.9
- ln_attn_bias: float32 [768], P('row'), may hold values from -2 to 2
- ln_mlp_gain: float32 [768], P('row'), may hold values from 0.1 to 1.9
- ln_mlp_bias: float32 [768], P('row'), may hold values from -2 to 2
- segments: int32 [8192], P('dp'), may hold values from 0 to 6, as said below
- positions: int32 [8192], P('dp'), may hold values from 0 to 1023, as said below
- d_out: bfloat16 [8192, 768], P(('dp', 'col'), 'row'), may hold values from -20 to 20
Outputs:
- block_output: bfloat16 [8192, 768], P(('dp', 'col'), 'row')
- d_input: float32 [8192, 768], P(('dp', 'col'), 'row')
- grad_w_qkv: float32 [768, 2304], P('row', 'col')
- grad_b_qkv: float32 [2304], P('col')
- grad_w_in: float32 [768, 3072], P('row', 'col')
- grad_b_in: float32 [3072], P('col')
- grad_w_dense: float32 [768, 768], P('col', 'row')
- grad_b_dense: float32 [768], P('row')
- grad_w_out: float32 [3072, 768], P('col', 'row')
- grad_b_out: float32 [768], P('row')
- grad_attn_gain: float32 [768], P('row')
- grad_attn_bias: float32 [768], P('row')
- grad_mlp_gain: float32 [768], P('row')
- grad_mlp_bias: float32 [768], P('row')
Inputs may be any that keep to these rules, and one draw needn't show every extreme that they name: `segments`: the segment numbers of each aligned sequence of 1024 tokens start at 0 and rise by 0 or 1 from one token to the next; a document within a sequence that does not touch the sequence's ends has at least 204 tokens. `positions`: A token's position counts the tokens before it in its segment.
All inputs are finite; a program needn't handle non-finite values.
Results may differ from a plain program's by a relative error of at most 0.0093.
Values may be sent and summed in bfloat16 or wider, within the bound.
No kernel may reach another device: no remote copies, remote signals or barrier semaphores. Data moves between devices by JAX's collectives and lax.ppermute only.
A program may use at most 128 MiB of HBM per device.

v0:
```python
import math

import jax
import jax.numpy as jnp
from jax import lax
from jax.sharding import PartitionSpec as P

D = 768
HEAD_DIM = 64
ROT = 16
SEQ_LEN = 1024


EPSILON = 1e-05


def dot_plain(left_side, right_side):
    return jnp.dot(left_side, right_side, preferred_element_type=jnp.float32)


def dot_first(left_side, right_side):
    return lax.dot_general(
        left_side, right_side, (((0,), (0,)), ((), ())), preferred_element_type=jnp.float32
    )


def dot_second(left_side, right_side):
    return lax.dot_general(
        left_side, right_side, (((1,), (1,)), ((), ())), preferred_element_type=jnp.float32
    )


def rotary_tables(positions):
    half_rot = ROT // 2
    freq_steps = jnp.arange(half_rot, dtype=jnp.float32) * (-2.0 * math.log(10000.0) / ROT)
    angles = positions.astype(jnp.float32)[:, None] * jnp.exp(freq_steps)[None, :]
    cos_table = jnp.concatenate([jnp.cos(angles), jnp.cos(angles)], axis=1)
    sin_table = jnp.concatenate([jnp.sin(angles), jnp.sin(angles)], axis=1)
    return (cos_table, sin_table)


def rotate_heads(joined, cos_table, sin_table):
    half_rot = ROT // 2
    cos_rows = cos_table[:, None, :]
    sin_rows = sin_table[:, None, :]

    def turned_member(member):
        leading = member[..., :ROT]
        swapped = jnp.concatenate([-leading[..., half_rot:], leading[..., :half_rot]], axis=-1)
        return jnp.concatenate(
            [leading * cos_rows + swapped * sin_rows, member[..., ROT:]], axis=-1
        )

    return jnp.stack(
        [turned_member(joined[:, :, 0]), turned_member(joined[:, :, 1]), joined[:, :, 2]], axis=2
    )


def gelu_exact(pre_value):
    return jax.nn.gelu(pre_value, approximate=False)


def gelu_back(pre_act, upstream):
    return jax.vjp(gelu_exact, pre_act)[1](upstream)[0]


def block_mask(seg_ids, row_start, row_count):
    places = jnp.arange(seg_ids.shape[0])
    query_places = row_start + jnp.arange(row_count)
    query_segs = seg_ids[row_start : row_start + row_count]
    return (places[None, :] <= query_places[:, None]) & (seg_ids[None, :] == query_segs[:, None])


def block_scores(query_rows, key_rows, seg_ids, row_start, row_count):
    score_scale = HEAD_DIM ** (-0.5)
    scores = (
        jnp.einsum("qhd,khd->hqk", query_rows, key_rows, preferred_element_type=jnp.float32)
        * score_scale
    )
    allowed = block_mask(seg_ids, row_start, row_count)
    return jnp.where(allowed[None], scores, -jnp.inf)


def attend_forward(operands):
    joined_seq, seg_ids = operands
    query_all = joined_seq[:, :, 0]
    key_rows = joined_seq[:, :, 1]
    value_rows = joined_seq[:, :, 2]
    block_rows = min(512, SEQ_LEN)
    outputs = []
    maxima = []
    totals = []
    for row_start in range(0, SEQ_LEN, block_rows):
        query_rows = query_all[row_start : row_start + block_rows]
        scores = block_scores(query_rows, key_rows, seg_ids, row_start, block_rows)
        row_max = jnp.max(scores, axis=-1, keepdims=True)
        shifted = jnp.exp(scores - row_max)
        row_total = jnp.sum(shifted, axis=-1, keepdims=True)
        probs_low = (shifted / row_total).astype(jnp.bfloat16)
        outputs.append(
            jnp.einsum("hqk,khd->qhd", probs_low, value_rows, preferred_element_type=jnp.float32)
        )
        maxima.append(row_max)
        totals.append(row_total)
    return (
        jnp.concatenate(outputs, axis=0),
        jnp.concatenate(maxima, axis=1),
        jnp.concatenate(totals, axis=1),
    )


def attend_backward(operands):
    joined_seq, seg_ids, maxima, totals, grad_context = operands
    score_scale = HEAD_DIM ** (-0.5)
    query_all = joined_seq[:, :, 0]
    key_rows = joined_seq[:, :, 1]
    value_rows = joined_seq[:, :, 2]
    block_rows = min(512, SEQ_LEN)
    grad_keys = jnp.zeros(key_rows.shape, jnp.float32)
    grad_values = jnp.zeros(value_rows.shape, jnp.float32)
    grad_queries = []
    for row_start in range(0, SEQ_LEN, block_rows):
        query_rows = query_all[row_start : row_start + block_rows]
        grad_rows = grad_context[row_start : row_start + block_rows]
        scores = block_scores(query_rows, key_rows, seg_ids, row_start, block_rows)
        row_max = maxima[:, row_start : row_start + block_rows]
        row_total = totals[:, row_start : row_start + block_rows]
        attn_probs = jnp.exp(scores - row_max) / row_total
        probs_low = attn_probs.astype(jnp.bfloat16)
        grad_probs = jnp.einsum(
            "qhd,khd->hqk", grad_rows, value_rows, preferred_element_type=jnp.float32
        )
        inner_term = jnp.sum(grad_probs * attn_probs, axis=-1, keepdims=True)
        grad_scores = (attn_probs * (grad_probs - inner_term)).astype(jnp.bfloat16)
        grad_queries.append(
            jnp.einsum("hqk,khd->qhd", grad_scores, key_rows, preferred_element_type=jnp.float32)
            * score_scale
        )
        grad_keys = (
            grad_keys
            + jnp.einsum(
                "hqk,qhd->khd", grad_scores, query_rows, preferred_element_type=jnp.float32
            )
            * score_scale
        )
        grad_values = grad_values + jnp.einsum(
            "hqk,qhd->khd", probs_low, grad_rows, preferred_element_type=jnp.float32
        )
    return jnp.stack([jnp.concatenate(grad_queries, axis=0), grad_keys, grad_values], axis=2)


def local(
    block_input,
    w_qkv,
    b_qkv,
    w_in,
    b_in,
    w_dense,
    b_dense,
    w_out,
    b_out,
    ln_attn_gain,
    ln_attn_bias,
    ln_mlp_gain,
    ln_mlp_bias,
    segments,
    positions,
    d_out,
):
    inputs_f = block_input.astype(jnp.float32)
    sum_first, sum_square = lax.psum(
        (jnp.sum(inputs_f, axis=1), jnp.sum(inputs_f * inputs_f, axis=1)), "row"
    )
    mean_row = (sum_first / D)[:, None]
    inv_std = lax.rsqrt(sum_square[:, None] / D - mean_row * mean_row + EPSILON)
    normed = (inputs_f - mean_row) * inv_std
    h_attn = (normed * ln_attn_gain + ln_attn_bias).astype(jnp.bfloat16)
    h_mlp = (normed * ln_mlp_gain + ln_mlp_bias).astype(jnp.bfloat16)
    attn_rows, mlp_rows, grad_rows_all = (
        lax.all_gather(h_attn, "col", axis=0, tiled=True),
        lax.all_gather(h_mlp, "col", axis=0, tiled=True),
        lax.all_gather(d_out, "col", axis=0, tiled=True),
    )
    group_rows = attn_rows.shape[0]
    joined_width = w_qkv.shape[1]
    heads_here = joined_width // (3 * HEAD_DIM)
    own_rows = group_rows // lax.axis_size("col")
    attn_in, mlp_in, grad_in = (attn_rows, mlp_rows, grad_rows_all)
    cos_table, sin_table = rotary_tables(positions)
    joined_sum, pre_sum = lax.psum((dot_plain(attn_rows, w_qkv), dot_plain(mlp_rows, w_in)), "row")
    local_rows = joined_sum.shape[0]
    joined = (joined_sum + b_qkv).reshape(local_rows, heads_here, 3, HEAD_DIM)
    turned = (
        rotate_heads(joined, cos_table, sin_table)
        .reshape(local_rows, joined_width)
        .astype(jnp.bfloat16)
    )
    pre_act = pre_sum + b_in
    hidden = gelu_exact(pre_act).astype(jnp.bfloat16)
    seq_count = local_rows // SEQ_LEN
    joined_seq = turned.reshape(seq_count, SEQ_LEN, heads_here, 3, HEAD_DIM)
    seg_seq = segments.reshape(seq_count, SEQ_LEN)
    context, maxima, totals = lax.map(attend_forward, (joined_seq, seg_seq))
    context_low = context.reshape(local_rows, heads_here * HEAD_DIM).astype(jnp.bfloat16)
    ctx_part = lax.slice_in_dim(context_low, 0, lax.axis_size("col") * own_rows, axis=0)
    mixed = lax.psum_scatter(
        dot_plain(ctx_part, w_dense) + dot_plain(hidden, w_out),
        "col",
        scatter_dimension=0,
        tiled=True,
    )
    block_output = (inputs_f + mixed + b_dense + b_out).astype(jnp.bfloat16)
    grad_w_dense = dot_first(context_low, grad_in)
    grad_w_out = dot_first(hidden, grad_in)
    grad_ctx, grad_hidden = lax.psum(
        (dot_second(grad_in, w_dense), dot_second(grad_in, w_out)), "row"
    )
    grad_ctx_low = grad_ctx.astype(jnp.bfloat16)
    grad_pre_low = gelu_back(pre_act, grad_hidden).astype(jnp.bfloat16)
    grad_seq = grad_ctx_low.reshape(seq_count, SEQ_LEN, heads_here, HEAD_DIM)
    grad_turned = lax.map(attend_backward, (joined_seq, seg_seq, maxima, totals, grad_seq))
    grad_turned = grad_turned.reshape(local_rows, heads_here, 3, HEAD_DIM)

    def rotate_only(joined_value):
        return rotate_heads(joined_value, cos_table, sin_table)

    rotate_pull = jax.vjp(rotate_only, jnp.zeros_like(grad_turned))[1]
    grad_joined_low = (
        rotate_pull(grad_turned)[0].reshape(local_rows, joined_width).astype(jnp.bfloat16)
    )
    grad_w_qkv = dot_first(attn_in, grad_joined_low)
    grad_b_qkv = jnp.sum(grad_joined_low, axis=0, dtype=jnp.float32)
    grad_w_in = dot_first(mlp_in, grad_pre_low)
    grad_b_in = jnp.sum(grad_pre_low, axis=0, dtype=jnp.float32)
    grad_normed_both = lax.psum_scatter(
        jnp.concatenate(
            [dot_second(grad_joined_low, w_qkv), dot_second(grad_pre_low, w_in)], axis=1
        ),
        "col",
        scatter_dimension=0,
        tiled=True,
    )
    own_width = block_input.shape[1]
    grad_h_attn = grad_normed_both[:, :own_width]
    grad_h_mlp = grad_normed_both[:, own_width:]
    grad_normed = grad_h_attn * ln_attn_gain + grad_h_mlp * ln_mlp_gain
    mean_grad, mean_cross = lax.psum(
        (jnp.sum(grad_normed, axis=1), jnp.sum(grad_normed * normed, axis=1)), "row"
    )
    grad_out_f = d_out.astype(jnp.float32)
    d_input = grad_out_f + inv_std * (
        grad_normed - mean_grad[:, None] / D - normed * (mean_cross[:, None] / D)
    )
    norm_sums = lax.psum(
        (
            jnp.sum(grad_h_attn * normed, axis=0),
            jnp.sum(grad_h_attn, axis=0),
            jnp.sum(grad_h_mlp * normed, axis=0),
            jnp.sum(grad_h_mlp, axis=0),
            jnp.sum(grad_out_f, axis=0),
        ),
        ("dp", "col"),
    )
    weight_sums = lax.psum(
        (grad_w_qkv, grad_b_qkv, grad_w_in, grad_b_in, grad_w_dense, grad_w_out), "dp"
    )
    return (
        block_output,
        d_input,
        weight_sums[0],
        weight_sums[1],
        weight_sums[2],
        weight_sums[3],
        weight_sums[4],
        norm_sums[4],
        weight_sums[5],
        norm_sums[4],
        norm_sums[0],
        norm_sums[1],
        norm_sums[2],
        norm_sums[3],
    )


def solution(mesh):
    placed = (
        P(("dp", "col"), "row"),
        P("row", "col"),
        P("col"),
        P("row", "col"),
        P("col"),
        P("col", "row"),
        P("row"),
        P("col", "row"),
        P("row"),
        P("row"),
        P("row"),
        P("row"),
        P("row"),
        P("dp"),
        P("dp"),
        P(("dp", "col"), "row"),
    )
    return jax.shard_map(
        local,
        mesh=mesh,
        in_specs=placed,
        out_specs=(
            P(("dp", "col"), "row"),
            P(("dp", "col"), "row"),
            P("row", "col"),
            P("col"),
            P("row", "col"),
            P("col"),
            P("col", "row"),
            P("row"),
            P("col", "row"),
            P("row"),
            P("row"),
            P("row"),
            P("row"),
            P("row"),
        ),
        check_vma=False,
    )
```

profile of v0, /device:TPU:0, one launch (start us, length us, event | category | flops | bytes accessed | tf_op | source)
XLA Modules:
  0.0 969.6 jit_solution(11491936356633016074)
XLA Ops:
  9.3 22.8 %all-gather.8.cloned.1.call-done = bf16[2048,384]{1,0:T(8,128)(2,1)} async-done(((bf16[512,384]{1,0:T(8,128)(2,1)}), bf16[2048,384]{1,0:T(8,128)(2,1)}) %all-gather.8.cloned.1.call-update) | async-done | bytes 1572880 | tf_op jit(solution)/shard_map/all_gather | solution.py:182
  32.0 3.4 fusion.80
  35.5 42.7 %all-reduce.24 = (f32[512]{0:T(512)S(1)}, f32[512]{0:T(512)S(1)}, bf16[2048,192]{0,1:T(8,128)(2,1)S(1)}) all-reduce(f32[512]{0:T(512)S(1)} %get-tuple-element.144, f32[512]{0:T(512)S(1)} %get-tuple-element.143, f32[2048,192]{0,1:T(8,128)} %fusion.80), channel_id=1, replica_groups=mesh['dp'=4,'row'=2,'col'=4] {'row'}, use_global_device_ids=true, to_apply=%region_3.0 | all-reduce | flops 394240 | bytes 2367488 | tf_op jit(solution)/shard_map/psum | solution.py:171
  80.2 4.5 fusion.82
  84.7 13.6 %all-gather.6.cloned.1.call-done = bf16[2048,384]{1,0:T(8,128)(2,1)} async-done(((bf16[512,384]{1,0:T(8,128)(2,1)}), bf16[2048,384]{1,0:T(8,128)(2,1)}) %all-gather.6.cloned.1.call-update) | async-done | bytes 1572880 | tf_op jit(solution)/shard_map/all_gather | solution.py:181
  98.3 5.9 fusion.78
  104.3 15.9 %all-gather.4.cloned.1.call-done = bf16[2048,384]{1,0:T(8,128)(2,1)} async-done(((bf16[512,384]{1,0:T(8,128)(2,1)}), bf16[2048,384]{1,0:T(8,128)(2,1)}) %all-gather.4.cloned.1.call-update) | async-done | bytes 1572880 | tf_op jit(solution)/shard_map/all_gather | solution.py:180
  120.2 4.9 fusion.77
  127.9 388.4 %all-reduce.23.cloned.1.call-done = (f32[2048,768]{1,0:T(8,128)}, f32[2048,576]{0,1:T(8,128)}, f32[2048,768]{1,0:T(8,128)}) async-done(((f32[2048,768]{1,0:T(8,128)}, f32[2048,576]{0,1:T(8,128)}, f32[2048,768]{1,0:T(8,128)}), (f32[2048,768]{1,0:T(8,128)}, f32[2048,576]{0,1:T(8,128)}, f32[2048,768]{1,0:T(8,128)})) %all-reduce.23.cloned.1.call-update) | async-done | bytes 17301520 | tf_op jit(solution)/shard_map/psum | solution.py:190
  516.3 2.7 broadcast_add_fusion
  523.4 2.6 stack.24
  526.9 2.6 stack.25
  529.5 4.0 pad_maximum_fusion.1
  533.5 2.2 copy.63
  535.7 26.0 %while.24 = (s32[]{:T(128)}, bf16[2,1024,3,64]{1,3,2,0:T(8,128)(2,1)S(1)}, f32[2,3,1024,1]{2,1,3,0:T(4,128)S(1)}, f32[2,3,1024,1]{2,1,3,0:T(4,128)S(1)}, bf16[2,...) while((s32[]{:T(128)}, ...), condition=%wide.region_10.11_spmd, body=%wide.region_5.10_spmd.sunk | while | flops 846987776 | bytes 47612032 | solution.py:203
  546.8 2.0 fusion.141
  562.7 18.6 %convert_reduce_fusion = (f32[768]{0:T(1024)}, bf16[2048,768]{1,0:T(8,128)(2,1)}, f32[2048,768]{1,0:T(8,128)S(1)}) fusion(f32[2048,768]{1,0:T(8,128)} %get-tuple-element.189, f32[2048,768]{1,0:T(8,128)} %get-tuple-element.187, f32[768]{0:T(1024)S(1)} %copy-done.33), kind=kLoop, calls=%fused_computation.89 | loop fusion | flops 117964032 | bytes 22026240 | tf_op jit(solution)/shard_map/reduce_sum | solution.py:234
  581.4 4.1 multiply_convert_fusion.2
  589.0 2.5 convolution_add_fusion.1
  591.6 143.6 %while.25 = (s32[]{:T(128)}, f32[2,1024,3,3,64]{1,0,4,3,2:T(2,128)}, bf16[2,1024,3,3,64]{1,4,2,3,0:T(8,128)(2,1)}, s32[2,1024]{1,0:T(2,128)S(1)}, f32[2,3,1024,1...) while((s32[]{:T(128)}, ...), condition=%wide.region_17.18_spmd, body=%wide.region_14.17_spmd.sunk | while | flops 2050029056 | bytes 139908304 | solution.py:221
  596.9 2.1 multiply_reduce_fusion.5
  600.7 3.0 exponential_divide_fusion.5
  603.6 4.6 multiply_reduce_fusion.4
  608.3 5.6 multiply_convert_fusion.5
  613.9 3.1 fusion.159
  620.0 2.4 copy.111
  622.4 41.0 %dynamic_update_slice.23 = f32[2,1024,3,3,64]{1,0,4,3,2:T(2,128)} dynamic-update-slice(f32[2,1024,3,3,64]{1,0,4,3,2:T(2,128)} %get-tuple-element.421, f32[1,1024,3,3,64]{1,0,4,3,2:T(1,128)S(1)} %copy.111, s32[]{:T(128)} %get-tuple-element.420, s32[]{:T(128)} %constant.63.clone.1..sunk.1, s32[]{:T(128)} %constant.63.clone.1..sunk.1, s32[]{:T(128)} %constant.63.clone.1..sunk.1, ...) | dynamic-update-slice | bytes 4718596 | tf_op jit(solution)/shard_map/while/body/jit(dynamic_update_index_in_dim)/dynamic_update_slice | solution.py:221
  668.6 2.1 multiply_reduce_fusion.5
  672.4 2.9 exponential_divide_fusion.5
  675.3 4.6 multiply_reduce_fusion.4
  679.9 5.5 multiply_convert_fusion.5
  685.4 3.1 fusion.159
  691.5 2.4 copy.111
  694.0 41.0 %dynamic_update_slice.23 = f32[2,1024,3,3,64]{1,0,4,3,2:T(2,128)} dynamic-update-slice(f32[2,1024,3,3,64]{1,0,4,3,2:T(2,128)} %get-tuple-element.421, f32[1,1024,3,3,64]{1,0,4,3,2:T(1,128)S(1)} %copy.111, s32[]{:T(128)} %get-tuple-element.420, s32[]{:T(128)} %constant.63.clone.1..sunk.1, s32[]{:T(128)} %constant.63.clone.1..sunk.1, s32[]{:T(128)} %constant.63.clone.1..sunk.1, ...) | dynamic-update-slice | bytes 4718596 | tf_op jit(solution)/shard_map/while/body/jit(dynamic_update_index_in_dim)/dynamic_update_slice | solution.py:221
  735.2 7.4 reshape.300
  742.6 2.8 slice_bitcast_fusion.30
  752.1 3.1 pad_maximum_fusion
  758.1 4.6 fusion.87
  762.7 2.4 fusion.84
  765.2 2.8 fusion.86
  768.2 12.5 %all-reduce.12 = (f32[576]{0:T(1024)}, f32[768]{0:T(1024)}) all-reduce(f32[576]{0:T(1024)S(1)} %reduce_sum.142, f32[768]{0:T(1024)S(1)} %copy-done.34), channel_id=1, replica_groups=mesh['dp'=4,'row'=2,'col'=4] {'dp'}, use_global_device_ids=true, to_apply=%region_26.27 | all-reduce | flops 1344 | bytes 10752 | tf_op jit(solution)/shard_map/psum | solution.py:264
  780.7 34.7 %reduce-scatter.5.cloned.1.call-done = f32[512,768]{1,0:T(8,128)} async-done(((f32[2048,768]{1,0:T(8,128)}), f32[512,768]{1,0:T(8,128)}) %reduce-scatter.5.cloned.1.call-update) | async-done | bytes 1572880 | tf_op jit(solution)/shard_map/reduce_scatter | solution.py:235
  815.5 3.0 slice_reduce_fusion
  818.4 4.9 all-reduce.14
  824.6 63.1 %all-reduce.11 = (f32[384]{0:T(512)S(1)}, f32[384]{0:T(512)}, f32[384]{0:T(512)}, f32[384]{0:T(512)}, f32[384]{0:T(512)}) all-reduce(f32[384]{0:T(512)S(1)} %get-tuple-element.235, f32[384]{0:T(512)S(1)} %get-tuple-element.139, f32[384]{0:T(512)S(1)} %get-tuple-element.138, ...), channel_id=1, replica_groups=mesh['dp'=4,'row'=2,'col'=4] {'dp','col'}, use_global_device_ids=true, to_apply=%region_32.33 | all-reduce | flops 1920 | bytes 15360 | tf_op jit(solution)/shard_map/psum | solution.py:254
  887.7 67.0 %all-reduce.21.cloned.1.call-done = (f32[384,576]{0,1:T(8,128)}, f32[384,768]{1,0:T(8,128)}, f32[192,384]{1,0:T(8,128)}, f32[768,384]{1,0:T(8,128)}) async-done(((f32[384,576]{0,1:T(8,128)}, f32[384,768]{1,0:T(8,128)}, f32[192,384]{1,0:T(8,128)}, f32[768,384]{1,0:T(8,128)}), (f32[384,576]{0,1:T(8,128)}, f32[384,768]{1,0:T(8,128)}, f32[192,384]{1,0:T(8,128)}, ...) | async-done | bytes 3538960 | tf_op jit(solution)/shard_map/psum | solution.py:264
  955.3 2.1 copy.147
  957.4 2.4 copy.148
  (222 shorter events, 73.5 us)
Async XLA Ops:
  7.2 73.0 %copy-start = (bf16[768,384]{1,0:T(8,128)(2,1)S(1)}, bf16[768,384]{1,0:T(8,128)(2,1)}, u32[]{:S(2)}) copy-start(bf16[768,384]{1,0:T(8,128)(2,1)} %param.27) | copy-start | bytes 1769476
  7.2 71.0 %copy-start.10 = (bf16[512,384]{1,0:T(8,128)(2,1)S(1)}, bf16[512,384]{1,0:T(8,128)(2,1)}, u32[]{:S(2)}) copy-start(bf16[512,384]{1,0:T(8,128)(2,1)} %param.20) | copy-start | bytes 1179652
  7.2 71.0 %copy-start.35 = (f32[384]{0:T(512)S(1)}, f32[384]{0:T(512)}, u32[]{:S(2)}) copy-start(f32[384]{0:T(512)} %param.29) | copy-start | bytes 4612
  7.2 71.0 %copy-start.42 = (f32[384]{0:T(512)S(1)}, f32[384]{0:T(512)}, u32[]{:S(2)}) copy-start(f32[384]{0:T(512)} %param.30) | copy-start | bytes 4612
  7.2 71.0 %copy-start.37 = (f32[384]{0:T(512)S(1)}, f32[384]{0:T(512)}, u32[]{:S(2)}) copy-start(f32[384]{0:T(512)} %param.31) | copy-start | bytes 4612
  7.2 71.0 %copy-start.43 = (f32[384]{0:T(512)S(1)}, f32[384]{0:T(512)}, u32[]{:S(2)}) copy-start(f32[384]{0:T(512)} %param.32) | copy-start | bytes 4612
  7.3 24.8 %all-gather.8.cloned.1.call-start = ((), (), s32[]{:S(2)}) async-start(), calls=%async_computation.5 | async-start | bytes 1966080 | tf_op jit(solution)/shard_map/all_gather | solution.py:182
  8.0 90.4 %all-gather.6.cloned.1.call-start = ((), (), s32[]{:S(2)}) async-start(), calls=%async_computation.3 | async-start | bytes 1966080 | tf_op jit(solution)/shard_map/all_gather | solution.py:181
  32.0 48.2 %copy-start.3 = (bf16[2048,384]{1,0:T(8,128)(2,1)S(1)}, bf16[2048,384]{1,0:T(8,128)(2,1)}, u32[]{:S(2)}) copy-start(bf16[2048,384]{1,0:T(8,128)(2,1)} %all-gather.8.cloned.1.call-done) | copy-start | bytes 4718596
  79.4 40.7 %all-gather.4.cloned.1.call-start = ((), (), s32[]{:S(2)}) async-start(), calls=%async_computation.2 | async-start | bytes 1966080 | tf_op jit(solution)/shard_map/all_gather | solution.py:180
  80.2 436.1 %all-reduce.23.cloned.1.call-start = ((), (), s32[]{:S(2)}) async-start(), calls=%async_computation.8 | async-start | bytes 34603008 | tf_op jit(solution)/shard_map/psum | solution.py:190
  84.7 35.5 %copy-start.25 = (bf16[384,576]{0,1:T(8,128)(2,1)S(1)}, bf16[384,576]{0,1:T(8,128)(2,1)}, u32[]{:S(2)}) copy-start(bf16[384,576]{0,1:T(8,128)(2,1)} %param.21) | copy-start | bytes 1327108
  125.1 391.2 %copy-start.41 = (f32[576]{0:T(1024)S(1)}, f32[576]{0:T(1024)}, u32[]{:S(2)}) copy-start(f32[576]{0:T(1024)} %param.22) | copy-start | bytes 6916
  125.1 655.6 %reduce-scatter.3.cloned.1.call-start = ((), (), s32[]{:S(2)}) async-start(), calls=%async_computation.4 | async-start | bytes 3932160 | tf_op jit(solution)/shard_map/reduce_scatter | solution.py:206
  126.2 393.9 %copy-start.17 = (f32[2048,16]{0,1:T(8,128)}, f32[2048,16]{0,1:T(8,128)S(1)}, u32[]{:S(2)}) copy-start(f32[2048,16]{0,1:T(8,128)S(1)} %get-tuple-element.253) | copy-start | bytes 393220
  126.2 393.9 %copy-start.20 = (f32[2048,16]{0,1:T(8,128)}, f32[2048,16]{0,1:T(8,128)S(1)}, u32[]{:S(2)}) copy-start(f32[2048,16]{0,1:T(8,128)S(1)} %get-tuple-element.254) | copy-start | bytes 393220
  529.4 6.2 copy-start.27
  529.4 6.2 copy-start.28
  533.5 2.2 copy-start.22
  535.6 27.1 %copy-start.33 = (f32[768]{0:T(1024)S(1)}, f32[768]{0:T(1024)}, u32[]{:S(2)}) copy-start(f32[768]{0:T(1024)} %param.24) | copy-start | bytes 9220
  562.7 26.3 %copy-start.8 = (bf16[24,8,2,1024]{3,1,2,0:T(8,128)(2,1)}, bf16[24,8,2,1024]{3,1,2,0:T(8,128)(2,1)S(1)}, u32[]{:S(2)}) copy-start(bf16[24,8,2,1024]{3,1,2,0:T(8,128)(2,1)S(1)} %copy.105) | copy-start | bytes 2359300
  585.5 1.7 copy-start.6
  587.1 1.8 copy-start.24
  591.5 223.9 %reduce-scatter.5.cloned.1.call-start = ((), (), s32[]{:S(2)}) async-start(), calls=%async_computation.6 | async-start | bytes 7864320 | tf_op jit(solution)/shard_map/reduce_scatter | solution.py:235
  613.9 3.2 copy-start.2
  617.1 1.4 copy-start.5
  685.4 3.2 copy-start.2
  747.3 2.2 copy-start.15
  747.3 2.8 copy-start.12
  747.3 2.9 copy-start.23
  755.2 1.4 copy-start.4
  755.2 1.6 copy-start.9
  755.2 199.5 %all-reduce.21.cloned.1.call-start = ((), (), s32[]{:S(2)}) async-start(), calls=%async_computation.7 | async-start | bytes 7077888 | tf_op jit(solution)/shard_map/psum | solution.py:264
  758.1 4.6 copy-start.13
  758.1 4.6 copy-start.14
  762.7 2.5 copy-start.7
  765.1 3.0 copy-start.34
  765.1 50.3 %copy-start.11 = (bf16[512,384]{1,0:T(8,128)(2,1)S(1)}, bf16[512,384]{1,0:T(8,128)(2,1)}, u32[]{:S(2)}) copy-start(bf16[512,384]{1,0:T(8,128)(2,1)} %param.20) | copy-start | bytes 1179652
  765.1 50.3 %copy-start.30 = (f32[512]{0:T(512)S(1)}, f32[512]{0:T(512)}, u32[]{:S(2)}) copy-start(f32[512]{0:T(512)} %copy-done.29) | copy-start | bytes 6148
  765.1 50.3 %copy-start.32 = (f32[512]{0:T(512)S(1)}, f32[512]{0:T(512)}, u32[]{:S(2)}) copy-start(f32[512]{0:T(512)} %copy-done.31) | copy-start | bytes 6148
  765.1 50.3 %copy-start.36 = (f32[384]{0:T(512)S(1)}, f32[384]{0:T(512)}, u32[]{:S(2)}) copy-start(f32[384]{0:T(512)} %param.29) | copy-start | bytes 4612
  765.2 50.3 %copy-start.38 = (f32[384]{0:T(512)S(1)}, f32[384]{0:T(512)}, u32[]{:S(2)}) copy-start(f32[384]{0:T(512)} %param.31) | copy-start | bytes 4612
  765.2 50.3 %copy-start.44 = (f32[384]{0:T(512)S(1)}, f32[384]{0:T(512)}, u32[]{:S(2)}) copy-start(f32[384]{0:T(512)} %param.28) | copy-start | bytes 4612
  765.2 50.3 %copy-start.45 = (f32[384]{0:T(512)S(1)}, f32[384]{0:T(512)}, u32[]{:S(2)}) copy-start(f32[384]{0:T(512)} %param.26) | copy-start | bytes 4612
  768.0 55.3 %copy-start.16 = (bf16[512,384]{1,0:T(8,128)(2,1)S(1)}, bf16[512,384]{1,0:T(8,128)(2,1)}, u32[]{:S(2)}) copy-start(bf16[512,384]{1,0:T(8,128)(2,1)} %param.35) | copy-start | bytes 1179652
  823.4 139.1 %copy-start.1 = (bf16[768,384]{1,0:T(8,128)(2,1)S(1)}, bf16[768,384]{1,0:T(8,128)(2,1)}, u32[]{:S(2)}) copy-start(bf16[768,384]{1,0:T(8,128)(2,1)} %param.27) | copy-start | bytes 1769476
  887.7 74.8 %copy-start.46 = (f32[384]{0:T(512)}, f32[384]{0:T(512)S(1)}, u32[]{:S(2)}) copy-start(f32[384]{0:T(512)S(1)} %get-tuple-element.475) | copy-start | bytes 4612
  954.7 6.8 copy-start.19
  (8 other events, 8.2 us)
Sparse Core Ops, SparseCore 0:
  9.6 22.3 all-gather.7
  79.6 18.7 all-gather.5
  100.5 19.6 all-gather.3
  125.3 391.0 all-reduce.22
  591.6 39.4 reduce-scatter.2
  755.4 60.0 reduce-scatter.4
  819.2 135.4 all-reduce.20
where the time goes:
time: 981 us; the launch traced here: 970 us
  waiting for transfers between devices  544 us (55%)
  local copies, waits for them, and re-layouts  129 us (13%)
  blocking collectives  123 us (13%)
  matrix products  88 us (9%)
  other arithmetic  68.6 us (7%)
  between operations  15.1 us (2%)
    psum x1, waiting for transfers between devices, local(): lax.psum((dot_plain(attn_rows, w_qkv), dot_plain(mlp_rows, w_in)), 'row')  388 us
    dynamic_update_slice x4, local copies, waits for them, and re-layouts, local(): lax.map(attend_backward, (joined_seq, seg_seq, maxima, totals, grad_seq))  86.8 us
    psum x1, waiting for transfers between devices, local(): lax.psum((grad_w_qkv, grad_b_qkv, grad_w_in, grad_b_in, grad_w_dense, gra...  67 us
    psum x1, blocking collectives, local(): lax.psum((jnp.sum(grad_h_attn * normed, axis=0), jnp.sum(grad_h_attn, axi...  63.1 us
    psum x1, blocking collectives, local(): lax.psum((jnp.sum(inputs_f, axis=1), jnp.sum(inputs_f * inputs_f, axis=1)...  42.7 us
    reduce_scatter x1, waiting for transfers between devices, local(): lax.psum_scatter(jnp.concatenate([dot_second(grad_joined_low, w_qkv), dot...  34.7 us
    all_gather x1, waiting for transfers between devices, local(): lax.all_gather(d_out, 'col', axis=0, tiled=True)  22.8 us
  transfers between devices with their start and end apart: 7, of which 6 were waited for; matrix products, arithmetic and copies ran while one was open for 20% of the time, Pallas kernels for 0%

commit v1 on v0

v1 whole, which is shorter than its diff:
```python
import math

import jax
import jax.numpy as jnp
from jax import lax
from jax.experimental import pallas as pl
from jax.experimental.pallas import tpu as pltpu
from jax.sharding import PartitionSpec as P

D = 768
HEAD_DIM = 64
ROT = 16
SEQ_LEN = 1024
EPSILON = 1e-05
BLOCK = 256
F32 = jnp.float32
BF16 = jnp.bfloat16
GROUP = ("row", "col")


def dot_nn(a, b):
    return lax.dot_general(a, b, (((1,), (0,)), ((), ())), preferred_element_type=F32)


def dot_tn(a, b):
    return lax.dot_general(a, b, (((0,), (0,)), ((), ())), preferred_element_type=F32)


def dot_nt(a, b):
    return lax.dot_general(a, b, (((1,), (1,)), ((), ())), preferred_element_type=F32)


def normalize(x_rows):
    x = x_rows.astype(F32)
    mean = jnp.mean(x, axis=1, keepdims=True)
    centered = x - mean
    var = jnp.mean(centered * centered, axis=1, keepdims=True)
    inv_std = lax.rsqrt(var + EPSILON)
    return centered * inv_std, inv_std


def norm_back(grad, normed, inv_std):
    mean_grad = jnp.mean(grad, axis=1, keepdims=True)
    mean_cross = jnp.mean(grad * normed, axis=1, keepdims=True)
    return inv_std * (grad - mean_grad - normed * mean_cross)


def mlp_kernel(
    x_ref, go_ref, wi_o, wi_p, wo_o, wo_p, b_ref, gain_ref, bias_ref,
    mix_ref, dx_ref, gwi_o, gwi_p, gwo_o, gwo_p, vec_ref,
    acc_ip, acc_op,
):
    step = pl.program_id(0)
    half = wi_o.shape[0]

    @pl.when(step == 0)
    def _():
        gwi_o[...] = jnp.zeros_like(gwi_o)
        gwo_o[...] = jnp.zeros_like(gwo_o)
        acc_ip[...] = jnp.zeros_like(acc_ip)
        acc_op[...] = jnp.zeros_like(acc_op)
        vec_ref[...] = jnp.zeros_like(vec_ref)

    normed, inv_std = normalize(x_ref[...])
    h = (normed * gain_ref[...] + bias_ref[...]).astype(BF16)
    go = go_ref[...]
    pre = dot_nn(h[:, :half], wi_o[...]) + dot_nn(h[:, half:], wi_p[...]) + b_ref[...]
    cdf = 0.5 * (1.0 + lax.erf(pre * (2.0 ** -0.5)))
    hidden = (pre * cdf).astype(BF16)
    slope = cdf + pre * (jnp.exp(-0.5 * pre * pre) * (1.0 / math.sqrt(2.0 * math.pi)))
    mix_ref[:, :half] = dot_nn(hidden, wo_o[...])
    mix_ref[:, half:] = dot_nn(hidden, wo_p[...])
    grad_hidden = dot_nt(go[:, :half], wo_o[...]) + dot_nt(go[:, half:], wo_p[...])
    grad_pre_f = grad_hidden * slope
    grad_pre = grad_pre_f.astype(BF16)
    gwi_o[...] += dot_tn(h[:, :half], grad_pre)
    acc_ip[...] += dot_tn(h[:, half:], grad_pre)
    gwo_o[...] += dot_tn(hidden, go[:, :half])
    acc_op[...] += dot_tn(hidden, go[:, half:])
    grad_h = jnp.concatenate([dot_nt(grad_pre, wi_o[...]), dot_nt(grad_pre, wi_p[...])], axis=1)
    vec_ref[0:1, :] += jnp.sum(grad_h * normed, axis=0, keepdims=True)
    vec_ref[1:2, :] += jnp.sum(grad_h, axis=0, keepdims=True)
    vec_ref[2:3, :] += jnp.sum(grad_pre.astype(F32), axis=0, keepdims=True)
    dx_ref[...] = norm_back(grad_h * gain_ref[...], normed, inv_std)

    @pl.when(step == pl.num_programs(0) - 1)
    def _():
        gwi_p[...] = acc_ip[...].astype(BF16)
        gwo_p[...] = acc_op[...].astype(BF16)


def mlp_branch(x_seq, go_seq, wi_o, wi_p, wo_o, wo_p, b_in, gain, bias):
    rows, width = x_seq.shape
    half, hid = wi_o.shape

    def whole(a):
        return pl.BlockSpec(a.shape, lambda i: (0,) * a.ndim)

    row_spec = pl.BlockSpec((BLOCK, width), lambda i: (i, 0))

    def shape(s, d):
        return jax.ShapeDtypeStruct(s, d)

    outs = [
        shape((rows, width), F32),
        shape((rows, width), F32),
        shape((half, hid), F32),
        shape((half, hid), BF16),
        shape((hid, half), F32),
        shape((hid, half), BF16),
        shape((8, width), F32),
    ]
    return pl.pallas_call(
        mlp_kernel,
        grid=(rows // BLOCK,),
        in_specs=[row_spec, row_spec]
        + [whole(a) for a in (wi_o, wi_p, wo_o, wo_p, b_in, gain, bias)],
        out_specs=[row_spec, row_spec] + [whole(a) for a in outs[2:]],
        out_shape=outs,
        scratch_shapes=[pltpu.VMEM((half, hid), F32), pltpu.VMEM((hid, half), F32)],
        compiler_params=pltpu.CompilerParams(
            dimension_semantics=("arbitrary",), vmem_limit_bytes=48 * 1024 * 1024
        ),
        cost_estimate=pl.CostEstimate(
            flops=12 * rows * width * hid, transcendentals=2 * rows * hid,
            bytes_accessed=24 * 1024 * 1024,
        ),
        name="mlp_branch",
    )(x_seq, go_seq, wi_o, wi_p, wo_o, wo_p, b_in, gain, bias)


def attn_kernel(
    x_ref, go_ref, w_ref, b_ref, wd_ref, cos_ref, s1_ref, s2_ref, segc_ref, segr_ref,
    gain_ref, bias_ref, mix_in, dx_in,
    mix_ref, dx_ref, gw_ref, gb_ref, gwd_ref, vec_ref,
    h_ref, mix_acc, dh_acc, qk_ref, v_ref, dctx_ref, ctxt_ref, dqt_ref, dk_ref, dv_ref, dj_ref,
):
    head = pl.program_id(0)
    last = pl.num_programs(0) - 1
    rows = x_ref.shape[0]
    tiles = rows // BLOCK

    @pl.when(head == 0)
    def _():
        @pl.loop(0, tiles)
        def _(t):
            at = pl.ds(t * BLOCK, BLOCK)
            normed, _ = normalize(x_ref[at, :])
            h_ref[at, :] = (normed * gain_ref[...] + bias_ref[...]).astype(BF16)

    lanes = lax.broadcasted_iota(jnp.int32, (1, 2 * HEAD_DIM), 1)
    scale = jnp.where(lanes < HEAD_DIM, HEAD_DIM ** (-0.5), 1.0)

    @pl.loop(0, tiles)
    def _(t):
        at = pl.ds(t * BLOCK, BLOCK)
        joined = dot_nn(h_ref[at, :], w_ref[0]) + b_ref[0]
        u = joined[:, : 2 * HEAD_DIM]
        turned = (
            u * cos_ref[at, :]
            + pltpu.roll(u, 2 * HEAD_DIM - ROT // 2, 1) * s1_ref[at, :]
            + pltpu.roll(u, ROT // 2, 1) * s2_ref[at, :]
        )
        qk_ref[at, :] = (turned * scale).astype(BF16)
        v_ref[at, :] = joined[:, 2 * HEAD_DIM :].astype(BF16)
        dctx_ref[at, :] = dot_nt(go_ref[at, :], wd_ref[0]).astype(BF16)

    qk_all = qk_ref[...]
    k_all = qk_all[:, HEAD_DIM:]
    kt = k_all.astype(F32).T.astype(BF16)
    vt = v_ref[...].astype(F32).T.astype(BF16)
    for i in range(tiles):
        lo = i * BLOCK
        hi = lo + BLOCK
        q_blk = qk_ref[lo:hi, :HEAD_DIM]
        g_blk = dctx_ref[lo:hi, :]
        st = dot_nt(k_all[:hi], q_blk)
        key_at = lax.broadcasted_iota(jnp.int32, (hi, BLOCK), 0)
        query_at = lax.broadcasted_iota(jnp.int32, (hi, BLOCK), 1) + lo
        allowed = (segc_ref[0:hi, :] == segr_ref[:, lo:hi]) & (key_at <= query_at)
        st = jnp.where(allowed, st, -1e30)
        top = jnp.max(st, axis=0, keepdims=True)
        p = jnp.exp(st - top)
        p = p * (1.0 / jnp.sum(p, axis=0, keepdims=True))
        pb = p.astype(BF16)
        ctxt_ref[:, lo:hi] = dot_nn(vt[:, :hi], pb).astype(BF16)
        dpt = dot_nt(v_ref[0:hi, :], g_blk)
        inner = jnp.sum(dpt * p, axis=0, keepdims=True)
        dst = (p * (dpt - inner)).astype(BF16)
        dqt_ref[:, lo:hi] = dot_nn(kt[:, :hi], dst)
        dk_new = dot_nn(dst, q_blk)
        dv_new = dot_nn(pb, g_blk)
        if i > 0:
            dk_ref[0:lo, :] += dk_new[:lo]
            dv_ref[0:lo, :] += dv_new[:lo]
        dk_ref[lo:hi, :] = dk_new[lo:]
        dv_ref[lo:hi, :] = dv_new[lo:]

    gwd_ref[0] = dot_nn(ctxt_ref[...], go_ref[...])
    dq = dqt_ref[...].T
    back = jnp.concatenate([dq * HEAD_DIM ** (-0.5), dk_ref[...]], axis=1)
    turned_back = (
        back * cos_ref[...]
        + pltpu.roll(back * s2_ref[...], 2 * HEAD_DIM - ROT // 2, 1)
        + pltpu.roll(back * s1_ref[...], ROT // 2, 1)
    )
    dj_ref[:, : 2 * HEAD_DIM] = turned_back.astype(BF16)
    dj_ref[:, 2 * HEAD_DIM :] = dv_ref[...].astype(BF16)
    gb_ref[0] = jnp.sum(dj_ref[...].astype(F32), axis=0, keepdims=True)

    for j in range(3):
        at = slice(j * BLOCK, (j + 1) * BLOCK)
        gw_ref[0, at, :] = dot_tn(h_ref[:, at], dj_ref[...])

    first = head == 0
    for t in range(tiles):
        at = slice(t * BLOCK, (t + 1) * BLOCK)
        dh_new = dot_nt(dj_ref[at, :], w_ref[0])
        mix_new = dot_tn(ctxt_ref[:, at], wd_ref[0])

        @pl.when(first)
        def _():
            dh_acc[at, :] = dh_new
            mix_acc[at, :] = mix_in[at, :] + mix_new

        @pl.when(head > 0)
        def _():
            dh_acc[at, :] += dh_new
            mix_acc[at, :] += mix_new

    @pl.when(head == last)
    def _():
        vec_ref[...] = jnp.zeros_like(vec_ref)

        @pl.loop(0, tiles)
        def _(t):
            at = pl.ds(t * BLOCK, BLOCK)
            normed, inv_std = normalize(x_ref[at, :])
            dh = dh_acc[at, :]
            vec_ref[0:1, :] += jnp.sum(dh * normed, axis=0, keepdims=True)
            vec_ref[1:2, :] += jnp.sum(dh, axis=0, keepdims=True)
            dx = norm_back(dh * gain_ref[...], normed, inv_std)
            dx_ref[at, :] = (dx_in[at, :] + dx).astype(BF16)
            mix_ref[at, :] = mix_acc[at, :].astype(BF16)


def attn_branch(x_seq, go_seq, w_heads, b_heads, wd_heads, tables, segc, segr, gain, bias, mix, dx):
    rows, width = x_seq.shape
    heads = w_heads.shape[0]
    inner = w_heads.shape[2]

    def whole(a):
        return pl.BlockSpec(a.shape, lambda i: (0,) * a.ndim)

    def per_head(a):
        return pl.BlockSpec((1,) + a.shape[1:], lambda i: (i,) + (0,) * (a.ndim - 1))

    def shape(s, d):
        return jax.ShapeDtypeStruct(s, d)

    outs = [
        shape((rows, width), BF16),
        shape((rows, width), BF16),
        shape((heads, width, inner), F32),
        shape((heads, 1, inner), F32),
        shape((heads, HEAD_DIM, width), F32),
        shape((8, width), F32),
    ]
    args = (x_seq, go_seq, w_heads, b_heads, wd_heads) + tables + (segc, segr, gain, bias, mix, dx)
    specs = [whole(a) for a in args]
    for j in (2, 3, 4):
        specs[j] = per_head(args[j])
    return pl.pallas_call(
        attn_kernel,
        grid=(heads,),
        in_specs=specs,
        out_specs=[whole(outs[0]), whole(outs[1])]
        + [per_head(a) for a in outs[2:5]]
        + [whole(outs[5])],
        out_shape=outs,
        scratch_shapes=[
            pltpu.VMEM((rows, width), BF16),
            pltpu.VMEM((rows, width), F32),
            pltpu.VMEM((rows, width), F32),
            pltpu.VMEM((rows, 2 * HEAD_DIM), BF16),
            pltpu.VMEM((rows, HEAD_DIM), BF16),
            pltpu.VMEM((rows, HEAD_DIM), BF16),
            pltpu.VMEM((HEAD_DIM, rows), BF16),
            pltpu.VMEM((HEAD_DIM, rows), F32),
            pltpu.VMEM((rows, HEAD_DIM), F32),
            pltpu.VMEM((rows, HEAD_DIM), F32),
            pltpu.VMEM((rows, inner), BF16),
        ],
        compiler_params=pltpu.CompilerParams(
            dimension_semantics=("arbitrary",), vmem_limit_bytes=56 * 1024 * 1024
        ),
        cost_estimate=pl.CostEstimate(
            flops=20 * 1000 * 1000 * 1000, transcendentals=heads * rows * rows,
            bytes_accessed=24 * 1024 * 1024,
        ),
        name="attn_branch",
    )(*args)


def group_perm(n_row, n_col, target):
    pairs = []
    for r in range(n_row):
        for c in range(n_col):
            to = target(r, c // 2, c % 2)
            if to is not None:
                pairs.append((r * n_col + c, to[0] * n_col + 2 * to[1] + to[2]))
    return pairs


def swap_row(value):
    return lax.ppermute(value, "row", [(0, 1), (1, 0)])


def dp_total(value):
    n_dp = lax.axis_size("dp")
    if n_dp != 4:
        return lax.psum(value, "dp")
    place = lax.axis_index("dp")
    inward = lax.ppermute(value.astype(BF16), "dp", [(0, 1), (3, 2)])
    pair = (value + inward.astype(F32)).astype(BF16)
    other = lax.ppermute(pair, "dp", [(1, 2), (2, 1)])
    total = (pair.astype(F32) + other.astype(F32)).astype(BF16)
    outward = lax.ppermute(total, "dp", [(1, 0), (2, 3)])
    return jnp.where((place == 1) | (place == 2), total, outward).astype(F32)


def swap_sum(value, axis, size, bit):
    return value + lax.ppermute(value, axis, [(i, i ^ bit) for i in range(size)])


def local(
    block_input, w_qkv, b_qkv, w_in, b_in, w_dense, b_dense, w_out, b_out,
    ln_attn_gain, ln_attn_bias, ln_mlp_gain, ln_mlp_bias, segments, positions, d_out,
):
    n_row = lax.axis_size("row")
    n_col = lax.axis_size("col")
    n_dp = lax.axis_size("dp")
    row = lax.axis_index("row")
    col = lax.axis_index("col")
    own_rows, half = block_input.shape
    upper = col // 2
    core = col % 2
    home = row == upper
    heads = w_qkv.shape[1] // (3 * HEAD_DIM)

    spread = group_perm(
        n_row, n_col, lambda r, u, k: (r, 1 - u, k) if r == u else (1 - r, u, k)
    )
    cross = group_perm(n_row, n_col, lambda r, u, k: None if r == u else (1 - r, 1 - u, k))
    pair = group_perm(n_row, n_col, lambda r, u, k: (r, u, 1 - k))
    collect = group_perm(
        n_row, n_col, lambda r, u, k: (1 - r, u, k) if r == u else (r, 1 - u, k)
    )

    def gather_seq(block):
        near = lax.ppermute(block, GROUP, spread)
        far = lax.ppermute(block, GROUP, cross)
        mine = jnp.concatenate(
            [jnp.where(home, block, near), jnp.where(home, near, far)], axis=1
        )
        other = lax.ppermute(mine, GROUP, pair)
        return jnp.where(
            core == 0,
            jnp.concatenate([mine, other], axis=0),
            jnp.concatenate([other, mine], axis=0),
        )

    def reduce_seq(part):
        low = part[:own_rows]
        high = part[own_rows:]
        got = lax.ppermute(jnp.where(core == 0, high, low), GROUP, pair)
        kept = jnp.where(core == 0, low, high)
        summed = kept.astype(F32) + got.astype(F32)
        low_sum = summed.astype(BF16)
        near = lax.ppermute(
            jnp.where(home, low_sum[:, half:], low_sum[:, :half]), GROUP, collect
        )
        far = lax.ppermute(low_sum[:, half:], GROUP, cross)
        return near.astype(F32) + jnp.where(home, summed[:, :half], far.astype(F32))

    norms = jnp.stack([ln_attn_gain, ln_attn_bias, ln_mlp_gain, ln_mlp_bias])
    norms = jnp.concatenate([norms, swap_row(norms)], axis=1)
    x_seq = gather_seq(block_input)
    wi_p = swap_row(w_in)
    go_seq = gather_seq(d_out)
    wo_p = swap_row(w_out)
    wq_p = swap_row(w_qkv)
    wd_p = swap_row(w_dense)

    at_seq = row * SEQ_LEN
    seg_seq = lax.dynamic_slice_in_dim(segments, at_seq, SEQ_LEN)
    pos_seq = lax.dynamic_slice_in_dim(positions, at_seq, SEQ_LEN)
    lane = jnp.arange(2 * HEAD_DIM) % HEAD_DIM
    freq_steps = (lane % (ROT // 2)).astype(F32) * (-2.0 * math.log(10000.0) / ROT)
    freq = jnp.where(lane < ROT, jnp.exp(freq_steps), 0.0)
    angles = pos_seq.astype(F32)[:, None] * freq[None, :]
    cos_table = jnp.cos(angles)
    sin_table = jnp.sin(angles)
    sin_up = jnp.where(lane < ROT // 2, -sin_table, 0.0)
    sin_down = jnp.where((lane >= ROT // 2) & (lane < ROT), sin_table, 0.0)

    w_heads = jnp.concatenate([w_qkv, wq_p], axis=0).reshape(D, heads, 3 * HEAD_DIM)
    w_heads = w_heads.transpose(1, 0, 2)
    wd_heads = jnp.concatenate([w_dense, wd_p], axis=1).reshape(heads, HEAD_DIM, D)

    mix, dx, gwi_o, gwi_p, gwo_o, gwo_p, mlp_vec = mlp_branch(
        x_seq, go_seq, w_in, wi_p, w_out, wo_p, b_in[None], norms[2:3], norms[3:4]
    )
    grad_w_in = dp_total(gwi_o + swap_row(gwi_p).astype(F32))
    grad_w_out = dp_total(gwo_o + swap_row(gwo_p).astype(F32))

    mix, dx, gw_heads, gb_heads, gwd, attn_vec = attn_branch(
        x_seq, go_seq, w_heads, b_qkv.reshape(heads, 1, 3 * HEAD_DIM), wd_heads,
        (cos_table, sin_up, sin_down), seg_seq[:, None], seg_seq[None, :],
        norms[0:1], norms[1:2], mix, dx,
    )
    gw = gw_heads.transpose(1, 0, 2).reshape(D, w_qkv.shape[1])
    grad_w_qkv = dp_total(gw[:half] + swap_row(gw[half:].astype(BF16)).astype(F32))
    gwd = gwd.reshape(w_dense.shape[0], D)
    grad_w_dense = dp_total(gwd[:, :half] + swap_row(gwd[:, half:].astype(BF16)).astype(F32))

    block_output = (
        block_input.astype(F32) + reduce_seq(mix) + b_dense + b_out
    ).astype(BF16)
    d_out_f = d_out.astype(F32)
    d_input = d_out_f + reduce_seq(dx)

    feature_vecs = jnp.concatenate([attn_vec[:2], mlp_vec[:2]], axis=0)
    wide = jnp.concatenate([mlp_vec[2], gb_heads.reshape(-1)])
    mine = jnp.concatenate([feature_vecs[:, :half].reshape(-1), wide])
    theirs = jnp.concatenate([feature_vecs[:, half:].reshape(-1), wide])
    vecs = mine + swap_row(theirs)
    vecs = jnp.concatenate([vecs, jnp.sum(d_out_f, axis=0)])
    if n_dp == 4:
        vecs = swap_sum(vecs, "dp", 4, 1)
        vecs = swap_sum(vecs, "dp", 4, 2)
    else:
        vecs = lax.psum(vecs, "dp")
    hid = b_in.shape[0]
    width = b_qkv.shape[0]
    at_in = 4 * half
    at_qkv = at_in + hid
    at_out = at_qkv + width
    grad_b_in = vecs[at_in:at_qkv]
    grad_b_qkv = vecs[at_qkv:at_out]
    rest = jnp.concatenate([vecs[:at_in], vecs[at_out:]])
    rest = swap_sum(rest, "col", n_col, 1)
    rest = swap_sum(rest, "col", n_col, 2)
    rest = rest.reshape(5, half)
    return (
        block_output, d_input, grad_w_qkv, grad_b_qkv, grad_w_in, grad_b_in,
        grad_w_dense, rest[4], grad_w_out, rest[4], rest[0], rest[1], rest[2], rest[3],
    )


def solution(mesh):
    token = P(("dp", "col"), "row")
    placed = (
        token, P("row", "col"), P("col"), P("row", "col"), P("col"), P("col", "row"), P("row"),
        P("col", "row"), P("row"), P("row"), P("row"), P("row"), P("row"), P("dp"), P("dp"), token,
    )
    return jax.shard_map(
        local,
        mesh=mesh,
        in_specs=placed,
        out_specs=(
            token, token, P("row", "col"), P("col"), P("row", "col"), P("col"), P("col", "row"),
            P("row"), P("col", "row"), P("row"), P("row"), P("row"), P("row"), P("row"),
        ),
        check_vma=False,
    )
```

time: 981 us -> 286 us (0.29)
  waiting for transfers between devices: 544 us -> 114 us
  blocking collectives: 123 us -> 0 us
  local copies, waits for them, and re-layouts: 129 us -> 24.7 us
  matrix products: 88 us -> 0 us
  Pallas kernels: 0 us -> 55.3 us
  starting transfers between devices: 0.46 us -> 49.2 us
  other arithmetic: 68.6 us -> 40 us
  between operations: 15.1 us -> 1.25 us
    psum x2 -> x0, waiting for transfers between devices: 455 us -> none  [the longest x1 388 us: local(): lax.psum((dot_plain(attn_rows, w_qkv), dot_plain(mlp_rows, w_in)), 'row')]
    psum x4 -> x0, blocking collectives: 123 us -> none  [the longest x1 63.1 us: local(): lax.psum((jnp.sum(grad_h_attn * normed, axis=0), jnp.sum(grad_h_attn, axi...]
    ppermute x0 -> x38, waiting for transfers between devices: none -> 114 us  [the longest x10 38.5 us: swap_row(): return lax.ppermute(value, 'row', [(0, 1), (1, 0)])]
    dot_general x40 -> x0, matrix products: 88 us -> none  [the longest x4 15.2 us: dot_plain(): return jnp.dot(left_side, right_side, preferred_element_type=jnp.float32)]
    dynamic_update_slice x4 -> x0, local copies, waits for them, and re-layouts: 86.8 us -> none  [local(): lax.map(attend_backward, (joined_seq, seg_seq, maxima, totals, grad_seq))]
    pallas_call x0 -> x2, Pallas kernels: none -> 55.3 us  [the longest x1 39.7 us: attn_branch(): pl.pallas_call(attn_kernel, grid=(heads,), in_specs=specs, out_specs=[who...]
    all_gather x3 -> x0, waiting for transfers between devices: 52.3 us -> none  [the longest x1 22.8 us: local(): lax.all_gather(d_out, 'col', axis=0, tiled=True)]
    ppermute x0 -> x38, starting transfers between devices: none -> 49.2 us  [the longest x10 11.3 us: swap_row(): return lax.ppermute(value, 'row', [(0, 1), (1, 0)])]
  transfers between devices with their start and end apart: 7 -> 38, of which waited for: 6 -> 13; matrix products, arithmetic and copies ran while one was open for 20% -> 19% of each run, Pallas kernels for 0% -> 0%
where the time goes in v1:
time: 286 us; the launch traced here: 284 us
  waiting for transfers between devices  114 us (40%)
  Pallas kernels  55.3 us (19%)
  starting transfers between devices  49.2 us (17%)
  other arithmetic  40 us (14%)
  local copies, waits for them, and re-layouts  24.7 us (9%)
    pallas_call x1, Pallas kernels, attn_branch(): pl.pallas_call(attn_kernel, grid=(heads,), in_specs=specs, out_specs=[who...  39.7 us
    ppermute x10, waiting for transfers between devices, swap_row(): return lax.ppermute(value, 'row', [(0, 1), (1, 0)])  38.5 us
    ppermute x4, waiting for transfers between devices, dp_total(): outward = lax.ppermute(total, 'dp', [(1, 0), (2, 3)])  35.1 us
    ppermute x4, waiting for transfers between devices, swap_sum(): lax.ppermute(value, axis, [(i, i ^ bit) for i in range(size)])  19.6 us
    pallas_call x1, Pallas kernels, mlp_branch(): pl.pallas_call(mlp_kernel, grid=(rows // BLOCK,), in_specs=[row_spec, row...  15.5 us
    ppermute x2, waiting for transfers between devices, gather_seq(): near = lax.ppermute(block, GROUP, spread)  12.6 us
    ppermute x10, starting transfers between devices, swap_row(): return lax.ppermute(value, 'row', [(0, 1), (1, 0)])  11.3 us
    ppermute x4, starting transfers between devices, dp_total(): inward = lax.ppermute(value.astype(BF16), 'dp', [(0, 1), (3, 2)])  10.4 us
  transfers between devices with their start and end apart: 38, of which 13 were waited for; matrix products, arithmetic and copies ran while one was open for 19% of the time, Pallas kernels for 0%

profile of v1, /device:TPU:0, one launch (start us, length us, event | category | flops | bytes accessed | tf_op | source)
XLA Modules:
  0.0 284.2 jit_solution(12981198894045051361)
XLA Ops:
  0.6 3.0 %collective-permute-start = (bf16[512,384]{1,0:T(8,128)(2,1)}, bf16[512,384]{1,0:T(8,128)(2,1)S(1)}, u32[]{:S(2)}, u32[]{:S(2)}) collective-permute-start(bf16[512,384]{1,0:T(8,128)(2,1)} %param.16), channel_id=1, source_target_pairs={{0,2},{1,3},{2,6},{3,7},{4,0},{5,1},{6,4},{7,5},{8,10},{9,11},{10,... | collective-permute-start | bytes 1179656 | tf_op jit(solution)/shard_map/ppermute | solution.py:361
  4.3 2.8 collective-permute-start.3
  11.2 2.7 collective-permute-start.8
  14.6 7.2 %collective-permute-done = bf16[512,384]{1,0:T(8,128)(2,1)S(1)} collective-permute-done((bf16[512,384]{1,0:T(8,128)(2,1)}, bf16[512,384]{1,0:T(8,128)(2,1)S(1)}, u32[]{:S(2)}, u32[]{:S(2)}) %collective-permute-start) | collective-permute-done | bytes 393248 | tf_op jit(solution)/shard_map/ppermute | solution.py:361
  21.8 1.5 collective-permute-start.10
  23.3 2.0 collective-permute-start.6
  25.3 5.4 %collective-permute-done.3 = bf16[512,384]{1,0:T(8,128)(2,1)S(1)} collective-permute-done((bf16[512,384]{1,0:T(8,128)(2,1)}, bf16[512,384]{1,0:T(8,128)(2,1)S(1)}, u32[]{:S(2)}, u32[]{:S(2)}) %collective-permute-start.3) | collective-permute-done | bytes 393248 | tf_op jit(solution)/shard_map/ppermute | solution.py:361
  31.7 1.3 broadcast_select_fusion.3
  34.1 3.3 %fusion.8 = (f32[1024,128]{1,0:T(8,128)}, f32[1024,128]{1,0:T(8,128)}, f32[1024,128]{1,0:T(8,128)}) fusion(f32[128]{0:T(128)S(1)} %compare_select_fusion.2, f32[1024]{0:T(1024)S(1)} %dynamic-slice_convert_fusion, pred[128]{0:T(512)(128)(4,1)S(1)} %get-tuple-element.70, pred[128]{0:T(512)(128)(4,1)S(1)} %get-tuple-element.71), kind=kLoop, calls=%fused_computation.33 | loop fusion | flops 524288 | bytes 1577728 | tf_op jit(solution)/shard_map/jit(_where)/select_n | solution.py:405
  41.8 22.0 %collective-permute-done.7 = bf16[192,384]{1,0:T(8,128)(2,1)} collective-permute-done((bf16[192,384]{1,0:T(8,128)(2,1)}, bf16[192,384]{1,0:T(8,128)(2,1)}, u32[]{:S(2)}, u32[]{:S(2)}) %collective-permute-start.7) | collective-permute-done | bytes 147488 | tf_op jit(solution)/shard_map/ppermute | solution.py:316
  63.9 1.6 pad_maximum_fusion.3
  65.5 1.2 pad_maximum_fusion
  66.7 1.4 copy.30
  68.2 3.5 %maximum_select_fusion.1.go_ref = bf16[1024,768]{1,0:T(8,128)(2,1)} fusion(bf16[512,768]{1,0:T(8,128)(2,1)} %collective-permute-done.5, bf16[512,384]{1,0:T(8,128)(2,1)} %copy-done.10, bf16[512,384]{1,0:T(8,128)(2,1)} %copy-done.9, pred[]{:T(512)S(6)} %eq.14), kind=kLoop, calls=%fused_computation.1 | loop fusion | flops 10223616 | bytes 3145729 | tf_op jit(solution)/shard_map/jit(_where)/select_n | solution.py:367
  71.6 3.1 %maximum_select_fusion.x_ref = bf16[1024,768]{1,0:T(8,128)(2,1)} fusion(bf16[512,768]{1,0:T(8,128)(2,1)} %collective-permute-done.2, bf16[512,384]{1,0:T(8,128)(2,1)S(1)} %get-tuple-element.68, bf16[512,384]{1,0:T(8,128)(2,1)S(1)} %get-tuple-element.69, pred[]{:T(512)S(6)} %eq.14), kind=kLoop, calls=%fused_computation | loop fusion | flops 10223616 | bytes 3145729 | tf_op jit(solution)/shard_map/jit(_where)/select_n | solution.py:367
  75.6 2.8 collective-permute-done.9.wi_p
  81.3 15.5 %mlp_branch.1 = (f32[1024,768]{1,0:T(8,128)}, f32[1024,768]{1,0:T(8,128)}, f32[384,768]{1,0:T(8,128)S(1)}, bf16[384,768]{1,0:T(8,128)(2,1)S(1)}, f32[768,384]{1,...) custom-call(bf16[1024,768]{1,0:T(8,128)(2,1)} %maximum_select_fusion.x_ref, ...), custom_call_target="tpu_custom_call" | custom-call | flops 7247757312 | bytes 25165824 | tf_op jit(solution)/shard_map/mlp_branch/pallas_call | solution.py:113
  96.9 39.7 %attn_branch.1 = (bf16[1024,768]{1,0:T(8,128)(2,1)}, bf16[1024,768]{1,0:T(8,128)(2,1)}, f32[3,768,192]{2,1,0:T(8,128)}, f32[3,1,192]{2,1,0:T(1,128)}, f32[3,64,768]{2,1,0:T(8,128)}, /*index=5*/f32[8,768]{1,0:T(8,128)}) custom-call(bf16[1024,768]{1,0:T(8,128)(2,1)} %maximum_select_fusion.x_ref, bf16[1024,768]{1,0:T(8,128)(2,1)} %maximum_select_fusion.1.go_ref, ...), custom_call_target="tpu_custom_call" | custom-call | flops 20000000000 | bytes 25165824 | tf_op jit(solution)/shard_map/attn_branch/pallas_call | solution.py:273
  136.6 2.4 slice.153
  139.0 1.3 slice.210
  144.7 1.7 collective-permute-start.21
  147.2 1.6 slice.211
  149.1 2.3 broadcast_select_fusion
  151.4 1.7 collective-permute-start.24
  153.2 2.5 copy.32
  156.7 3.7 %collective-permute-done.28 = bf16[192,384]{1,0:T(8,128)(2,1)} collective-permute-done((bf16[192,384]{1,0:T(8,128)(2,1)}, bf16[192,384]{1,0:T(8,128)(2,1)}, u32[]{:S(2)}, u32[]{:S(2)}) %collective-permute-start.28) | collective-permute-done | bytes 147488 | tf_op jit(solution)/shard_map/ppermute | solution.py:316
  161.5 3.1 %collective-permute-start.29 = (bf16[192,384]{1,0:T(8,128)(2,1)S(1)}, bf16[192,384]{1,0:T(8,128)(2,1)S(1)}, u32[]{:S(2)}, u32[]{:S(2)}) collective-permute-start(bf16[192,384]{1,0:T(8,128)(2,1)S(1)} %fusion.12), channel_id=1, source_target_pairs={{0,8},{24,16},{1,9},{25,17},{2,10},{26,18},{3,11},{27,19},{4,12},{... | collective-permute-start | bytes 442376 | tf_op jit(solution)/shard_map/ppermute | solution.py:324
  164.6 1.5 broadcast_select_fusion.1
  169.7 10.0 %collective-permute-done.17 = bf16[384,576]{0,1:T(8,128)(2,1)S(1)} collective-permute-done((bf16[384,576]{0,1:T(8,128)(2,1)S(1)}, bf16[384,576]{0,1:T(8,128)(2,1)S(1)}, u32[]{:S(2)}, u32[]{:S(2)}) %collective-permute-start.17) | collective-permute-done | bytes 442400 | tf_op jit(solution)/shard_map/ppermute | solution.py:316
  179.8 1.3 collective-permute-start.31
  181.2 4.6 %collective-permute-start.18 = (bf16[384,576]{0,1:T(8,128)(2,1)S(1)}, bf16[384,576]{0,1:T(8,128)(2,1)S(1)}, u32[]{:S(2)}, u32[]{:S(2)}) collective-permute-start(bf16[384,576]{0,1:T(8,128)(2,1)S(1)} %fusion.10), channel_id=1, source_target_pairs={{0,8},{24,16},{1,9},{25,17},{2,10},{26,18},{3,11},{27,19},{4,12},{... | collective-permute-start | bytes 1327112 | tf_op jit(solution)/shard_map/ppermute | solution.py:324
  186.9 1.5 collective-permute-start.35
  189.6 1.3 collective-permute-start.25
  191.7 1.5 fusion.20
  195.2 6.8 %collective-permute-done.15 = bf16[512,384]{1,0:T(8,128)(2,1)S(1)} collective-permute-done((bf16[512,384]{1,0:T(8,128)(2,1)S(1)}, bf16[512,384]{1,0:T(8,128)(2,1)S(1)}, u32[]{:S(2)}, u32[]{:S(2)}) %collective-permute-start.15) | collective-permute-done | bytes 393248 | tf_op jit(solution)/shard_map/ppermute | solution.py:380
  201.9 1.2 collective-permute-start.12
  205.2 12.9 %collective-permute-done.22 = f32[3264]{0:T(1024)S(1)} collective-permute-done((f32[3264]{0:T(1024)S(1)}, f32[3264]{0:T(1024)S(1)}, u32[]{:S(2)}, u32[]{:S(2)}) %collective-permute-start.22) | collective-permute-done | bytes 13088 | tf_op jit(solution)/shard_map/ppermute | solution.py:333
  218.8 5.4 %collective-permute-start.23 = (f32[3264]{0:T(1024)S(1)}, f32[3264]{0:T(1024)S(1)}, u32[]{:S(2)}, u32[]{:S(2)}) collective-permute-start(f32[3264]{0:T(1024)S(1)} %fusion.19), channel_id=1, source_target_pairs={{0,16},{8,24},{16,0},{24,8},{1,17},{9,25},{17,1},{25,9},{2,18},{10... | collective-permute-start | bytes 39176 | tf_op jit(solution)/shard_map/ppermute | solution.py:333
  224.2 1.3 add_convert_fusion.1
  225.6 6.7 %collective-permute-done.23 = f32[3264]{0:T(1024)S(1)} collective-permute-done((f32[3264]{0:T(1024)S(1)}, f32[3264]{0:T(1024)S(1)}, u32[]{:S(2)}, u32[]{:S(2)}) %collective-permute-start.23) | collective-permute-done | bytes 13088 | tf_op jit(solution)/shard_map/ppermute | solution.py:333
  233.2 1.3 add_convert_fusion.3
  235.2 3.1 %collective-permute-start.33 = (f32[1920]{0:T(1024)S(1)}, f32[1920]{0:T(1024)S(1)}, u32[]{:S(2)}, u32[]{:S(2)}) collective-permute-start(f32[1920]{0:T(1024)S(1)} %fusion.24), channel_id=1, source_target_pairs={{0,2},{1,3},{2,0},{3,1},{4,6},{5,7},{6,4},{7,5},{8,10},{9,11},{10,... | collective-permute-start | bytes 23048 | tf_op jit(solution)/shard_map/ppermute | solution.py:333
  240.6 1.3 collective-permute-start.20
  242.0 1.3 collective-permute-start.37
  243.5 1.3 collective-permute-start.27
  245.4 12.6 %collective-permute-done.20 = bf16[384,576]{0,1:T(8,128)(2,1)S(1)} collective-permute-done((bf16[384,576]{0,1:T(8,128)(2,1)S(1)}, bf16[384,576]{0,1:T(8,128)(2,1)S(1)}, u32[]{:S(2)}, u32[]{:S(2)}) %collective-permute-start.20) | collective-permute-done | bytes 442400 | tf_op jit(solution)/shard_map/ppermute | solution.py:328
  258.9 11.7 %collective-permute-done.37 = bf16[768,384]{1,0:T(8,128)(2,1)S(1)} collective-permute-done((bf16[768,384]{1,0:T(8,128)(2,1)S(1)}, bf16[768,384]{1,0:T(8,128)(2,1)S(1)}, u32[]{:S(2)}, u32[]{:S(2)}) %collective-permute-start.37) | collective-permute-done | bytes 589856 | tf_op jit(solution)/shard_map/ppermute | solution.py:328
  271.7 10.8 %collective-permute-done.27 = bf16[384,768]{1,0:T(8,128)(2,1)S(1)} collective-permute-done((bf16[384,768]{1,0:T(8,128)(2,1)S(1)}, bf16[384,768]{1,0:T(8,128)(2,1)S(1)}, u32[]{:S(2)}, u32[]{:S(2)}) %collective-permute-start.27) | collective-permute-done | bytes 589856 | tf_op jit(solution)/shard_map/ppermute | solution.py:328
  (160 shorter events, 43.2 us)
Async XLA Ops:
  0.6 21.1 %collective-permute-start = (bf16[512,384]{1,0:T(8,128)(2,1)}, bf16[512,384]{1,0:T(8,128)(2,1)S(1)}, u32[]{:S(2)}, u32[]{:S(2)}) collective-permute-start(bf16[512,384]{1,0:T(8,128)(2,1)} %param.16), channel_id=1, source_target_pairs={{0,2},{1,3},{2,6},{3,7},{4,0},{5,1},{6,4},{7,5},{8,10},{9,11},{10,... | collective-permute-start | bytes 1179656 | tf_op jit(solution)/shard_map/ppermute | solution.py:361
  3.7 19.6 %collective-permute-start.1 = (bf16[512,384]{1,0:T(8,128)(2,1)}, bf16[512,384]{1,0:T(8,128)(2,1)S(1)}, u32[]{:S(2)}, u32[]{:S(2)}) collective-permute-start(bf16[512,384]{1,0:T(8,128)(2,1)} %param.16), channel_id=1, source_target_pairs={{2,4},{3,5},{4,2},{5,3},{10,12},{11,13},{12,10},{13,11},{18,20},{1... | collective-permute-start | bytes 1179656 | tf_op jit(solution)/shard_map/ppermute | solution.py:362
  4.3 26.3 %collective-permute-start.3 = (bf16[512,384]{1,0:T(8,128)(2,1)}, bf16[512,384]{1,0:T(8,128)(2,1)S(1)}, u32[]{:S(2)}, u32[]{:S(2)}) collective-permute-start(bf16[512,384]{1,0:T(8,128)(2,1)} %param.31), channel_id=1, source_target_pairs={{0,2},{1,3},{2,6},{3,7},{4,0},{5,1},{6,4},{7,5},{8,10},{9,11},{10,... | collective-permute-start | bytes 1179656 | tf_op jit(solution)/shard_map/ppermute | solution.py:361
  7.1 24.6 %collective-permute-start.4 = (bf16[512,384]{1,0:T(8,128)(2,1)}, bf16[512,384]{1,0:T(8,128)(2,1)S(1)}, u32[]{:S(2)}, u32[]{:S(2)}) collective-permute-start(bf16[512,384]{1,0:T(8,128)(2,1)} %param.31), channel_id=1, source_target_pairs={{2,4},{3,5},{4,2},{5,3},{10,12},{11,13},{12,10},{13,11},{18,20},{1... | collective-permute-start | bytes 1179656 | tf_op jit(solution)/shard_map/ppermute | solution.py:362
  9.9 23.1 %copy-start.17 = (f32[1,384]{1,0:T(1,128)}, f32[1,384]{1,0:T(1,128)S(1)}, u32[]{:S(2)}) copy-start(f32[1,384]{1,0:T(1,128)S(1)} %stack.17) | copy-start | bytes 4612
  10.5 22.4 %copy-start.19 = (f32[1,384]{1,0:T(1,128)}, f32[1,384]{1,0:T(1,128)S(1)}, u32[]{:S(2)}) copy-start(f32[1,384]{1,0:T(1,128)S(1)} %stack.18) | copy-start | bytes 4612
  11.2 28.9 %collective-permute-start.8 = (f32[4,384]{1,0:T(4,128)}, f32[4,384]{1,0:T(4,128)}, u32[]{:S(2)}, u32[]{:S(2)}) collective-permute-start(f32[4,384]{1,0:T(4,128)} %pad_maximum_fusion.12), channel_id=1, source_target_pairs={{0,4},{4,0},{1,5},{5,1},{2,6},{6,2},{3,7},{7,3},{8,12},{12,8},{9,1... | collective-permute-start | bytes 18440 | tf_op jit(solution)/shard_map/ppermute | solution.py:316
  21.8 53.0 %collective-permute-start.10 = (bf16[768,384]{1,0:T(8,128)(2,1)}, bf16[768,384]{1,0:T(8,128)(2,1)S(1)}, u32[]{:S(2)}, u32[]{:S(2)}) collective-permute-start(bf16[768,384]{1,0:T(8,128)(2,1)} %wo_o.1), channel_id=1, source_target_pairs={{0,4},{4,0},{1,5},{5,1},{2,6},{6,2},{3,7},{7,3},{8,12},{12,8},{9,1... | collective-permute-start | bytes 1769480 | tf_op jit(solution)/shard_map/ppermute | solution.py:316
  23.3 42.2 %collective-permute-start.6 = (bf16[384,576]{0,1:T(8,128)(2,1)}, bf16[384,576]{0,1:T(8,128)(2,1)}, u32[]{:S(2)}, u32[]{:S(2)}) collective-permute-start(bf16[384,576]{0,1:T(8,128)(2,1)} %param.17), channel_id=1, source_target_pairs={{0,4},{4,0},{1,5},{5,1},{2,6},{6,2},{3,7},{7,3},{8,12},{12,8},{9,1... | collective-permute-start | bytes 1327112 | tf_op jit(solution)/shard_map/ppermute | solution.py:316
  30.7 33.2 %collective-permute-start.7 = (bf16[192,384]{1,0:T(8,128)(2,1)}, bf16[192,384]{1,0:T(8,128)(2,1)}, u32[]{:S(2)}, u32[]{:S(2)}) collective-permute-start(bf16[192,384]{1,0:T(8,128)(2,1)} %param.21), channel_id=1, source_target_pairs={{0,4},{4,0},{1,5},{5,1},{2,6},{6,2},{3,7},{7,3},{8,12},{12,8},{9,1... | collective-permute-start | bytes 442376 | tf_op jit(solution)/shard_map/ppermute | solution.py:316
  34.0 34.2 %collective-permute-start.5 = (bf16[512,768]{1,0:T(8,128)(2,1)}, bf16[512,768]{1,0:T(8,128)(2,1)}, u32[]{:S(2)}, u32[]{:S(2)}) collective-permute-start(bf16[512,768]{1,0:T(8,128)(2,1)} %pad_maximum_fusion.2), channel_id=1, source_target_pairs={{0,1},{1,0},{2,3},{3,2},{4,5},{5,4},{6,7},{7,6},{8,9},{9,8},{10,11... | collective-permute-start | bytes 2359304 | tf_op jit(solution)/shard_map/ppermute | solution.py:366
  34.1 29.7 %copy-start = (bf16[384,768]{1,0:T(8,128)(2,1)S(1)}, bf16[384,768]{1,0:T(8,128)(2,1)}, u32[]{:S(2)}) copy-start(bf16[384,768]{1,0:T(8,128)(2,1)} %wi_o.1) | copy-start | bytes 1769476
  34.1 29.7 %copy-start.15 = (bf16[192,384]{1,0:T(8,128)(2,1)S(1)}, bf16[192,384]{1,0:T(8,128)(2,1)}, u32[]{:S(2)}) copy-start(bf16[192,384]{1,0:T(8,128)(2,1)} %param.21) | copy-start | bytes 442372
  37.4 29.3 %copy-start.16 = (s32[1024]{0:T(1024)}, s32[1024]{0:T(1024)S(1)}, u32[]{:S(2)}) copy-start(s32[1024]{0:T(1024)S(1)} %dynamic_slice.7) | copy-start | bytes 12292
  40.1 31.5 %collective-permute-start.2 = (bf16[512,768]{1,0:T(8,128)(2,1)}, bf16[512,768]{1,0:T(8,128)(2,1)}, u32[]{:S(2)}, u32[]{:S(2)}) collective-permute-start(bf16[512,768]{1,0:T(8,128)(2,1)} %pad_maximum_fusion.1), channel_id=1, source_target_pairs={{0,1},{1,0},{2,3},{3,2},{4,5},{5,4},{6,7},{7,6},{8,9},{9,8},{10,11... | collective-permute-start | bytes 2359304 | tf_op jit(solution)/shard_map/ppermute | solution.py:366
  63.9 14.5 %collective-permute-start.9 = (bf16[384,768]{1,0:T(8,128)(2,1)S(1)}, bf16[384,768]{1,0:T(8,128)(2,1)S(1)}, u32[]{:S(2)}, u32[]{:S(2)}) collective-permute-start(bf16[384,768]{1,0:T(8,128)(2,1)S(1)} %copy-done), channel_id=1, source_target_pairs={{0,4},{4,0},{1,5},{5,1},{2,6},{6,2},{3,7},{7,3},{8,12},{12,8},{9,1... | collective-permute-start | bytes 1769480 | tf_op jit(solution)/shard_map/ppermute | solution.py:316
  140.3 40.8 %collective-permute-start.34 = (bf16[768,384]{1,0:T(8,128)(2,1)}, bf16[768,384]{1,0:T(8,128)(2,1)}, u32[]{:S(2)}, u32[]{:S(2)}) collective-permute-start(bf16[768,384]{1,0:T(8,128)(2,1)} %get-tuple-element.39), channel_id=1, source_target_pairs={{0,4},{4,0},{1,5},{5,1},{2,6},{6,2},{3,7},{7,3},{8,12},{12,8},{9,1... | collective-permute-start | bytes 1769480 | tf_op jit(solution)/shard_map/ppermute | solution.py:316
  144.7 23.5 %collective-permute-start.21 = (f32[2880]{0:T(1024)}, f32[2880]{0:T(1024)}, u32[]{:S(2)}, u32[]{:S(2)}) collective-permute-start(f32[2880]{0:T(1024)} %pad_maximum_fusion.5), channel_id=1, source_target_pairs={{0,4},{4,0},{1,5},{5,1},{2,6},{6,2},{3,7},{7,3},{8,12},{12,8},{9,1... | collective-permute-start | bytes 34568 | tf_op jit(solution)/shard_map/ppermute | solution.py:316
  148.8 11.6 %collective-permute-start.28 = (bf16[192,384]{1,0:T(8,128)(2,1)}, bf16[192,384]{1,0:T(8,128)(2,1)}, u32[]{:S(2)}, u32[]{:S(2)}) collective-permute-start(bf16[192,384]{1,0:T(8,128)(2,1)} %slice.211), channel_id=1, source_target_pairs={{0,4},{4,0},{1,5},{5,1},{2,6},{6,2},{3,7},{7,3},{8,12},{12,8},{9,1... | collective-permute-start | bytes 442376 | tf_op jit(solution)/shard_map/ppermute | solution.py:316
  151.4 40.3 %collective-permute-start.14 = (bf16[512,768]{1,0:T(8,128)(2,1)}, bf16[512,768]{1,0:T(8,128)(2,1)}, u32[]{:S(2)}, u32[]{:S(2)}) collective-permute-start(bf16[512,768]{1,0:T(8,128)(2,1)} %broadcast_select_fusion), channel_id=1, source_target_pairs={{0,1},{1,0},{2,3},{3,2},{4,5},{5,4},{6,7},{7,6},{8,9},{9,8},{10,11... | collective-permute-start | bytes 2359304 | tf_op jit(solution)/shard_map/ppermute | solution.py:376
  151.4 35.5 %collective-permute-start.24 = (bf16[384,768]{1,0:T(8,128)(2,1)S(1)}, bf16[384,768]{1,0:T(8,128)(2,1)}, u32[]{:S(2)}, u32[]{:S(2)}) collective-permute-start(bf16[384,768]{1,0:T(8,128)(2,1)S(1)} %get-tuple-element.36), channel_id=1, source_target_pairs={{0,4},{4,0},{1,5},{5,1},{2,6},{6,2},{3,7},{7,3},{8,12},{12,8},{9,1... | collective-permute-start | bytes 1769480 | tf_op jit(solution)/shard_map/ppermute | solution.py:316
  161.5 5.7 %collective-permute-start.29 = (bf16[192,384]{1,0:T(8,128)(2,1)S(1)}, bf16[192,384]{1,0:T(8,128)(2,1)S(1)}, u32[]{:S(2)}, u32[]{:S(2)}) collective-permute-start(bf16[192,384]{1,0:T(8,128)(2,1)S(1)} %fusion.12), channel_id=1, source_target_pairs={{0,8},{24,16},{1,9},{25,17},{2,10},{26,18},{3,11},{27,19},{4,12},{... | collective-permute-start | bytes 442376 | tf_op jit(solution)/shard_map/ppermute | solution.py:324
  164.6 16.5 %copy-start.6 = (f32[384,3,192]{0,2,1:T(8,128)S(1)}, f32[384,3,192]{0,2,1:T(8,128)}, u32[]{:S(2)}) copy-start(f32[384,3,192]{0,2,1:T(8,128)} %copy.32) | copy-start | bytes 2654212
  167.2 12.5 %collective-permute-start.17 = (bf16[384,576]{0,1:T(8,128)(2,1)S(1)}, bf16[384,576]{0,1:T(8,128)(2,1)S(1)}, u32[]{:S(2)}, u32[]{:S(2)}) collective-permute-start(bf16[384,576]{0,1:T(8,128)(2,1)S(1)} %bitcast.21), channel_id=1, source_target_pairs={{0,4},{4,0},{1,5},{5,1},{2,6},{6,2},{3,7},{7,3},{8,12},{12,8},{9,1... | collective-permute-start | bytes 1327112 | tf_op jit(solution)/shard_map/ppermute | solution.py:316
  168.2 1.4 collective-permute-start.30
  169.6 24.3 %collective-permute-start.11 = (bf16[512,768]{1,0:T(8,128)(2,1)S(1)}, bf16[512,768]{1,0:T(8,128)(2,1)S(1)}, u32[]{:S(2)}, u32[]{:S(2)}) collective-permute-start(bf16[512,768]{1,0:T(8,128)(2,1)S(1)} %broadcast_select_fusion.1), channel_id=1, source_target_pairs={{0,1},{1,0},{2,3},{3,2},{4,5},{5,4},{6,7},{7,6},{8,9},{9,8},{10,11... | collective-permute-start | bytes 2359304 | tf_op jit(solution)/shard_map/ppermute | solution.py:376
  179.8 9.8 %collective-permute-start.31 = (bf16[192,384]{1,0:T(8,128)(2,1)S(1)}, bf16[192,384]{1,0:T(8,128)(2,1)S(1)}, u32[]{:S(2)}, u32[]{:S(2)}) collective-permute-start(bf16[192,384]{1,0:T(8,128)(2,1)S(1)} %add_convert_fusion.6), channel_id=1, source_target_pairs={{8,0},{16,24},{9,1},{17,25},{10,2},{18,26},{11,3},{19,27},{12,4},{... | collective-permute-start | bytes 442376 | tf_op jit(solution)/shard_map/ppermute | solution.py:328
  181.2 23.8 %collective-permute-start.18 = (bf16[384,576]{0,1:T(8,128)(2,1)S(1)}, bf16[384,576]{0,1:T(8,128)(2,1)S(1)}, u32[]{:S(2)}, u32[]{:S(2)}) collective-permute-start(bf16[384,576]{0,1:T(8,128)(2,1)S(1)} %fusion.10), channel_id=1, source_target_pairs={{0,8},{24,16},{1,9},{25,17},{2,10},{26,18},{3,11},{27,19},{4,12},{... | collective-permute-start | bytes 1327112 | tf_op jit(solution)/shard_map/ppermute | solution.py:324
  186.9 31.9 %collective-permute-start.35 = (bf16[768,384]{1,0:T(8,128)(2,1)S(1)}, bf16[768,384]{1,0:T(8,128)(2,1)S(1)}, u32[]{:S(2)}, u32[]{:S(2)}) collective-permute-start(bf16[768,384]{1,0:T(8,128)(2,1)S(1)} %fusion.1), channel_id=1, source_target_pairs={{0,8},{24,16},{1,9},{25,17},{2,10},{26,18},{3,11},{27,19},{4,12},{... | collective-permute-start | bytes 1769480 | tf_op jit(solution)/shard_map/ppermute | solution.py:324
  189.6 43.5 %collective-permute-start.25 = (bf16[384,768]{1,0:T(8,128)(2,1)S(1)}, bf16[384,768]{1,0:T(8,128)(2,1)S(1)}, u32[]{:S(2)}, u32[]{:S(2)}) collective-permute-start(bf16[384,768]{1,0:T(8,128)(2,1)S(1)} %fusion), channel_id=1, source_target_pairs={{0,8},{24,16},{1,9},{25,17},{2,10},{26,18},{3,11},{27,19},{4,12},{... | collective-permute-start | bytes 1769480 | tf_op jit(solution)/shard_map/ppermute | solution.py:324
  193.2 8.7 %collective-permute-start.15 = (bf16[512,384]{1,0:T(8,128)(2,1)S(1)}, bf16[512,384]{1,0:T(8,128)(2,1)S(1)}, u32[]{:S(2)}, u32[]{:S(2)}) collective-permute-start(bf16[512,384]{1,0:T(8,128)(2,1)S(1)} %get-tuple-element.44), channel_id=1, source_target_pairs={{0,4},{1,5},{2,0},{3,1},{4,6},{5,7},{6,2},{7,3},{8,12},{9,13},{10,... | collective-permute-start | bytes 1179656 | tf_op jit(solution)/shard_map/ppermute | solution.py:380
  193.9 9.3 %collective-permute-start.16 = (bf16[512,384]{1,0:T(8,128)(2,1)S(1)}, bf16[512,384]{1,0:T(8,128)(2,1)S(1)}, u32[]{:S(2)}, u32[]{:S(2)}) collective-permute-start(bf16[512,384]{1,0:T(8,128)(2,1)S(1)} %get-tuple-element.45), channel_id=1, source_target_pairs={{2,4},{3,5},{4,2},{5,3},{10,12},{11,13},{12,10},{13,11},{18,20},{1... | collective-permute-start | bytes 1179656 | tf_op jit(solution)/shard_map/ppermute | solution.py:383
  201.9 33.2 %collective-permute-start.12 = (bf16[512,384]{1,0:T(8,128)(2,1)S(1)}, bf16[512,384]{1,0:T(8,128)(2,1)S(1)}, u32[]{:S(2)}, u32[]{:S(2)}) collective-permute-start(bf16[512,384]{1,0:T(8,128)(2,1)S(1)} %get-tuple-element.46), channel_id=1, source_target_pairs={{0,4},{1,5},{2,0},{3,1},{4,6},{5,7},{6,2},{7,3},{8,12},{9,13},{10,... | collective-permute-start | bytes 1179656 | tf_op jit(solution)/shard_map/ppermute | solution.py:380
  203.1 35.1 %collective-permute-start.13 = (bf16[512,384]{1,0:T(8,128)(2,1)S(1)}, bf16[512,384]{1,0:T(8,128)(2,1)S(1)}, u32[]{:S(2)}, u32[]{:S(2)}) collective-permute-start(bf16[512,384]{1,0:T(8,128)(2,1)S(1)} %get-tuple-element.47), channel_id=1, source_target_pairs={{2,4},{3,5},{4,2},{5,3},{10,12},{11,13},{12,10},{13,11},{18,20},{1... | collective-permute-start | bytes 1179656 | tf_op jit(solution)/shard_map/ppermute | solution.py:383
  205.0 13.1 %collective-permute-start.22 = (f32[3264]{0:T(1024)S(1)}, f32[3264]{0:T(1024)S(1)}, u32[]{:S(2)}, u32[]{:S(2)}) collective-permute-start(f32[3264]{0:T(1024)S(1)} %pad_maximum_fusion.4), channel_id=1, source_target_pairs={{0,8},{8,0},{16,24},{24,16},{1,9},{9,1},{17,25},{25,17},{2,10},{10... | collective-permute-start | bytes 39176 | tf_op jit(solution)/shard_map/ppermute | solution.py:333
  218.1 22.4 %collective-permute-start.19 = (bf16[384,576]{0,1:T(8,128)(2,1)S(1)}, bf16[384,576]{0,1:T(8,128)(2,1)S(1)}, u32[]{:S(2)}, u32[]{:S(2)}) collective-permute-start(bf16[384,576]{0,1:T(8,128)(2,1)S(1)} %add_convert_fusion.5), channel_id=1, source_target_pairs={{8,16},{16,8},{9,17},{17,9},{10,18},{18,10},{11,19},{19,11},{12,20... | collective-permute-start | bytes 1327112 | tf_op jit(solution)/shard_map/ppermute | solution.py:326
  218.8 13.4 %collective-permute-start.23 = (f32[3264]{0:T(1024)S(1)}, f32[3264]{0:T(1024)S(1)}, u32[]{:S(2)}, u32[]{:S(2)}) collective-permute-start(f32[3264]{0:T(1024)S(1)} %fusion.19), channel_id=1, source_target_pairs={{0,16},{8,24},{16,0},{24,8},{1,17},{9,25},{17,1},{25,9},{2,18},{10... | collective-permute-start | bytes 39176 | tf_op jit(solution)/shard_map/ppermute | solution.py:333
  225.5 12.7 %copy-start.12 = (bf16[512,384]{1,0:T(8,128)(2,1)S(1)}, bf16[512,384]{1,0:T(8,128)(2,1)}, u32[]{:S(2)}) copy-start(bf16[512,384]{1,0:T(8,128)(2,1)} %param.16) | copy-start | bytes 1179652
  225.6 12.7 %copy-start.26 = (f32[384]{0:T(512)S(1)}, f32[384]{0:T(512)}, u32[]{:S(2)}) copy-start(f32[384]{0:T(512)} %param.24) | copy-start | bytes 4612
  225.6 12.7 %copy-start.27 = (f32[384]{0:T(512)S(1)}, f32[384]{0:T(512)}, u32[]{:S(2)}) copy-start(f32[384]{0:T(512)} %param.22) | copy-start | bytes 4612
  232.3 9.6 %collective-permute-start.36 = (bf16[768,384]{1,0:T(8,128)(2,1)S(1)}, bf16[768,384]{1,0:T(8,128)(2,1)S(1)}, u32[]{:S(2)}, u32[]{:S(2)}) collective-permute-start(bf16[768,384]{1,0:T(8,128)(2,1)S(1)} %add_convert_fusion.1), channel_id=1, source_target_pairs={{8,16},{16,8},{9,17},{17,9},{10,18},{18,10},{11,19},{19,11},{12,20... | collective-permute-start | bytes 1769480 | tf_op jit(solution)/shard_map/ppermute | solution.py:326
  233.1 1.3 collective-permute-start.32
  234.4 8.9 %collective-permute-start.26 = (bf16[384,768]{1,0:T(8,128)(2,1)S(1)}, bf16[384,768]{1,0:T(8,128)(2,1)S(1)}, u32[]{:S(2)}, u32[]{:S(2)}) collective-permute-start(bf16[384,768]{1,0:T(8,128)(2,1)S(1)} %add_convert_fusion.3), channel_id=1, source_target_pairs={{8,16},{16,8},{9,17},{17,9},{10,18},{18,10},{11,19},{19,11},{12,20... | collective-permute-start | bytes 1769480 | tf_op jit(solution)/shard_map/ppermute | solution.py:326
  235.2 5.2 %collective-permute-start.33 = (f32[1920]{0:T(1024)S(1)}, f32[1920]{0:T(1024)S(1)}, u32[]{:S(2)}, u32[]{:S(2)}) collective-permute-start(f32[1920]{0:T(1024)S(1)} %fusion.24), channel_id=1, source_target_pairs={{0,2},{1,3},{2,0},{3,1},{4,6},{5,7},{6,4},{7,5},{8,10},{9,11},{10,... | collective-permute-start | bytes 23048 | tf_op jit(solution)/shard_map/ppermute | solution.py:333
  240.6 17.4 %collective-permute-start.20 = (bf16[384,576]{0,1:T(8,128)(2,1)S(1)}, bf16[384,576]{0,1:T(8,128)(2,1)S(1)}, u32[]{:S(2)}, u32[]{:S(2)}) collective-permute-start(bf16[384,576]{0,1:T(8,128)(2,1)S(1)} %add_convert_fusion.4), channel_id=1, source_target_pairs={{8,0},{16,24},{9,1},{17,25},{10,2},{18,26},{11,3},{19,27},{12,4},{... | collective-permute-start | bytes 1327112 | tf_op jit(solution)/shard_map/ppermute | solution.py:328
  242.0 28.6 %collective-permute-start.37 = (bf16[768,384]{1,0:T(8,128)(2,1)S(1)}, bf16[768,384]{1,0:T(8,128)(2,1)S(1)}, u32[]{:S(2)}, u32[]{:S(2)}) collective-permute-start(bf16[768,384]{1,0:T(8,128)(2,1)S(1)} %add_convert_fusion), channel_id=1, source_target_pairs={{8,0},{16,24},{9,1},{17,25},{10,2},{18,26},{11,3},{19,27},{12,4},{... | collective-permute-start | bytes 1769480 | tf_op jit(solution)/shard_map/ppermute | solution.py:328
  243.5 39.0 %collective-permute-start.27 = (bf16[384,768]{1,0:T(8,128)(2,1)S(1)}, bf16[384,768]{1,0:T(8,128)(2,1)S(1)}, u32[]{:S(2)}, u32[]{:S(2)}) collective-permute-start(bf16[384,768]{1,0:T(8,128)(2,1)S(1)} %add_convert_fusion.2), channel_id=1, source_target_pairs={{8,0},{16,24},{9,1},{17,25},{10,2},{18,26},{11,3},{19,27},{12,4},{... | collective-permute-start | bytes 1769480 | tf_op jit(solution)/shard_map/ppermute | solution.py:328
  245.4 38.2 %copy-start.21 = (f32[384]{0:T(512)}, f32[384]{0:T(512)S(1)}, u32[]{:S(2)}) copy-start(f32[384]{0:T(512)S(1)} %get-tuple-element.95) | copy-start | bytes 4612
  (18 other events, 82.7 us)

commit v2 on v1

v2 whole, which is shorter than its diff:
```python
import math

import jax
import jax.numpy as jnp
from jax import lax
from jax.experimental import pallas as pl
from jax.experimental.pallas import tpu as pltpu
from jax.sharding import PartitionSpec as P

D = 768
HEAD_DIM = 64
ROT = 16
SEQ_LEN = 1024
EPSILON = 1e-05
BLOCK = 256
F32 = jnp.float32
BF16 = jnp.bfloat16
GROUP = ("row", "col")
VMEM_BYTES = 60 * 1024 * 1024


def dot_nn(a, b):
    return lax.dot_general(a, b, (((1,), (0,)), ((), ())), preferred_element_type=F32)


def dot_tn(a, b):
    return lax.dot_general(a, b, (((0,), (0,)), ((), ())), preferred_element_type=F32)


def dot_nt(a, b):
    return lax.dot_general(a, b, (((1,), (1,)), ((), ())), preferred_element_type=F32)


def normalize(x_rows):
    x = x_rows.astype(F32)
    mean = jnp.mean(x, axis=1, keepdims=True)
    centered = x - mean
    var = jnp.mean(centered * centered, axis=1, keepdims=True)
    inv_std = lax.rsqrt(var + EPSILON)
    return centered * inv_std, inv_std


def norm_back(grad, normed, inv_std):
    mean_grad = jnp.mean(grad, axis=1, keepdims=True)
    mean_cross = jnp.mean(grad * normed, axis=1, keepdims=True)
    return inv_std * (grad - mean_grad - normed * mean_cross)


def mlp_part(x_rows, go, wi_o, wi_p, wo_o, wo_p, b_ref, gain_ref, bias_ref, own_ref, send_acc):
    half = wi_o.shape[0]
    normed, _ = normalize(x_rows)
    h = (normed * gain_ref[...] + bias_ref[...]).astype(BF16)
    pre = dot_nn(h[:, :half], wi_o[...]) + dot_nn(h[:, half:], wi_p[...]) + b_ref[...]
    cdf = 0.5 * (1.0 + lax.erf(pre * (2.0 ** -0.5)))
    hidden = (pre * cdf).astype(BF16)
    slope = cdf + pre * (jnp.exp(-0.5 * pre * pre) * (1.0 / math.sqrt(2.0 * math.pi)))
    mix = jnp.concatenate([dot_nn(hidden, wo_o[...]), dot_nn(hidden, wo_p[...])], axis=1)
    grad_hidden = dot_nt(go[:, :half], wo_o[...]) + dot_nt(go[:, half:], wo_p[...])
    grad_pre = (grad_hidden * slope).astype(BF16)
    own_ref[:half, :] += dot_tn(h[:, :half], grad_pre)
    send_acc[:half, :] += dot_tn(h[:, half:], grad_pre)
    own_ref[half:, :] += dot_tn(hidden, go[:, :half])
    send_acc[half:, :] += dot_tn(hidden, go[:, half:])
    grad_h = jnp.concatenate([dot_nt(grad_pre, wi_o[...]), dot_nt(grad_pre, wi_p[...])], axis=1)
    return normed, mix, grad_h, jnp.sum(grad_pre.astype(F32), axis=0, keepdims=True)


def mlp_first_kernel(
    core_ref, xm_ref, xo_ref, gm_ref, go_ref, wi_o, wo_o, wi_p, wo_p, b_ref, gain_ref, bias_ref,
    again_ref, abias_ref,
    mix_ref, gh_ref, x_out, go_out, h_out, own_ref, send_ref, gb_ref,
    own_acc, acc_ref,
):
    step = pl.program_id(0)

    @pl.when(step == 0)
    def _():
        own_acc[...] = jnp.zeros_like(own_acc)
        acc_ref[...] = jnp.zeros_like(acc_ref)
        gb_ref[...] = jnp.zeros_like(gb_ref)

    held = step // (pl.num_programs(0) // 2) == core_ref[0]
    x_rows = jnp.where(held, xm_ref[...], xo_ref[...])
    go = jnp.where(held, gm_ref[...], go_ref[...])
    x_out[...] = x_rows
    go_out[...] = go
    normed, mix, grad_h, gb = mlp_part(
        x_rows, go, wi_o, wi_p, wo_o, wo_p, b_ref, gain_ref, bias_ref, own_acc, acc_ref
    )
    h_out[...] = (normed * again_ref[...] + abias_ref[...]).astype(BF16)
    mix_ref[...] = mix
    gh_ref[...] = grad_h
    gb_ref[0:1, :] += gb

    @pl.when(step == pl.num_programs(0) - 1)
    def _():
        own_ref[...] = own_acc[...].astype(BF16)
        send_ref[...] = acc_ref[...].astype(BF16)


def mlp_second_kernel(
    x_ref, go_ref, mix_in, gh_in, wi_o, wo_o, wi_p, wo_p, b_ref, gain_ref, bias_ref,
    mix_ref, gh_ref, own_ref, send_ref, gb_ref,
    own_acc, acc_ref,
):
    step = pl.program_id(0)

    @pl.when(step == 0)
    def _():
        own_acc[...] = jnp.zeros_like(own_acc)
        acc_ref[...] = jnp.zeros_like(acc_ref)
        gb_ref[...] = jnp.zeros_like(gb_ref)

    _, mix, grad_h, gb = mlp_part(
        x_ref[...], go_ref[...], wi_o, wi_p, wo_o, wo_p, b_ref, gain_ref, bias_ref, own_acc, acc_ref
    )
    mix_ref[...] = mix_in[...] + mix
    gh_ref[...] = gh_in[...] + grad_h
    gb_ref[0:1, :] += gb

    @pl.when(step == pl.num_programs(0) - 1)
    def _():
        own_ref[...] = own_acc[...].astype(BF16)
        send_ref[...] = acc_ref[...].astype(BF16)


def brief():
    return pl.CostEstimate(flops=1024, transcendentals=0, bytes_accessed=1024)


def whole(a):
    return pl.BlockSpec(a.shape, lambda *i: (0,) * a.ndim)


def shape(s, d):
    return jax.ShapeDtypeStruct(s, d)


def mlp_params():
    return pltpu.CompilerParams(
        dimension_semantics=("arbitrary",), vmem_limit_bytes=VMEM_BYTES
    )


def part_spec(size, at):
    return pl.BlockSpec((size, size), lambda *i: at)


def mlp_first(core, x_mine, x_other, go_mine, go_other, w_in, w_out, pack, b_in, *norms):
    held, width = x_mine.shape
    rows = 2 * held
    half = width // 2
    steps = held // BLOCK

    def held_map(i, core_ref):
        return (jnp.clip(i - core_ref[0] * steps, 0, steps - 1), 0)

    def other_map(i, core_ref):
        return (jnp.clip(i - (1 - core_ref[0]) * steps, 0, steps - 1), 0)

    mine_spec = pl.BlockSpec((BLOCK, width), held_map)
    other_spec = pl.BlockSpec((BLOCK, width), other_map)
    row_spec = pl.BlockSpec((BLOCK, width), lambda i, core_ref: (i, 0))
    outs = [
        shape((rows, width), F32),
        shape((rows, width), F32),
        shape((rows, width), BF16),
        shape((rows, width), BF16),
        shape((rows, width), BF16),
        shape((2 * half, half), BF16),
        shape((2 * half, half), BF16),
        shape((8, half), F32),
    ]
    return pl.pallas_call(
        mlp_first_kernel,
        grid_spec=pltpu.PrefetchScalarGridSpec(
            num_scalar_prefetch=1,
            grid=(rows // BLOCK,),
            in_specs=[mine_spec, other_spec, mine_spec, other_spec]
            + [part_spec(half, (0, 0)), part_spec(half, (0, 0))]
            + [part_spec(half, (0, 0)), part_spec(half, (1, 0))]
            + [pl.BlockSpec((1, half), lambda *i: (0, 0))]
            + [whole(a) for a in norms],
            out_specs=[row_spec] * 5 + [whole(a) for a in outs[5:]],
            scratch_shapes=[pltpu.VMEM((2 * half, half), F32)] * 2,
        ),
        out_shape=outs,
        compiler_params=mlp_params(),
        cost_estimate=brief(),
        name="mlp_first",
    )(core, x_mine, x_other, go_mine, go_other, w_in, w_out, pack, pack, b_in, *norms)


def mlp_second(x_seq, go_seq, mix, gh, w_in, w_out, pack, b_in, *norms):
    rows, width = x_seq.shape
    half = width // 2
    row_spec = pl.BlockSpec((BLOCK, width), lambda i: (i, 0))
    outs = [
        shape((rows, width), F32),
        shape((rows, width), F32),
        shape((2 * half, half), BF16),
        shape((2 * half, half), BF16),
        shape((8, half), F32),
    ]
    return pl.pallas_call(
        mlp_second_kernel,
        grid=(rows // BLOCK,),
        in_specs=[row_spec] * 4
        + [part_spec(half, (0, 1)), part_spec(half, (1, 0))]
        + [part_spec(half, (0, 0)), part_spec(half, (1, 0))]
        + [pl.BlockSpec((1, half), lambda *i: (0, 1))]
        + [whole(a) for a in norms],
        out_specs=[row_spec] * 2 + [whole(a) for a in outs[2:]],
        out_shape=outs,
        scratch_shapes=[pltpu.VMEM((2 * half, half), F32)] * 2,
        compiler_params=mlp_params(),
        cost_estimate=brief(),
        name="mlp_second",
    )(x_seq, go_seq, mix, gh, w_in, w_out, pack, pack, b_in, *norms)


def attn_kernel(
    h_ref, go_ref, wo_ref, wp_ref, b_ref, do_ref, dp_ref, cos_ref, s1_ref, s2_ref,
    segc_ref, segr_ref,
    ctx_out, dj_out, own_ref, send_ref, gb_ref,
    qk_ref, v_ref, dctx_ref, ctxt_ref, dqt_ref, dk_ref, dv_ref,
):
    rows = h_ref.shape[0]
    inner, half = wo_ref.shape
    tiles = rows // BLOCK
    lanes = lax.broadcasted_iota(jnp.int32, (1, 2 * HEAD_DIM), 1)
    scale = jnp.where(lanes < HEAD_DIM, HEAD_DIM ** (-0.5), 1.0)

    for t in range(tiles):
        at = slice(t * BLOCK, (t + 1) * BLOCK)
        joined = (
            dot_nt(h_ref[at, :half], wo_ref[...]) + dot_nt(h_ref[at, half:], wp_ref[...]) + b_ref[0]
        )
        u = joined[:, : 2 * HEAD_DIM]
        turned = (
            u * cos_ref[at, :]
            + pltpu.roll(u, 2 * HEAD_DIM - ROT // 2, 1) * s1_ref[at, :]
            + pltpu.roll(u, ROT // 2, 1) * s2_ref[at, :]
        )
        qk_ref[at, :] = (turned * scale).astype(BF16)
        v_ref[at, :] = joined[:, 2 * HEAD_DIM :].astype(BF16)
        dctx_ref[at, :] = (
            dot_nt(go_ref[at, :half], do_ref[...]) + dot_nt(go_ref[at, half:], dp_ref[...])
        ).astype(BF16)

    k_all = qk_ref[:, HEAD_DIM:]
    kt = k_all.astype(F32).T.astype(BF16)
    vt = v_ref[...].astype(F32).T.astype(BF16)
    for i in range(tiles):
        lo = i * BLOCK
        hi = lo + BLOCK
        q_blk = qk_ref[lo:hi, :HEAD_DIM]
        g_blk = dctx_ref[lo:hi, :]
        st = dot_nt(k_all[:hi], q_blk)
        key_at = lax.broadcasted_iota(jnp.int32, (hi, BLOCK), 0)
        query_at = lax.broadcasted_iota(jnp.int32, (hi, BLOCK), 1) + lo
        allowed = (segc_ref[0:hi, :] == segr_ref[:, lo:hi]) & (key_at <= query_at)
        st = jnp.where(allowed, st, -1e30)
        top = jnp.max(st, axis=0, keepdims=True)
        p = jnp.exp(st - top)
        p = p * (1.0 / jnp.sum(p, axis=0, keepdims=True))
        pb = p.astype(BF16)
        ctxt_ref[:, lo:hi] = dot_nn(vt[:, :hi], pb).astype(BF16)
        dpt = dot_nt(v_ref[0:hi, :], g_blk)
        inner_term = jnp.sum(dpt * p, axis=0, keepdims=True)
        dst = (p * (dpt - inner_term)).astype(BF16)
        dqt_ref[:, lo:hi] = dot_nn(kt[:, :hi], dst)
        dk_new = dot_nn(dst, q_blk)
        dv_new = dot_nn(pb, g_blk)
        if i > 0:
            dk_ref[0:lo, :] += dk_new[:lo]
            dv_ref[0:lo, :] += dv_new[:lo]
        dk_ref[lo:hi, :] = dk_new[lo:]
        dv_ref[lo:hi, :] = dv_new[lo:]

    ctx_out[0] = ctxt_ref[...]
    dq = dqt_ref[...].T
    back = jnp.concatenate([dq * HEAD_DIM ** (-0.5), dk_ref[...]], axis=1)
    turned_back = (
        back * cos_ref[...]
        + pltpu.roll(back * s2_ref[...], 2 * HEAD_DIM - ROT // 2, 1)
        + pltpu.roll(back * s1_ref[...], ROT // 2, 1)
    )
    dj = jnp.concatenate([turned_back.astype(BF16), dv_ref[...].astype(BF16)], axis=1)
    dj_out[0] = dj
    gb_ref[0] = jnp.sum(dj.astype(F32), axis=0, keepdims=True)
    own_ref[0, :inner, :] = dot_tn(dj, h_ref[:, :half]).astype(BF16)
    own_ref[0, inner:, :] = dot_nn(ctxt_ref[...], go_ref[:, :half]).astype(BF16)
    send_ref[0, :inner, :] = dot_tn(dj, h_ref[:, half:]).astype(BF16)
    send_ref[0, inner:, :] = dot_nn(ctxt_ref[...], go_ref[:, half:]).astype(BF16)


def attn_head(first, count, h_seq, go_seq, wq_o, wq_p, b_heads, wd_o, wd_p, *tables):
    rows = h_seq.shape[0]
    half = wq_o.shape[1]
    inner = 3 * HEAD_DIM
    skip = wq_o.shape[0] // HEAD_DIM

    def per_head(a, base):
        return pl.BlockSpec((1,) + a.shape[1:], lambda i: (i + base,) + (0,) * (a.ndim - 1))

    outs = [
        shape((count, HEAD_DIM, rows), BF16),
        shape((count, rows, inner), BF16),
        shape((count, inner + HEAD_DIM, half), BF16),
        shape((count, inner + HEAD_DIM, half), BF16),
        shape((count, 1, inner), F32),
    ]
    args = (h_seq, go_seq, wq_o, wq_p, b_heads, wd_o, wd_p) + tables
    specs = [whole(a) for a in args]
    for j in (2, 3):
        specs[j] = pl.BlockSpec((inner, half), lambda i: (i + first, 0))
    specs[4] = per_head(b_heads, first)
    specs[5] = pl.BlockSpec((HEAD_DIM, half), lambda i: (i + first, 0))
    specs[6] = pl.BlockSpec((HEAD_DIM, half), lambda i: (i + first + skip, 0))
    return pl.pallas_call(
        attn_kernel,
        grid=(count,),
        in_specs=specs,
        out_specs=[per_head(a, 0) for a in outs],
        out_shape=outs,
        scratch_shapes=[
            pltpu.VMEM((rows, 2 * HEAD_DIM), BF16),
            pltpu.VMEM((rows, HEAD_DIM), BF16),
            pltpu.VMEM((rows, HEAD_DIM), BF16),
            pltpu.VMEM((HEAD_DIM, rows), BF16),
            pltpu.VMEM((HEAD_DIM, rows), F32),
            pltpu.VMEM((rows, HEAD_DIM), F32),
            pltpu.VMEM((rows, HEAD_DIM), F32),
        ],
        compiler_params=pltpu.CompilerParams(
            dimension_semantics=("arbitrary",), vmem_limit_bytes=VMEM_BYTES
        ),
        cost_estimate=brief(),
        name="attn_head",
    )(*args)


def close_kernel(
    core_ref, x_ref, mix_ref, gh_ref, c01, c2, j01, j2, wq_o, wq_p, wd_o, wd_p,
    again_ref, mgain_ref,
    mix_send, mix_keep, dx_send, dx_keep, vec_ref,
):
    del core_ref
    step = pl.program_id(0)
    sending = step < pl.num_programs(0) // 2

    @pl.when(step == 0)
    def _():
        vec_ref[...] = jnp.zeros_like(vec_ref)

    ctxt = jnp.concatenate([c01[0], c01[1], c2[0]], axis=0)
    mix = mix_ref[...] + jnp.concatenate(
        [dot_tn(ctxt, wd_o[...]), dot_tn(ctxt, wd_p[...])], axis=1
    )
    grad_h = jnp.concatenate(
        [
            sum(
                dot_nn(j, w[n * 3 * HEAD_DIM : (n + 1) * 3 * HEAD_DIM, :])
                for n, j in enumerate((j01[0], j01[1], j2[0]))
            )
            for w in (wq_o, wq_p)
        ],
        axis=1,
    )
    normed, inv_std = normalize(x_ref[...])
    vec_ref[0:1, :] += jnp.sum(grad_h * normed, axis=0, keepdims=True)
    vec_ref[1:2, :] += jnp.sum(grad_h, axis=0, keepdims=True)
    grad_m = gh_ref[...]
    vec_ref[2:3, :] += jnp.sum(grad_m * normed, axis=0, keepdims=True)
    vec_ref[3:4, :] += jnp.sum(grad_m, axis=0, keepdims=True)
    dx = norm_back(grad_h * again_ref[...] + grad_m * mgain_ref[...], normed, inv_std)

    @pl.when(sending)
    def _():
        mix_send[...] = mix.astype(BF16)
        dx_send[...] = dx.astype(BF16)

    @pl.when(jnp.logical_not(sending))
    def _():
        mix_keep[...] = mix.astype(BF16)
        dx_keep[...] = dx.astype(BF16)


def close_layer(core, x_seq, mix, gh, ctx, djs, *weights):
    rows, width = x_seq.shape
    held = rows // 2
    steps = held // BLOCK

    def block_of(i, core_ref):
        return jnp.where(i < steps, (1 - core_ref[0]) * steps + i, (core_ref[0] - 1) * steps + i)

    row_spec = pl.BlockSpec((BLOCK, width), lambda i, c: (block_of(i, c), 0))
    send_spec = pl.BlockSpec((BLOCK, width), lambda i, c: (jnp.minimum(i, steps - 1), 0))
    keep_spec = pl.BlockSpec((BLOCK, width), lambda i, c: (jnp.maximum(i - steps, 0), 0))
    ctx_specs = [
        pl.BlockSpec((a.shape[0], HEAD_DIM, BLOCK), lambda i, c: (0, 0, block_of(i, c)))
        for a in ctx
    ]
    dj_specs = [
        pl.BlockSpec((a.shape[0], BLOCK, 3 * HEAD_DIM), lambda i, c: (0, block_of(i, c), 0))
        for a in djs
    ]
    specs = [whole(a) for a in weights]
    wide, half = weights[0].shape
    deep = weights[2].shape[0]
    specs[1] = pl.BlockSpec((wide, half), lambda *i: (0, 0))
    specs[3] = pl.BlockSpec((deep, half), lambda *i: (wide // deep, 0))
    outs = [
        shape((held, width), BF16),
        shape((held, width), BF16),
        shape((held, width), BF16),
        shape((held, width), BF16),
        shape((8, width), F32),
    ]
    return pl.pallas_call(
        close_kernel,
        grid_spec=pltpu.PrefetchScalarGridSpec(
            num_scalar_prefetch=1,
            grid=(rows // BLOCK,),
            in_specs=[row_spec] * 3 + ctx_specs + dj_specs + specs,
            out_specs=[send_spec, keep_spec, send_spec, keep_spec, whole(outs[4])],
        ),
        out_shape=outs,
        compiler_params=pltpu.CompilerParams(
            dimension_semantics=("arbitrary",), vmem_limit_bytes=VMEM_BYTES
        ),
        cost_estimate=brief(),
        name="close_layer",
    )(core, x_seq, mix, gh, *ctx, *djs, *weights)


def group_perm(n_row, n_col, target):
    pairs = []
    for r in range(n_row):
        for c in range(n_col):
            to = target(r, c // 2, c % 2)
            if to is not None:
                pairs.append((r * n_col + c, to[0] * n_col + 2 * to[1] + to[2]))
    return pairs


def swap_row(value):
    return lax.ppermute(value, "row", [(0, 1), (1, 0)])


def dp_inward(value):
    return lax.ppermute(value, "dp", [(0, 1), (3, 2)])


def dp_middle(value, inward):
    pair = (value.astype(F32) + inward.astype(F32)).astype(BF16)
    return pair, lax.ppermute(pair, "dp", [(1, 2), (2, 1)])


def dp_outward(pair, other):
    total = (pair.astype(F32) + other.astype(F32)).astype(BF16)
    return total, lax.ppermute(total, "dp", [(1, 0), (2, 3)])


def dp_finish(total, outward=None):
    if outward is None:
        return total
    place = lax.axis_index("dp")
    return jnp.where((place == 1) | (place == 2), total, outward).astype(F32)


def swap_sum(value, axis, size, bit):
    return value + lax.ppermute(value, axis, [(i, i ^ bit) for i in range(size)])


def local(
    block_input, w_qkv, b_qkv, w_in, b_in, w_dense, b_dense, w_out, b_out,
    ln_attn_gain, ln_attn_bias, ln_mlp_gain, ln_mlp_bias, segments, positions, d_out,
):
    n_row = lax.axis_size("row")
    n_col = lax.axis_size("col")
    n_dp = lax.axis_size("dp")
    row = lax.axis_index("row")
    col = lax.axis_index("col")
    half = block_input.shape[1]
    barrier = lax.optimization_barrier
    upper = col // 2
    core = col % 2
    home = row == upper
    heads = w_qkv.shape[1] // (3 * HEAD_DIM)

    spread = group_perm(
        n_row, n_col, lambda r, u, k: (r, 1 - u, k) if r == u else (1 - r, u, k)
    )
    cross = group_perm(n_row, n_col, lambda r, u, k: None if r == u else (1 - r, 1 - u, k))
    pair = group_perm(n_row, n_col, lambda r, u, k: (r, u, 1 - k))
    forward = group_perm(n_row, n_col, lambda r, u, k: (r, 1 - u, k) if r == u else None)
    collect = group_perm(
        n_row, n_col, lambda r, u, k: (1 - r, u, k) if r == u else (r, 1 - u, k)
    )

    chain = n_dp == 4
    inner = 3 * HEAD_DIM
    wq_t = w_qkv.T
    pack_a = jnp.concatenate([w_in[:, :half], w_out[:half]], axis=0)
    pack_b = jnp.concatenate([w_in[:, half:], w_out[half:]], axis=0)
    pack_c = jnp.concatenate([wq_t, w_dense], axis=0)
    norms = jnp.stack([ln_attn_gain, ln_attn_bias, ln_mlp_gain, ln_mlp_bias])
    core_at = core.reshape(1)

    at_seq = row * SEQ_LEN
    seg_seq = lax.dynamic_slice_in_dim(segments, at_seq, SEQ_LEN)
    pos_seq = lax.dynamic_slice_in_dim(positions, at_seq, SEQ_LEN)
    lane = jnp.arange(2 * HEAD_DIM) % HEAD_DIM
    freq_steps = (lane % (ROT // 2)).astype(F32) * (-2.0 * math.log(10000.0) / ROT)
    freq = jnp.where(lane < ROT, jnp.exp(freq_steps), 0.0)
    angles = pos_seq.astype(F32)[:, None] * freq[None, :]
    cos_table = jnp.cos(angles)
    sin_table = jnp.sin(angles)
    sin_up = jnp.where(lane < ROT // 2, -sin_table, 0.0)
    sin_down = jnp.where((lane >= ROT // 2) & (lane < ROT), sin_table, 0.0)

    def join(block, near, far):
        return jnp.concatenate(
            [jnp.where(home, block, near), jnp.where(home, near, far)], axis=1
        )

    d_out_f = d_out.astype(F32)
    d_sum = jnp.sum(d_out_f, axis=0)
    norms_got = swap_row(norms)
    near_x = lax.ppermute(block_input, GROUP, spread)
    segc = seg_seq[:, None]
    go_in, cos_table, sin_up, sin_down, pack_a, pack_b, pack_c, segc, d_sum = barrier(
        (d_out, cos_table, sin_up, sin_down, pack_a, pack_b, pack_c, segc, d_sum)
    )
    near_go = lax.ppermute(go_in, GROUP, spread)
    near_x, norms, norms_got, pack_a = barrier((near_x, norms, norms_got, pack_a))
    far_x = lax.ppermute(near_x, GROUP, forward)
    got_a = swap_row(pack_a)
    far_go = lax.ppermute(near_go, GROUP, forward)
    x_mine = join(block_input, near_x, far_x)
    x_other = lax.ppermute(x_mine, GROUP, pair)
    far_go, got_a, pack_b = barrier((far_go, got_a, pack_b))
    go_mine = join(d_out, near_go, far_go)
    go_other = lax.ppermute(go_mine, GROUP, pair)
    got_b = swap_row(pack_b)
    x_other, pack_c = barrier((x_other, pack_c))
    got_c = swap_row(pack_c)
    norms = jnp.concatenate([norms, norms_got], axis=1)

    mix, gh, x_seq, go_seq, h_seq, own_a, send_a, gb_a = mlp_first(
        core_at, x_mine, x_other, go_mine, go_other, w_in, w_out, got_a, b_in[None],
        norms[2:3], norms[3:4], norms[0:1], norms[1:2],
    )
    x_seq, send_a = barrier((x_seq, send_a))
    back_a = swap_row(send_a)
    mix, gh, own_b, send_b, gb_b = mlp_second(
        x_seq, go_seq, mix, gh, w_in, w_out, got_b, b_in[None], norms[2:3], norms[3:4]
    )
    h_seq, send_b, got_c = barrier((h_seq, send_b, got_c))
    back_b = swap_row(send_b)
    width = wq_t.shape[0]
    heads_args = (
        wq_t, got_c, b_qkv.reshape(heads, 1, inner), w_dense, got_c,
        cos_table, sin_up, sin_down, segc, seg_seq[None, :],
    )

    def payload_sum(own, got):
        return (own.astype(F32) + got.astype(F32)).astype(BF16)

    heads01 = attn_head(0, heads - 1, h_seq, go_seq, *heads_args)
    go_seq, heads01, back_a = barrier((go_seq, heads01, back_a))
    back01 = swap_row(heads01[3])
    sum_a = payload_sum(own_a, back_a)
    if chain:
        in_a = dp_inward(sum_a)
    head2 = attn_head(heads - 1, 1, h_seq, go_seq, *heads_args)
    x_seq, head2, back_b = barrier((x_seq, head2, back_b))
    back2 = swap_row(head2[3])
    sum_b = payload_sum(own_b, back_b)
    if chain:
        in_b = dp_inward(sum_b)
    done = [heads01, head2]
    mix_s, mix_k, dx_s, dx_k, attn_vec = close_layer(
        core_at, x_seq, mix, gh, [a[0] for a in done], [a[1] for a in done],
        wq_t, got_c, w_dense, got_c, norms[0:1], norms[2:3],
    )
    if chain:
        mix_s, dx_s, in_a, sum_a, back01 = barrier((mix_s, dx_s, in_a, sum_a, back01))
        pair_a, other_a = dp_middle(sum_a, in_a)
    mix_got = lax.ppermute(mix_s, GROUP, pair)
    dx_got = lax.ppermute(dx_s, GROUP, pair)
    sum_c = payload_sum(heads01[2], back01).reshape(-1, half)
    if chain:
        in_c = dp_inward(sum_c)
    hid = b_in.shape[0]
    wide = jnp.concatenate([gb_a[0], gb_b[0]] + [a[4].reshape(-1) for a in done])
    mine = jnp.concatenate([attn_vec[:4, :half].reshape(-1), wide])
    theirs = jnp.concatenate([attn_vec[:4, half:].reshape(-1), wide])
    vec_got = swap_row(theirs)
    mix_got, dx_got, back2 = barrier((mix_got, dx_got, back2))
    sum_d = payload_sum(head2[2], back2).reshape(-1, half)
    if chain:
        in_d = dp_inward(sum_d)

    def reduce_start(got, kept):
        low_sum = (kept.astype(F32) + got.astype(F32)).astype(BF16)
        near = lax.ppermute(
            jnp.where(home, low_sum[:, half:], low_sum[:, :half]), GROUP, collect
        )
        return near, lax.ppermute(low_sum[:, half:], GROUP, cross), low_sum[:, :half]

    def reduce_end(near, far, kept):
        return near.astype(F32) + jnp.where(home, kept, far).astype(F32)

    mix_parts = reduce_start(mix_got, mix_k)
    dx_parts = reduce_start(dx_got, dx_k)
    vecs = mine + vec_got
    wide = vecs[4 * half :]
    rest = jnp.concatenate([vecs[: 4 * half], d_sum])
    rest = swap_sum(rest, "col", n_col, 1)
    rest = swap_sum(rest, "col", n_col, 2)
    vecs = jnp.concatenate([rest, wide])
    if chain:
        in_b, sum_b, other_a = barrier((in_b, sum_b, other_a))
        pair_b, other_b = dp_middle(sum_b, in_b)
        totals_a = dp_outward(pair_a, other_a)
        in_c, sum_c, in_d, sum_d = barrier((in_c, sum_c, in_d, sum_d))
        pair_c, other_c = dp_middle(sum_c, in_c)
        pair_d, other_d = dp_middle(sum_d, in_d)
        mix_parts, dx_parts, vecs, other_b = barrier((mix_parts, dx_parts, vecs, other_b))
        totals_b = dp_outward(pair_b, other_b)
        vecs = swap_sum(vecs, "dp", 4, 1)
        vecs, other_c, other_d, totals_a = barrier((vecs, other_c, other_d, totals_a))
        totals_c = dp_outward(pair_c, other_c)
        totals_d = dp_outward(pair_d, other_d)
        vecs = swap_sum(vecs, "dp", 4, 2)
    else:
        vecs = lax.psum(vecs, "dp")
        totals_a, totals_b, totals_c, totals_d = (
            (lax.psum(v.astype(F32), "dp"),) for v in (sum_a, sum_b, sum_c, sum_d)
        )

    def finish(totals, *at):
        return dp_finish(*[a[at] for a in totals])

    block_output = (
        block_input.astype(F32) + reduce_end(*mix_parts) + b_dense + b_out
    ).astype(BF16)
    d_input = d_out_f + reduce_end(*dx_parts)
    upper_rows = slice(0, half)
    lower_rows = slice(half, 2 * half)
    grad_w_in = jnp.concatenate(
        [finish(totals_a, upper_rows), finish(totals_b, upper_rows)], axis=1
    )
    grad_w_out = jnp.concatenate(
        [finish(totals_a, lower_rows), finish(totals_b, lower_rows)], axis=0
    )
    split = [finish(totals_c, slice(n * (inner + HEAD_DIM), (n + 1) * (inner + HEAD_DIM)))
             for n in range(heads - 1)] + [finish(totals_d, slice(0, inner + HEAD_DIM))]
    grad_w_qkv = jnp.concatenate([a[:inner] for a in split], axis=0).T
    grad_w_dense = jnp.concatenate([a[inner:] for a in split], axis=0)
    rest = vecs[: 5 * half].reshape(5, half)
    grad_b_in = vecs[5 * half : 5 * half + hid]
    grad_b_qkv = vecs[5 * half + hid :]
    return (
        block_output, d_input, grad_w_qkv, grad_b_qkv, grad_w_in, grad_b_in,
        grad_w_dense, rest[4], grad_w_out, rest[4], rest[0], rest[1], rest[2], rest[3],
    )


def solution(mesh):
    token = P(("dp", "col"), "row")
    placed = (
        token, P("row", "col"), P("col"), P("row", "col"), P("col"), P("col", "row"), P("row"),
        P("col", "row"), P("row"), P("row"), P("row"), P("row"), P("row"), P("dp"), P("dp"), token,
    )
    return jax.shard_map(
        local,
        mesh=mesh,
        in_specs=placed,
        out_specs=(
            token, token, P("row", "col"), P("col"), P("row", "col"), P("col"), P("col", "row"),
            P("row"), P("col", "row"), P("row"), P("row"), P("row"), P("row"), P("row"),
        ),
        check_vma=False,
    )
```

time: 286 us -> 210 us (0.73)
  waiting for transfers between devices: 114 us -> 50.3 us
  other arithmetic: 40 us -> 20.3 us
  starting transfers between devices: 49.2 us -> 58.7 us
  local copies, waits for them, and re-layouts: 24.7 us -> 15.4 us
  Pallas kernels: 55.3 us -> 62.3 us
    ppermute x10 -> x9, waiting for transfers between devices: 38.5 us -> 0.02 us  [swap_row(): return lax.ppermute(value, 'row', [(0, 1), (1, 0)])]
    ppermute x24, starting transfers between devices: 29.4 us -> 42.6 us  [the longest x4 17.4 us: dp_inward(): return lax.ppermute(value, 'dp', [(0, 1), (3, 2)])]
    ppermute x4, waiting for transfers between devices: 19.6 us -> 6.98 us  [swap_sum(): lax.ppermute(value, axis, [(i, i ^ bit) for i in range(size)])]
    ppermute x24, waiting for transfers between devices: 55.6 us -> 43.3 us  [the longest x4 13.5 us: dp_outward(): return (total, lax.ppermute(total, 'dp', [(1, 0), (2, 3)]))]
    select_n x7 -> x4, other arithmetic: 11.9 us -> 2.5 us  [the longest x2 2.36 us: join(): jnp.where(home, block, near)]
    convert_element_type x19 -> x16, other arithmetic: 14.3 us -> 7.05 us  [the longest x3 3.63 us: payload_sum(): return (own.astype(F32) + got.astype(F32)).astype(BF16)]
    pallas_call x2 -> x5, Pallas kernels: 55.3 us -> 62.3 us  [the longest x2 28.4 us: attn_head(): pl.pallas_call(attn_kernel, grid=(count,), in_specs=specs, out_specs=[per...]
    slice x13 -> x18, local copies, waits for them, and re-layouts: 11.5 us -> 6.06 us  [the longest x2 1.22 us: local(): pack_b = jnp.concatenate([w_in[:, half:], w_out[half:]], axis=0)]
  transfers between devices with their start and end apart: 38 -> 37, of which waited for: 13 -> 12; matrix products, arithmetic and copies ran while one was open for 19% -> 13% of each run, Pallas kernels for 0% -> 30%
where the time goes in v2:
time: 210 us; the launch traced here: 208 us
  Pallas kernels  62.3 us (30%)
  starting transfers between devices  58.7 us (28%)
  waiting for transfers between devices  50.3 us (24%)
  other arithmetic  20.3 us (10%)
  local copies, waits for them, and re-layouts  15.4 us (7%)
    pallas_call x2, Pallas kernels, attn_head(): pl.pallas_call(attn_kernel, grid=(count,), in_specs=specs, out_specs=[per...  28.4 us
    ppermute x4, starting transfers between devices, dp_inward(): return lax.ppermute(value, 'dp', [(0, 1), (3, 2)])  17.4 us
    ppermute x4, waiting for transfers between devices, dp_outward(): return (total, lax.ppermute(total, 'dp', [(1, 0), (2, 3)]))  13.5 us
    pallas_call x1, Pallas kernels, mlp_first(): pl.pallas_call(mlp_first_kernel, grid_spec=pltpu.PrefetchScalarGridSpec(n...  12.9 us
    pallas_call x1, Pallas kernels, mlp_second(): pl.pallas_call(mlp_second_kernel, grid=(rows // BLOCK,), in_specs=[row_sp...  12.5 us
    ppermute x9, starting transfers between devices, swap_row(): return lax.ppermute(value, 'row', [(0, 1), (1, 0)])  10.1 us
    ppermute x2, waiting for transfers between devices, reduce_start(): lax.ppermute(jnp.where(home, low_sum[:, half:], low_sum[:, :half]), GROUP...  9.45 us
    pallas_call x1, Pallas kernels, close_layer(): pl.pallas_call(close_kernel, grid_spec=pltpu.PrefetchScalarGridSpec(num_s...  8.51 us
  transfers between devices with their start and end apart: 37, of which 12 were waited for; matrix products, arithmetic and copies ran while one was open for 13% of the time, Pallas kernels for 30%

profile of v2, /device:TPU:0, one launch (start us, length us, event | category | flops | bytes accessed | tf_op | source)
XLA Modules:
  0.0 208.5 jit_solution(703856144075295833)
XLA Ops:
  3.5 3.0 %collective-permute-start.1 = (f32[4,384]{1,0:T(4,128)S(1)}, f32[4,384]{1,0:T(4,128)S(1)}, u32[]{:S(2)}, u32[]{:S(2)}) collective-permute-start(f32[4,384]{1,0:T(4,128)S(1)} %pad_maximum_fusion.8), channel_id=1, source_target_pairs={{0,4},{4,0},{1,5},{5,1},{2,6},{6,2},{3,7},{7,3},{8,12},{12,8},{9,1... | collective-permute-start | bytes 18440 | tf_op jit(solution)/shard_map/ppermute | solution.py:449
  6.5 1.5 collective-permute-start
  8.0 1.2 fusion.12
  9.4 1.1 pad_maximum_fusion.2
  10.6 3.2 %fusion = (f32[1024,128]{1,0:T(8,128)}, f32[1024,128]{1,0:T(8,128)}, f32[1024,128]{1,0:T(8,128)}) fusion(f32[128]{0:T(128)S(1)} %compare_select_fusion.2, f32[1024]{0:T(1024)S(1)} %dynamic-slice_convert_fusion, pred[128]{0:T(512)(128)(4,1)S(1)} %get-tuple-element.242, pred[128]{0:T(512)(128)(4,1)S(1)} %get-tuple-element.243), kind=kLoop, calls=%fused_computation.19 | loop fusion | flops 524288 | bytes 1577728 | tf_op jit(solution)/shard_map/jit(_where)/select_n | solution.py:522
  15.2 2.7 %collective-permute-done = bf16[512,384]{1,0:T(8,128)(2,1)S(1)} collective-permute-done((bf16[512,384]{1,0:T(8,128)(2,1)}, bf16[512,384]{1,0:T(8,128)(2,1)S(1)}, u32[]{:S(2)}, u32[]{:S(2)}) %collective-permute-start) | collective-permute-done | bytes 393248 | tf_op jit(solution)/shard_map/ppermute | solution.py:532
  17.9 4.3 %collective-permute-start.2 = (bf16[512,384]{1,0:T(8,128)(2,1)S(1)}, bf16[512,384]{1,0:T(8,128)(2,1)S(1)}, u32[]{:S(2)}, u32[]{:S(2)}) collective-permute-start(bf16[512,384]{1,0:T(8,128)(2,1)S(1)} %collective-permute-done), channel_id=1, source_target_pairs={{0,2},{1,3},{6,4},{7,5},{8,10},{9,11},{14,12},{15,13},{16,18},{17,... | collective-permute-start | bytes 1179656 | tf_op jit(solution)/shard_map/ppermute | solution.py:539
  22.3 4.6 %collective-permute-done.4 = bf16[512,384]{1,0:T(8,128)(2,1)} collective-permute-done((bf16[512,384]{1,0:T(8,128)(2,1)S(1)}, bf16[512,384]{1,0:T(8,128)(2,1)}, u32[]{:S(2)}, u32[]{:S(2)}) %collective-permute-start.4) | collective-permute-done | bytes 393248 | tf_op jit(solution)/shard_map/ppermute | solution.py:537
  26.8 3.8 %collective-permute-start.5 = (bf16[512,384]{1,0:T(8,128)(2,1)}, bf16[512,384]{1,0:T(8,128)(2,1)S(1)}, u32[]{:S(2)}, u32[]{:S(2)}) collective-permute-start(bf16[512,384]{1,0:T(8,128)(2,1)} %collective-permute-done.4), channel_id=1, source_target_pairs={{0,2},{1,3},{6,4},{7,5},{8,10},{9,11},{14,12},{15,13},{16,18},{17,... | collective-permute-start | bytes 1179656 | tf_op jit(solution)/shard_map/ppermute | solution.py:541
  30.7 3.9 %collective-permute-done.2 = bf16[512,384]{1,0:T(8,128)(2,1)S(1)} collective-permute-done((bf16[512,384]{1,0:T(8,128)(2,1)S(1)}, bf16[512,384]{1,0:T(8,128)(2,1)S(1)}, u32[]{:S(2)}, u32[]{:S(2)}) %collective-permute-start.2) | collective-permute-done | bytes 393248 | tf_op jit(solution)/shard_map/ppermute | solution.py:539
  34.6 1.1 broadcast_select_fusion.5
  35.9 5.8 %collective-permute-done.5 = bf16[512,384]{1,0:T(8,128)(2,1)S(1)} collective-permute-done((bf16[512,384]{1,0:T(8,128)(2,1)}, bf16[512,384]{1,0:T(8,128)(2,1)S(1)}, u32[]{:S(2)}, u32[]{:S(2)}) %collective-permute-start.5) | collective-permute-done | bytes 393248 | tf_op jit(solution)/shard_map/ppermute | solution.py:541
  41.7 1.3 broadcast_select_fusion.3
  44.2 1.2 collective-permute-start.8
  46.9 12.9 %mlp_first.1 = (f32[1024,768]{1,0:T(8,128)}, f32[1024,768]{1,0:T(8,128)}, bf16[1024,768]{1,0:T(8,128)(2,1)}, bf16[1024,768]{1,0:T(8,128)(2,1)}, bf16[1024,768]{1...) custom-call(s32[1]{0:T(128)} %bitcast.core_ref, ...), custom_call_target="tpu_custom_call" | custom-call | flops 1024 | bytes 1024 | tf_op jit(solution)/shard_map/mlp_first/pallas_call | solution.py:174
  59.8 1.3 collective-permute-start.10
  61.9 12.5 %mlp_second.1 = (f32[1024,768]{1,0:T(8,128)}, f32[1024,768]{1,0:T(8,128)}, bf16[768,384]{1,0:T(8,128)(2,1)}, bf16[768,384]{1,0:T(8,128)(2,1)}, f32[8,384]{1,0:T(8,128)}) custom-call(bf16[1024,768]{1,0:T(8,128)(2,1)} %get-tuple-element.147.x_ref, bf16[1024,768]{1,0:T(8,128)(2,1)} %get-tuple-element.140.go_ref, f32[1024,768]{1,0:T(8,128)} %get-tuple-element.123.mix_in, ...), custom_call_target="tpu_custom_call" | custom-call | flops 1024 | bytes 1024 | tf_op jit(solution)/shard_map/mlp_second/pallas_call | solution.py:205
  75.2 1.0 copy.30.segc_ref
  78.4 17.9 %attn_head.2 = (bf16[2,64,1024]{2,1,0:T(8,128)(2,1)}, bf16[2,1024,192]{2,1,0:T(8,128)(2,1)}, bf16[2,256,384]{2,1,0:T(8,128)(2,1)}, bf16[2,256,384]{2,1,0:T(8,128)(2,1)}, f32[2,1,192]{2,1,0:T(1,128)}) custom-call(bf16[1024,768]{1,0:T(8,128)(2,1)} %get-tuple-element.128.h_ref, bf16[1024,768]{1,0:T(8,128)(2,1)} %get-tuple-element.140.go_ref, ...), custom_call_target="tpu_custom_call" | custom-call | flops 1024 | bytes 1024 | tf_op jit(solution)/shard_map/attn_head/pallas_call | solution.py:321
  96.3 1.2 add_convert_fusion.7
  97.6 3.9 %collective-permute-start.12 = (bf16[768,384]{1,0:T(8,128)(2,1)S(1)}, bf16[768,384]{1,0:T(8,128)(2,1)S(1)}, u32[]{:S(2)}, u32[]{:S(2)}) collective-permute-start(bf16[768,384]{1,0:T(8,128)(2,1)S(1)} %add_convert_fusion.7), channel_id=1, source_target_pairs={{0,8},{24,16},{1,9},{25,17},{2,10},{26,18},{3,11},{27,19},{4,12},{... | collective-permute-start | bytes 1769480 | tf_op jit(solution)/shard_map/ppermute | solution.py:453
  101.5 10.5 %attn_head.3 = (bf16[1,64,1024]{2,1,0:T(8,128)(2,1)}, bf16[1,1024,192]{2,1,0:T(8,128)(2,1)}, bf16[1,256,384]{2,1,0:T(8,128)(2,1)}, bf16[1,256,384]{2,1,0:T(8,128)(2,1)}, f32[1,1,192]{2,1,0:T(1,128)}) custom-call(bf16[1024,768]{1,0:T(8,128)(2,1)} %get-tuple-element.128.h_ref, bf16[1024,768]{1,0:T(8,128)(2,1)} %get-tuple-element.140.go_ref, ...), custom_call_target="tpu_custom_call" | custom-call | flops 1024 | bytes 1024 | tf_op jit(solution)/shard_map/attn_head/pallas_call | solution.py:321
  112.0 1.3 collective-permute-start.13
  114.2 8.5 %close_layer.1 = (bf16[512,768]{1,0:T(8,128)(2,1)}, bf16[512,768]{1,0:T(8,128)(2,1)}, bf16[512,768]{1,0:T(8,128)(2,1)}, bf16[512,768]{1,0:T(8,128)(2,1)}, f32[8,768]{1,0:T(8,128)}) custom-call(s32[1]{0:T(128)} %bitcast.core_ref, bf16[1024,768]{1,0:T(8,128)(2,1)} %get-tuple-element.147.x_ref, f32[1024,768]{1,0:T(8,128)} %get-tuple-element.148.mix_ref, ...), custom_call_target="tpu_custom_call" | custom-call | flops 1024 | bytes 1024 | tf_op jit(solution)/shard_map/close_layer/pallas_call | solution.py:421
  124.4 1.2 add_convert_fusion.6
  125.6 2.3 %collective-permute-start.24 = (bf16[768,384]{1,0:T(8,128)(2,1)S(1)}, bf16[768,384]{1,0:T(8,128)(2,1)}, u32[]{:S(2)}, u32[]{:S(2)}) collective-permute-start(bf16[768,384]{1,0:T(8,128)(2,1)S(1)} %add_convert_fusion.6), channel_id=1, source_target_pairs={{0,8},{24,16},{1,9},{25,17},{2,10},{26,18},{3,11},{27,19},{4,12},{... | collective-permute-start | bytes 1769480 | tf_op jit(solution)/shard_map/ppermute | solution.py:453
  129.1 2.2 %collective-permute-start.23 = (f32[1920]{0:T(1024)S(1)}, f32[1920]{0:T(1024)S(1)}, u32[]{:S(2)}, u32[]{:S(2)}) collective-permute-start(f32[1920]{0:T(1024)S(1)} %fusion.17), channel_id=1, source_target_pairs={{0,2},{1,3},{2,0},{3,1},{4,6},{5,7},{6,4},{7,5},{8,10},{9,11},{10,... | collective-permute-start | bytes 23048 | tf_op jit(solution)/shard_map/ppermute | solution.py:474
  133.5 1.2 add_convert_fusion.10
  134.7 3.3 %collective-permute-done.24 = bf16[768,384]{1,0:T(8,128)(2,1)} collective-permute-done((bf16[768,384]{1,0:T(8,128)(2,1)S(1)}, bf16[768,384]{1,0:T(8,128)(2,1)}, u32[]{:S(2)}, u32[]{:S(2)}) %collective-permute-start.24) | collective-permute-done | bytes 589856 | tf_op jit(solution)/shard_map/ppermute | solution.py:453
  138.1 4.5 %collective-permute-start.27 = (bf16[512,384]{1,0:T(8,128)(2,1)S(1)}, bf16[512,384]{1,0:T(8,128)(2,1)S(1)}, u32[]{:S(2)}, u32[]{:S(2)}) collective-permute-start(bf16[512,384]{1,0:T(8,128)(2,1)S(1)} %bitcast.14), channel_id=1, source_target_pairs={{0,8},{24,16},{1,9},{25,17},{2,10},{26,18},{3,11},{27,19},{4,12},{... | collective-permute-start | bytes 1179656 | tf_op jit(solution)/shard_map/ppermute | solution.py:453
  142.6 1.2 add_convert_fusion.4
  144.9 6.7 %collective-permute-start.28 = (bf16[256,384]{1,0:T(8,128)(2,1)S(1)}, bf16[256,384]{1,0:T(8,128)(2,1)S(1)}, u32[]{:S(2)}, u32[]{:S(2)}) collective-permute-start(bf16[256,384]{1,0:T(8,128)(2,1)S(1)} %fusion.3), channel_id=1, source_target_pairs={{0,8},{24,16},{1,9},{25,17},{2,10},{26,18},{3,11},{27,19},{4,12},{... | collective-permute-start | bytes 589832 | tf_op jit(solution)/shard_map/ppermute | solution.py:453
  151.9 1.1 collective-permute-start.19
  154.0 3.7 %collective-permute-start.17 = (bf16[512,384]{1,0:T(8,128)(2,1)S(1)}, bf16[512,384]{1,0:T(8,128)(2,1)S(1)}, u32[]{:S(2)}, u32[]{:S(2)}) collective-permute-start(bf16[512,384]{1,0:T(8,128)(2,1)S(1)} %get-tuple-element.210), channel_id=1, source_target_pairs={{0,4},{1,5},{2,0},{3,1},{4,6},{5,7},{6,2},{7,3},{8,12},{9,13},{10,... | collective-permute-start | bytes 1179656 | tf_op jit(solution)/shard_map/ppermute | solution.py:609
  158.6 1.3 collective-permute-start.32
  159.9 4.1 %collective-permute-done.19 = bf16[512,384]{1,0:T(8,128)(2,1)S(1)} collective-permute-done((bf16[512,384]{1,0:T(8,128)(2,1)S(1)}, bf16[512,384]{1,0:T(8,128)(2,1)S(1)}, u32[]{:S(2)}, u32[]{:S(2)}) %collective-permute-start.19) | collective-permute-done | bytes 393248 | tf_op jit(solution)/shard_map/ppermute | solution.py:609
  165.4 5.3 %collective-permute-done.17 = bf16[512,384]{1,0:T(8,128)(2,1)S(1)} collective-permute-done((bf16[512,384]{1,0:T(8,128)(2,1)S(1)}, bf16[512,384]{1,0:T(8,128)(2,1)S(1)}, u32[]{:S(2)}, u32[]{:S(2)}) %collective-permute-start.17) | collective-permute-done | bytes 393248 | tf_op jit(solution)/shard_map/ppermute | solution.py:609
  170.9 1.4 collective-permute-start.36
  172.4 1.1 convert_add_fusion
  173.4 1.0 add_convert_fusion.11
  174.4 4.2 %collective-permute-done.29 = f32[3264]{0:T(1024)S(1)} collective-permute-done((f32[3264]{0:T(1024)S(1)}, f32[3264]{0:T(1024)S(1)}, u32[]{:S(2)}, u32[]{:S(2)}) %collective-permute-start.29) | collective-permute-done | bytes 13088 | tf_op jit(solution)/shard_map/ppermute | solution.py:474
  178.7 1.3 collective-permute-start.33
  180.1 1.3 collective-permute-start.34
  181.4 3.7 %collective-permute-start.35 = (f32[3264]{0:T(1024)S(1)}, f32[3264]{0:T(1024)S(1)}, u32[]{:S(2)}, u32[]{:S(2)}) collective-permute-start(f32[3264]{0:T(1024)S(1)} %add.140), channel_id=1, source_target_pairs={{0,16},{8,24},{16,0},{24,8},{1,17},{9,25},{17,1},{25,9},{2,18},{10... | collective-permute-start | bytes 39176 | tf_op jit(solution)/shard_map/ppermute | solution.py:474
  185.2 1.8 collective-permute-done.35
  188.8 13.5 %collective-permute-done.34 = bf16[256,384]{1,0:T(8,128)(2,1)S(1)} collective-permute-done((bf16[256,384]{1,0:T(8,128)(2,1)S(1)}, bf16[256,384]{1,0:T(8,128)(2,1)S(1)}, u32[]{:S(2)}, u32[]{:S(2)}) %collective-permute-start.34) | collective-permute-done | bytes 196640 | tf_op jit(solution)/shard_map/ppermute | solution.py:463
  203.0 1.1 maximum_convert_fusion.1
  204.1 1.1 maximum_convert_fusion
  (180 shorter events, 27.7 us)
Async XLA Ops:
  0.6 8.5 %copy-start.2 = (bf16[768,384]{1,0:T(8,128)(2,1)S(1)}, bf16[768,384]{1,0:T(8,128)(2,1)}, u32[]{:S(2)}) copy-start(bf16[768,384]{1,0:T(8,128)(2,1)} %wo_o.3) | copy-start | bytes 1769476
  3.5 11.8 %collective-permute-start.1 = (f32[4,384]{1,0:T(4,128)S(1)}, f32[4,384]{1,0:T(4,128)S(1)}, u32[]{:S(2)}, u32[]{:S(2)}) collective-permute-start(f32[4,384]{1,0:T(4,128)S(1)} %pad_maximum_fusion.8), channel_id=1, source_target_pairs={{0,4},{4,0},{1,5},{5,1},{2,6},{6,2},{3,7},{7,3},{8,12},{12,8},{9,1... | collective-permute-start | bytes 18440 | tf_op jit(solution)/shard_map/ppermute | solution.py:449
  6.5 11.4 %collective-permute-start = (bf16[512,384]{1,0:T(8,128)(2,1)}, bf16[512,384]{1,0:T(8,128)(2,1)S(1)}, u32[]{:S(2)}, u32[]{:S(2)}) collective-permute-start(bf16[512,384]{1,0:T(8,128)(2,1)} %param.16), channel_id=1, source_target_pairs={{0,2},{1,3},{2,6},{3,7},{4,0},{5,1},{6,4},{7,5},{8,10},{9,11},{10,... | collective-permute-start | bytes 1179656 | tf_op jit(solution)/shard_map/ppermute | solution.py:532
  10.5 24.1 %copy-start.10 = (bf16[512,384]{1,0:T(8,128)(2,1)S(1)}, bf16[512,384]{1,0:T(8,128)(2,1)}, u32[]{:S(2)}) copy-start(bf16[512,384]{1,0:T(8,128)(2,1)} %param.16) | copy-start | bytes 1179652
  14.7 60.6 %copy-start.20 = (s32[1024]{0:T(1024)}, s32[1024]{0:T(1024)S(1)}, u32[]{:S(2)}) copy-start(s32[1024]{0:T(1024)S(1)} %dynamic_slice.7) | copy-start | bytes 12292
  14.7 12.2 %collective-permute-start.4 = (bf16[512,384]{1,0:T(8,128)(2,1)S(1)}, bf16[512,384]{1,0:T(8,128)(2,1)}, u32[]{:S(2)}, u32[]{:S(2)}) collective-permute-start(bf16[512,384]{1,0:T(8,128)(2,1)S(1)} %copy-done.3), channel_id=1, source_target_pairs={{0,2},{1,3},{2,6},{3,7},{4,0},{5,1},{6,4},{7,5},{8,10},{9,11},{10,... | collective-permute-start | bytes 1179656 | tf_op jit(solution)/shard_map/ppermute | solution.py:537
  17.9 12.8 %copy-start.18 = (bf16[512,384]{1,0:T(8,128)(2,1)}, bf16[512,384]{1,0:T(8,128)(2,1)S(1)}, u32[]{:S(2)}) copy-start(bf16[512,384]{1,0:T(8,128)(2,1)S(1)} %collective-permute-done) | copy-start | bytes 1179652
  17.9 16.7 %collective-permute-start.2 = (bf16[512,384]{1,0:T(8,128)(2,1)S(1)}, bf16[512,384]{1,0:T(8,128)(2,1)S(1)}, u32[]{:S(2)}, u32[]{:S(2)}) collective-permute-start(bf16[512,384]{1,0:T(8,128)(2,1)S(1)} %collective-permute-done), channel_id=1, source_target_pairs={{0,2},{1,3},{6,4},{7,5},{8,10},{9,11},{14,12},{15,13},{16,18},{17,... | collective-permute-start | bytes 1179656 | tf_op jit(solution)/shard_map/ppermute | solution.py:539
  22.2 19.5 %collective-permute-start.6 = (bf16[768,384]{1,0:T(8,128)(2,1)}, bf16[768,384]{1,0:T(8,128)(2,1)S(1)}, u32[]{:S(2)}, u32[]{:S(2)}) collective-permute-start(bf16[768,384]{1,0:T(8,128)(2,1)} %get-tuple-element.112), channel_id=1, source_target_pairs={{0,4},{4,0},{1,5},{5,1},{2,6},{6,2},{3,7},{7,3},{8,12},{12,8},{9,1... | collective-permute-start | bytes 1769480 | tf_op jit(solution)/shard_map/ppermute | solution.py:449
  26.8 14.8 %collective-permute-start.5 = (bf16[512,384]{1,0:T(8,128)(2,1)}, bf16[512,384]{1,0:T(8,128)(2,1)S(1)}, u32[]{:S(2)}, u32[]{:S(2)}) collective-permute-start(bf16[512,384]{1,0:T(8,128)(2,1)} %collective-permute-done.4), channel_id=1, source_target_pairs={{0,2},{1,3},{6,4},{7,5},{8,10},{9,11},{14,12},{15,13},{16,18},{17,... | collective-permute-start | bytes 1179656 | tf_op jit(solution)/shard_map/ppermute | solution.py:541
  35.8 9.7 %collective-permute-start.3 = (bf16[512,768]{1,0:T(8,128)(2,1)S(1)}, bf16[512,768]{1,0:T(8,128)(2,1)}, u32[]{:S(2)}, u32[]{:S(2)}) collective-permute-start(bf16[512,768]{1,0:T(8,128)(2,1)S(1)} %pad_maximum_fusion.xm_ref), channel_id=1, source_target_pairs={{0,1},{1,0},{2,3},{3,2},{4,5},{5,4},{6,7},{7,6},{8,9},{9,8},{10,11... | collective-permute-start | bytes 2359304 | tf_op jit(solution)/shard_map/ppermute | solution.py:543
  43.1 3.8 %collective-permute-start.7 = (bf16[512,768]{1,0:T(8,128)(2,1)S(1)}, bf16[512,768]{1,0:T(8,128)(2,1)}, u32[]{:S(2)}, u32[]{:S(2)}) collective-permute-start(bf16[512,768]{1,0:T(8,128)(2,1)S(1)} %pad_maximum_fusion.1.gm_ref), channel_id=1, source_target_pairs={{0,1},{1,0},{2,3},{3,2},{4,5},{5,4},{6,7},{7,6},{8,9},{9,8},{10,11... | collective-permute-start | bytes 2359304 | tf_op jit(solution)/shard_map/ppermute | solution.py:546
  44.2 16.8 %collective-permute-start.8 = (bf16[768,384]{1,0:T(8,128)(2,1)}, bf16[768,384]{1,0:T(8,128)(2,1)S(1)}, u32[]{:S(2)}, u32[]{:S(2)}) collective-permute-start(bf16[768,384]{1,0:T(8,128)(2,1)} %get-tuple-element.125), channel_id=1, source_target_pairs={{0,4},{4,0},{1,5},{5,1},{2,6},{6,2},{3,7},{7,3},{8,12},{12,8},{9,1... | collective-permute-start | bytes 1769480 | tf_op jit(solution)/shard_map/ppermute | solution.py:449
  45.5 28.9 %collective-permute-start.9 = (bf16[768,384]{1,0:T(8,128)(2,1)}, bf16[768,384]{1,0:T(8,128)(2,1)S(1)}, u32[]{:S(2)}, u32[]{:S(2)}) collective-permute-start(bf16[768,384]{1,0:T(8,128)(2,1)} %pad_maximum_fusion.4), channel_id=1, source_target_pairs={{0,4},{4,0},{1,5},{5,1},{2,6},{6,2},{3,7},{7,3},{8,12},{12,8},{9,1... | collective-permute-start | bytes 1769480 | tf_op jit(solution)/shard_map/ppermute | solution.py:449
  59.8 36.5 %collective-permute-start.10 = (bf16[768,384]{1,0:T(8,128)(2,1)}, bf16[768,384]{1,0:T(8,128)(2,1)}, u32[]{:S(2)}, u32[]{:S(2)}) collective-permute-start(bf16[768,384]{1,0:T(8,128)(2,1)} %get-tuple-element.139), channel_id=1, source_target_pairs={{0,4},{4,0},{1,5},{5,1},{2,6},{6,2},{3,7},{7,3},{8,12},{12,8},{9,1... | collective-permute-start | bytes 1769480 | tf_op jit(solution)/shard_map/ppermute | solution.py:449
  61.9 14.4 %copy-start.23 = (f32[576]{0:T(1024)S(1)}, f32[576]{0:T(1024)}, u32[]{:S(2)}) copy-start(f32[576]{0:T(1024)} %param.18) | copy-start | bytes 6916
  74.4 38.9 %collective-permute-start.11 = (bf16[768,384]{1,0:T(8,128)(2,1)}, bf16[768,384]{1,0:T(8,128)(2,1)S(1)}, u32[]{:S(2)}, u32[]{:S(2)}) collective-permute-start(bf16[768,384]{1,0:T(8,128)(2,1)} %get-tuple-element.146), channel_id=1, source_target_pairs={{0,4},{4,0},{1,5},{5,1},{2,6},{6,2},{3,7},{7,3},{8,12},{12,8},{9,1... | collective-permute-start | bytes 1769480 | tf_op jit(solution)/shard_map/ppermute | solution.py:449
  78.4 17.9 %copy-start.16 = (bf16[768,384]{1,0:T(8,128)(2,1)S(1)}, bf16[768,384]{1,0:T(8,128)(2,1)}, u32[]{:S(2)}) copy-start(bf16[768,384]{1,0:T(8,128)(2,1)} %get-tuple-element.157) | copy-start | bytes 1769476
  97.5 15.7 %copy-start.26 = (f32[2,1,192]{2,1,0:T(1,128)S(1)}, f32[2,1,192]{2,1,0:T(1,128)}, u32[]{:S(2)}) copy-start(f32[2,1,192]{2,1,0:T(1,128)} %get-tuple-element.169) | copy-start | bytes 4612
  97.6 30.4 %collective-permute-start.12 = (bf16[768,384]{1,0:T(8,128)(2,1)S(1)}, bf16[768,384]{1,0:T(8,128)(2,1)S(1)}, u32[]{:S(2)}, u32[]{:S(2)}) collective-permute-start(bf16[768,384]{1,0:T(8,128)(2,1)S(1)} %add_convert_fusion.7), channel_id=1, source_target_pairs={{0,8},{24,16},{1,9},{25,17},{2,10},{26,18},{3,11},{27,19},{4,12},{... | collective-permute-start | bytes 1769480 | tf_op jit(solution)/shard_map/ppermute | solution.py:453
  112.0 16.0 %collective-permute-start.13 = (bf16[2,256,384]{2,1,0:T(8,128)(2,1)}, bf16[2,256,384]{2,1,0:T(8,128)(2,1)S(1)}, u32[]{:S(2)}, u32[]{:S(2)}) collective-permute-start(bf16[2,256,384]{2,1,0:T(8,128)(2,1)} %get-tuple-element.159), channel_id=1, source_target_pairs={{0,4},{4,0},{1,5},{5,1},{2,6},{6,2},{3,7},{7,3},{8,12},{12,8},{9,1... | collective-permute-start | bytes 1179656 | tf_op jit(solution)/shard_map/ppermute | solution.py:449
  114.2 9.3 %copy-start.29 = (f32[1,1,192]{2,1,0:T(1,128)S(1)}, f32[1,1,192]{2,1,0:T(1,128)}, u32[]{:S(2)}) copy-start(f32[1,1,192]{2,1,0:T(1,128)} %get-tuple-element.170) | copy-start | bytes 2308
  114.2 10.2 %copy-start.14 = (bf16[768,384]{1,0:T(8,128)(2,1)S(1)}, bf16[768,384]{1,0:T(8,128)(2,1)}, u32[]{:S(2)}) copy-start(bf16[768,384]{1,0:T(8,128)(2,1)} %get-tuple-element.172) | copy-start | bytes 1769476
  123.5 4.3 %collective-permute-start.21 = (f32[2880]{0:T(1024)S(1)}, f32[2880]{0:T(1024)S(1)}, u32[]{:S(2)}, u32[]{:S(2)}) collective-permute-start(f32[2880]{0:T(1024)S(1)} %get-tuple-element.240), channel_id=1, source_target_pairs={{0,4},{4,0},{1,5},{5,1},{2,6},{6,2},{3,7},{7,3},{8,12},{12,8},{9,1... | collective-permute-start | bytes 34568 | tf_op jit(solution)/shard_map/ppermute | solution.py:449
  125.6 12.5 %collective-permute-start.24 = (bf16[768,384]{1,0:T(8,128)(2,1)S(1)}, bf16[768,384]{1,0:T(8,128)(2,1)}, u32[]{:S(2)}, u32[]{:S(2)}) collective-permute-start(bf16[768,384]{1,0:T(8,128)(2,1)S(1)} %add_convert_fusion.6), channel_id=1, source_target_pairs={{0,8},{24,16},{1,9},{25,17},{2,10},{26,18},{3,11},{27,19},{4,12},{... | collective-permute-start | bytes 1769480 | tf_op jit(solution)/shard_map/ppermute | solution.py:453
  127.9 1.2 collective-permute-start.22
  128.1 14.4 %collective-permute-start.25 = (bf16[768,384]{1,0:T(8,128)(2,1)S(1)}, bf16[768,384]{1,0:T(8,128)(2,1)S(1)}, u32[]{:S(2)}, u32[]{:S(2)}) collective-permute-start(bf16[768,384]{1,0:T(8,128)(2,1)S(1)} %add_convert_fusion.5), channel_id=1, source_target_pairs={{8,16},{16,8},{9,17},{17,9},{10,18},{18,10},{11,19},{19,11},{12,20... | collective-permute-start | bytes 1769480 | tf_op jit(solution)/shard_map/ppermute | solution.py:458
  129.1 3.8 %collective-permute-start.23 = (f32[1920]{0:T(1024)S(1)}, f32[1920]{0:T(1024)S(1)}, u32[]{:S(2)}, u32[]{:S(2)}) collective-permute-start(f32[1920]{0:T(1024)S(1)} %fusion.17), channel_id=1, source_target_pairs={{0,2},{1,3},{2,0},{3,1},{4,6},{5,7},{6,4},{7,5},{8,10},{9,11},{10,... | collective-permute-start | bytes 23048 | tf_op jit(solution)/shard_map/ppermute | solution.py:474
  131.3 13.5 %collective-permute-start.16 = (bf16[1,256,384]{2,1,0:T(8,128)(2,1)S(1)}, bf16[1,256,384]{2,1,0:T(8,128)(2,1)S(1)}, u32[]{:S(2)}, u32[]{:S(2)}) collective-permute-start(bf16[1,256,384]{2,1,0:T(8,128)(2,1)S(1)} %copy-done.30), channel_id=1, source_target_pairs={{0,4},{4,0},{1,5},{5,1},{2,6},{6,2},{3,7},{7,3},{8,12},{12,8},{9,1... | collective-permute-start | bytes 589832 | tf_op jit(solution)/shard_map/ppermute | solution.py:449
  132.9 11.9 %collective-permute-start.14 = (bf16[512,768]{1,0:T(8,128)(2,1)}, bf16[512,768]{1,0:T(8,128)(2,1)S(1)}, u32[]{:S(2)}, u32[]{:S(2)}) collective-permute-start(bf16[512,768]{1,0:T(8,128)(2,1)} %get-tuple-element.160), channel_id=1, source_target_pairs={{0,1},{1,0},{2,3},{3,2},{4,5},{5,4},{6,7},{7,6},{8,9},{9,8},{10,11... | collective-permute-start | bytes 2359304 | tf_op jit(solution)/shard_map/ppermute | solution.py:592
  133.0 11.8 %collective-permute-start.15 = (bf16[512,768]{1,0:T(8,128)(2,1)}, bf16[512,768]{1,0:T(8,128)(2,1)S(1)}, u32[]{:S(2)}, u32[]{:S(2)}) collective-permute-start(bf16[512,768]{1,0:T(8,128)(2,1)} %get-tuple-element.161), channel_id=1, source_target_pairs={{0,1},{1,0},{2,3},{3,2},{4,5},{5,4},{6,7},{7,6},{8,9},{9,8},{10,11... | collective-permute-start | bytes 2359304 | tf_op jit(solution)/shard_map/ppermute | solution.py:593
  138.1 15.9 %collective-permute-start.27 = (bf16[512,384]{1,0:T(8,128)(2,1)S(1)}, bf16[512,384]{1,0:T(8,128)(2,1)S(1)}, u32[]{:S(2)}, u32[]{:S(2)}) collective-permute-start(bf16[512,384]{1,0:T(8,128)(2,1)S(1)} %bitcast.14), channel_id=1, source_target_pairs={{0,8},{24,16},{1,9},{25,17},{2,10},{26,18},{3,11},{27,19},{4,12},{... | collective-permute-start | bytes 1179656 | tf_op jit(solution)/shard_map/ppermute | solution.py:453
  143.8 7.8 %copy-start.13 = (bf16[512,768]{1,0:T(8,128)(2,1)S(1)}, bf16[512,768]{1,0:T(8,128)(2,1)}, u32[]{:S(2)}) copy-start(bf16[512,768]{1,0:T(8,128)(2,1)} %get-tuple-element.164) | copy-start | bytes 2359300
  143.8 14.8 %collective-permute-start.26 = (bf16[768,384]{1,0:T(8,128)(2,1)S(1)}, bf16[768,384]{1,0:T(8,128)(2,1)S(1)}, u32[]{:S(2)}, u32[]{:S(2)}) collective-permute-start(bf16[768,384]{1,0:T(8,128)(2,1)S(1)} %add_convert_fusion.4), channel_id=1, source_target_pairs={{8,16},{16,8},{9,17},{17,9},{10,18},{18,10},{11,19},{19,11},{12,20... | collective-permute-start | bytes 1769480 | tf_op jit(solution)/shard_map/ppermute | solution.py:458
  144.9 12.8 %collective-permute-start.28 = (bf16[256,384]{1,0:T(8,128)(2,1)S(1)}, bf16[256,384]{1,0:T(8,128)(2,1)S(1)}, u32[]{:S(2)}, u32[]{:S(2)}) collective-permute-start(bf16[256,384]{1,0:T(8,128)(2,1)S(1)} %fusion.3), channel_id=1, source_target_pairs={{0,8},{24,16},{1,9},{25,17},{2,10},{26,18},{3,11},{27,19},{4,12},{... | collective-permute-start | bytes 589832 | tf_op jit(solution)/shard_map/ppermute | solution.py:453
  151.9 12.1 %collective-permute-start.19 = (bf16[512,384]{1,0:T(8,128)(2,1)S(1)}, bf16[512,384]{1,0:T(8,128)(2,1)S(1)}, u32[]{:S(2)}, u32[]{:S(2)}) collective-permute-start(bf16[512,384]{1,0:T(8,128)(2,1)S(1)} %get-tuple-element.207), channel_id=1, source_target_pairs={{0,4},{1,5},{2,0},{3,1},{4,6},{5,7},{6,2},{7,3},{8,12},{9,13},{10,... | collective-permute-start | bytes 1179656 | tf_op jit(solution)/shard_map/ppermute | solution.py:609
  153.0 11.7 %collective-permute-start.20 = (bf16[512,384]{1,0:T(8,128)(2,1)S(1)}, bf16[512,384]{1,0:T(8,128)(2,1)S(1)}, u32[]{:S(2)}, u32[]{:S(2)}) collective-permute-start(bf16[512,384]{1,0:T(8,128)(2,1)S(1)} %get-tuple-element.208), channel_id=1, source_target_pairs={{2,4},{3,5},{4,2},{5,3},{10,12},{11,13},{12,10},{13,11},{18,20},{1... | collective-permute-start | bytes 1179656 | tf_op jit(solution)/shard_map/ppermute | solution.py:612
  154.0 16.7 %collective-permute-start.17 = (bf16[512,384]{1,0:T(8,128)(2,1)S(1)}, bf16[512,384]{1,0:T(8,128)(2,1)S(1)}, u32[]{:S(2)}, u32[]{:S(2)}) collective-permute-start(bf16[512,384]{1,0:T(8,128)(2,1)S(1)} %get-tuple-element.210), channel_id=1, source_target_pairs={{0,4},{1,5},{2,0},{3,1},{4,6},{5,7},{6,2},{7,3},{8,12},{9,13},{10,... | collective-permute-start | bytes 1179656 | tf_op jit(solution)/shard_map/ppermute | solution.py:609
  157.7 13.0 %collective-permute-start.18 = (bf16[512,384]{1,0:T(8,128)(2,1)S(1)}, bf16[512,384]{1,0:T(8,128)(2,1)S(1)}, u32[]{:S(2)}, u32[]{:S(2)}) collective-permute-start(bf16[512,384]{1,0:T(8,128)(2,1)S(1)} %get-tuple-element.211), channel_id=1, source_target_pairs={{2,4},{3,5},{4,2},{5,3},{10,12},{11,13},{12,10},{13,11},{18,20},{1... | collective-permute-start | bytes 1179656 | tf_op jit(solution)/shard_map/ppermute | solution.py:612
  158.6 20.0 %collective-permute-start.32 = (bf16[768,384]{1,0:T(8,128)(2,1)S(1)}, bf16[768,384]{1,0:T(8,128)(2,1)S(1)}, u32[]{:S(2)}, u32[]{:S(2)}) collective-permute-start(bf16[768,384]{1,0:T(8,128)(2,1)S(1)} %add_convert_fusion.3), channel_id=1, source_target_pairs={{8,0},{16,24},{9,1},{17,25},{10,2},{18,26},{11,3},{19,27},{12,4},{... | collective-permute-start | bytes 1769480 | tf_op jit(solution)/shard_map/ppermute | solution.py:463
  164.0 14.6 %collective-permute-start.31 = (bf16[256,384]{1,0:T(8,128)(2,1)S(1)}, bf16[256,384]{1,0:T(8,128)(2,1)S(1)}, u32[]{:S(2)}, u32[]{:S(2)}) collective-permute-start(bf16[256,384]{1,0:T(8,128)(2,1)S(1)} %add_convert_fusion.13), channel_id=1, source_target_pairs={{8,16},{16,8},{9,17},{17,9},{10,18},{18,10},{11,19},{19,11},{12,20... | collective-permute-start | bytes 589832 | tf_op jit(solution)/shard_map/ppermute | solution.py:458
  164.7 13.9 %collective-permute-start.30 = (bf16[512,384]{1,0:T(8,128)(2,1)S(1)}, bf16[512,384]{1,0:T(8,128)(2,1)S(1)}, u32[]{:S(2)}, u32[]{:S(2)}) collective-permute-start(bf16[512,384]{1,0:T(8,128)(2,1)S(1)} %add_convert_fusion.9), channel_id=1, source_target_pairs={{8,16},{16,8},{9,17},{17,9},{10,18},{18,10},{11,19},{19,11},{12,20... | collective-permute-start | bytes 1179656 | tf_op jit(solution)/shard_map/ppermute | solution.py:458
  170.7 7.9 %collective-permute-start.29 = (f32[3264]{0:T(1024)S(1)}, f32[3264]{0:T(1024)S(1)}, u32[]{:S(2)}, u32[]{:S(2)}) collective-permute-start(f32[3264]{0:T(1024)S(1)} %pad_maximum_fusion.6), channel_id=1, source_target_pairs={{0,8},{8,0},{16,24},{24,16},{1,9},{9,1},{17,25},{25,17},{2,10},{10... | collective-permute-start | bytes 39176 | tf_op jit(solution)/shard_map/ppermute | solution.py:474
  170.9 31.4 %collective-permute-start.36 = (bf16[768,384]{1,0:T(8,128)(2,1)S(1)}, bf16[768,384]{1,0:T(8,128)(2,1)S(1)}, u32[]{:S(2)}, u32[]{:S(2)}) collective-permute-start(bf16[768,384]{1,0:T(8,128)(2,1)S(1)} %add_convert_fusion.2), channel_id=1, source_target_pairs={{8,0},{16,24},{9,1},{17,25},{10,2},{18,26},{11,3},{19,27},{12,4},{... | collective-permute-start | bytes 1769480 | tf_op jit(solution)/shard_map/ppermute | solution.py:463
  178.7 26.5 %collective-permute-start.33 = (bf16[512,384]{1,0:T(8,128)(2,1)S(1)}, bf16[512,384]{1,0:T(8,128)(2,1)S(1)}, u32[]{:S(2)}, u32[]{:S(2)}) collective-permute-start(bf16[512,384]{1,0:T(8,128)(2,1)S(1)} %add_convert_fusion.8), channel_id=1, source_target_pairs={{8,0},{16,24},{9,1},{17,25},{10,2},{18,26},{11,3},{19,27},{12,4},{... | collective-permute-start | bytes 1179656 | tf_op jit(solution)/shard_map/ppermute | solution.py:463
  180.1 22.2 %collective-permute-start.34 = (bf16[256,384]{1,0:T(8,128)(2,1)S(1)}, bf16[256,384]{1,0:T(8,128)(2,1)S(1)}, u32[]{:S(2)}, u32[]{:S(2)}) collective-permute-start(bf16[256,384]{1,0:T(8,128)(2,1)S(1)} %add_convert_fusion.12), channel_id=1, source_target_pairs={{8,0},{16,24},{9,1},{17,25},{10,2},{18,26},{11,3},{19,27},{12,4},{... | collective-permute-start | bytes 589832 | tf_op jit(solution)/shard_map/ppermute | solution.py:463
  181.4 5.6 %collective-permute-start.35 = (f32[3264]{0:T(1024)S(1)}, f32[3264]{0:T(1024)S(1)}, u32[]{:S(2)}, u32[]{:S(2)}) collective-permute-start(f32[3264]{0:T(1024)S(1)} %add.140), channel_id=1, source_target_pairs={{0,16},{8,24},{16,0},{24,8},{1,17},{9,25},{17,1},{25,9},{2,18},{10... | collective-permute-start | bytes 39176 | tf_op jit(solution)/shard_map/ppermute | solution.py:474
  188.7 19.1 %copy-start.21 = (f32[384]{0:T(512)}, f32[384]{0:T(512)S(1)}, u32[]{:S(2)}) copy-start(f32[384]{0:T(512)S(1)} %get-tuple-element.269) | copy-start | bytes 4612
  (22 other events, 56.7 us)

commit v3 on v2

--- a/solution.py
+++ b/solution.py
@@ -16,6 +16,7 @@
 F32 = jnp.float32
 BF16 = jnp.bfloat16
 GROUP = ("row", "col")
+EXTRA = 16
 VMEM_BYTES = 60 * 1024 * 1024
 
 
@@ -54,22 +55,20 @@
     cdf = 0.5 * (1.0 + lax.erf(pre * (2.0 ** -0.5)))
     hidden = (pre * cdf).astype(BF16)
     slope = cdf + pre * (jnp.exp(-0.5 * pre * pre) * (1.0 / math.sqrt(2.0 * math.pi)))
-    mix = jnp.concatenate([dot_nn(hidden, wo_o[...]), dot_nn(hidden, wo_p[...])], axis=1)
     grad_hidden = dot_nt(go[:, :half], wo_o[...]) + dot_nt(go[:, half:], wo_p[...])
     grad_pre = (grad_hidden * slope).astype(BF16)
     own_ref[:half, :] += dot_tn(h[:, :half], grad_pre)
     send_acc[:half, :] += dot_tn(h[:, half:], grad_pre)
     own_ref[half:, :] += dot_tn(hidden, go[:, :half])
     send_acc[half:, :] += dot_tn(hidden, go[:, half:])
-    grad_h = jnp.concatenate([dot_nt(grad_pre, wi_o[...]), dot_nt(grad_pre, wi_p[...])], axis=1)
-    return normed, mix, grad_h, jnp.sum(grad_pre.astype(F32), axis=0, keepdims=True)
+    return normed, hidden, grad_pre, jnp.sum(grad_pre.astype(F32), axis=0, keepdims=True)
 
 
 def mlp_first_kernel(
     core_ref, xm_ref, xo_ref, gm_ref, go_ref, wi_o, wo_o, wi_p, wo_p, b_ref, gain_ref, bias_ref,
     again_ref, abias_ref,
-    mix_ref, gh_ref, x_out, go_out, h_out, own_ref, send_ref, gb_ref,
-    own_acc, acc_ref,
+    hid_ref, dp_ref, x_out, go_out, h_out, own_ref, send_ref,
+    own_acc, acc_ref, sums,
 ):
     step = pl.program_id(0)
 
@@ -77,31 +76,39 @@
     def _():
         own_acc[...] = jnp.zeros_like(own_acc)
         acc_ref[...] = jnp.zeros_like(acc_ref)
-        gb_ref[...] = jnp.zeros_like(gb_ref)
+        sums[...] = jnp.zeros_like(sums)
 
     held = step // (pl.num_programs(0) // 2) == core_ref[0]
     x_rows = jnp.where(held, xm_ref[...], xo_ref[...])
     go = jnp.where(held, gm_ref[...], go_ref[...])
     x_out[...] = x_rows
     go_out[...] = go
-    normed, mix, grad_h, gb = mlp_part(
+    normed, hidden, grad_pre, gb = mlp_part(
         x_rows, go, wi_o, wi_p, wo_o, wo_p, b_ref, gain_ref, bias_ref, own_acc, acc_ref
     )
     h_out[...] = (normed * again_ref[...] + abias_ref[...]).astype(BF16)
-    mix_ref[...] = mix
-    gh_ref[...] = grad_h
-    gb_ref[0:1, :] += gb
+    hid_ref[...] = hidden
+    dp_ref[...] = grad_pre
+    sums[0:1, :] += gb
+    sums[EXTRA : EXTRA + 1, :] += gb
+    total = jnp.sum(go.astype(F32), axis=0, keepdims=True)
+    half = wi_o.shape[0]
+    sums[1:2, :] += total[:, :half]
+    sums[EXTRA + 1 : EXTRA + 2, :] += total[:, half:]
 
     @pl.when(step == pl.num_programs(0) - 1)
     def _():
-        own_ref[...] = own_acc[...].astype(BF16)
-        send_ref[...] = acc_ref[...].astype(BF16)
+        deep = own_acc.shape[0]
+        own_ref[:deep, :] = own_acc[...].astype(BF16)
+        send_ref[:deep, :] = acc_ref[...].astype(BF16)
+        own_ref[deep:, :] = sums[:EXTRA, :].astype(BF16)
+        send_ref[deep:, :] = sums[EXTRA:, :].astype(BF16)
 
 
 def mlp_second_kernel(
-    x_ref, go_ref, mix_in, gh_in, wi_o, wo_o, wi_p, wo_p, b_ref, gain_ref, bias_ref,
-    mix_ref, gh_ref, own_ref, send_ref, gb_ref,
-    own_acc, acc_ref,
+    x_ref, go_ref, wi_o, wo_o, wi_p, wo_p, b_ref, gain_ref, bias_ref,
+    hid_ref, dp_ref, own_ref, send_ref,
+    own_acc, acc_ref, sums,
 ):
     step = pl.program_id(0)
 
@@ -109,19 +116,23 @@
     def _():
         own_acc[...] = jnp.zeros_like(own_acc)
         acc_ref[...] = jnp.zeros_like(acc_ref)
-        gb_ref[...] = jnp.zeros_like(gb_ref)
-
-    _, mix, grad_h, gb = mlp_part(
+        sums[...] = jnp.zeros_like(sums)
+
+    _, hidden, grad_pre, gb = mlp_part(
         x_ref[...], go_ref[...], wi_o, wi_p, wo_o, wo_p, b_ref, gain_ref, bias_ref, own_acc, acc_ref
     )
-    mix_ref[...] = mix_in[...] + mix
-    gh_ref[...] = gh_in[...] + grad_h
-    gb_ref[0:1, :] += gb
+    hid_ref[...] = hidden
+    dp_ref[...] = grad_pre
+    sums[0:1, :] += gb
+    sums[EXTRA : EXTRA + 1, :] += gb
 
     @pl.when(step == pl.num_programs(0) - 1)
     def _():
-        own_ref[...] = own_acc[...].astype(BF16)
-        send_ref[...] = acc_ref[...].astype(BF16)
+        deep = own_acc.shape[0]
+        own_ref[:deep, :] = own_acc[...].astype(BF16)
+        send_ref[:deep, :] = acc_ref[...].astype(BF16)
+        own_ref[deep:, :] = sums[:EXTRA, :].astype(BF16)
+        send_ref[deep:, :] = sums[EXTRA:, :].astype(BF16)
 
 
 def brief():
@@ -161,15 +172,15 @@
     mine_spec = pl.BlockSpec((BLOCK, width), held_map)
     other_spec = pl.BlockSpec((BLOCK, width), other_map)
     row_spec = pl.BlockSpec((BLOCK, width), lambda i, core_ref: (i, 0))
+    half_spec = pl.BlockSpec((BLOCK, half), lambda i, core_ref: (i, 0))
     outs = [
-        shape((rows, width), F32),
-        shape((rows, width), F32),
+        shape((rows, half), BF16),
+        shape((rows, half), BF16),
         shape((rows, width), BF16),
         shape((rows, width), BF16),
         shape((rows, width), BF16),
-        shape((2 * half, half), BF16),
-        shape((2 * half, half), BF16),
-        shape((8, half), F32),
+        shape((2 * half + EXTRA, half), BF16),
+        shape((2 * half + EXTRA, half), BF16),
     ]
     return pl.pallas_call(
         mlp_first_kernel,
@@ -181,8 +192,9 @@
             + [part_spec(half, (0, 0)), part_spec(half, (1, 0))]
             + [pl.BlockSpec((1, half), lambda *i: (0, 0))]
             + [whole(a) for a in norms],
-            out_specs=[row_spec] * 5 + [whole(a) for a in outs[5:]],
-            scratch_shapes=[pltpu.VMEM((2 * half, half), F32)] * 2,
+            out_specs=[half_spec] * 2 + [row_spec] * 3 + [whole(a) for a in outs[5:]],
+            scratch_shapes=[pltpu.VMEM((2 * half, half), F32)] * 2
+            + [pltpu.VMEM((2 * EXTRA, half), F32)],
         ),
         out_shape=outs,
         compiler_params=mlp_params(),
@@ -191,38 +203,39 @@
     )(core, x_mine, x_other, go_mine, go_other, w_in, w_out, pack, pack, b_in, *norms)
 
 
-def mlp_second(x_seq, go_seq, mix, gh, w_in, w_out, pack, b_in, *norms):
+def mlp_second(x_seq, go_seq, w_in, w_out, pack, b_in, *norms):
     rows, width = x_seq.shape
     half = width // 2
     row_spec = pl.BlockSpec((BLOCK, width), lambda i: (i, 0))
+    half_spec = pl.BlockSpec((BLOCK, half), lambda i: (i, 0))
     outs = [
-        shape((rows, width), F32),
-        shape((rows, width), F32),
-        shape((2 * half, half), BF16),
-        shape((2 * half, half), BF16),
-        shape((8, half), F32),
+        shape((rows, half), BF16),
+        shape((rows, half), BF16),
+        shape((2 * half + EXTRA, half), BF16),
+        shape((2 * half + EXTRA, half), BF16),
     ]
     return pl.pallas_call(
         mlp_second_kernel,
         grid=(rows // BLOCK,),
-        in_specs=[row_spec] * 4
+        in_specs=[row_spec] * 2
         + [part_spec(half, (0, 1)), part_spec(half, (1, 0))]
         + [part_spec(half, (0, 0)), part_spec(half, (1, 0))]
         + [pl.BlockSpec((1, half), lambda *i: (0, 1))]
         + [whole(a) for a in norms],
-        out_specs=[row_spec] * 2 + [whole(a) for a in outs[2:]],
+        out_specs=[half_spec] * 2 + [whole(a) for a in outs[2:]],
         out_shape=outs,
-        scratch_shapes=[pltpu.VMEM((2 * half, half), F32)] * 2,
+        scratch_shapes=[pltpu.VMEM((2 * half, half), F32)] * 2
+            + [pltpu.VMEM((2 * EXTRA, half), F32)],
         compiler_params=mlp_params(),
         cost_estimate=brief(),
         name="mlp_second",
-    )(x_seq, go_seq, mix, gh, w_in, w_out, pack, pack, b_in, *norms)
+    )(x_seq, go_seq, w_in, w_out, pack, pack, b_in, *norms)
 
 
 def attn_kernel(
     h_ref, go_ref, wo_ref, wp_ref, b_ref, do_ref, dp_ref, cos_ref, s1_ref, s2_ref,
     segc_ref, segr_ref,
-    ctx_out, dj_out, own_ref, send_ref, gb_ref,
+    ctx_out, dj_out, own_ref, send_ref,
     qk_ref, v_ref, dctx_ref, ctxt_ref, dqt_ref, dk_ref, dv_ref,
 ):
     rows = h_ref.shape[0]
@@ -288,18 +301,23 @@
     )
     dj = jnp.concatenate([turned_back.astype(BF16), dv_ref[...].astype(BF16)], axis=1)
     dj_out[0] = dj
-    gb_ref[0] = jnp.sum(dj.astype(F32), axis=0, keepdims=True)
-    own_ref[0, :inner, :] = dot_tn(dj, h_ref[:, :half]).astype(BF16)
-    own_ref[0, inner:, :] = dot_nn(ctxt_ref[...], go_ref[:, :half]).astype(BF16)
-    send_ref[0, :inner, :] = dot_tn(dj, h_ref[:, half:]).astype(BF16)
-    send_ref[0, inner:, :] = dot_nn(ctxt_ref[...], go_ref[:, half:]).astype(BF16)
+    gb = jnp.sum(dj.astype(F32), axis=0, keepdims=True)
+    gb = jnp.concatenate([gb, jnp.zeros((1, half - inner), F32)], axis=1)
+    gb = jnp.concatenate([gb, jnp.zeros((EXTRA - 1, half), F32)], axis=0).astype(BF16)
+    deep = inner + HEAD_DIM
+    for out, at in ((own_ref, slice(0, half)), (send_ref, slice(half, 2 * half))):
+        out[0, :inner, :] = dot_tn(dj, h_ref[:, at]).astype(BF16)
+        out[0, inner:deep, :] = dot_nn(ctxt_ref[...], go_ref[:, at]).astype(BF16)
+        out[0, deep:, :] = gb
 
 
 def attn_head(first, count, h_seq, go_seq, wq_o, wq_p, b_heads, wd_o, wd_p, *tables):
     rows = h_seq.shape[0]
     half = wq_o.shape[1]
     inner = 3 * HEAD_DIM
-    skip = wq_o.shape[0] // HEAD_DIM
+    before = 2 * half
+    deep = (before + wq_o.shape[0]) // HEAD_DIM
+    before = before // inner
 
     def per_head(a, base):
         return pl.BlockSpec((1,) + a.shape[1:], lambda i: (i + base,) + (0,) * (a.ndim - 1))
@@ -307,17 +325,16 @@
     outs = [
         shape((count, HEAD_DIM, rows), BF16),
         shape((count, rows, inner), BF16),
-        shape((count, inner + HEAD_DIM, half), BF16),
-        shape((count, inner + HEAD_DIM, half), BF16),
-        shape((count, 1, inner), F32),
+        shape((count, inner + HEAD_DIM + EXTRA, half), BF16),
+        shape((count, inner + HEAD_DIM + EXTRA, half), BF16),
     ]
     args = (h_seq, go_seq, wq_o, wq_p, b_heads, wd_o, wd_p) + tables
     specs = [whole(a) for a in args]
-    for j in (2, 3):
-        specs[j] = pl.BlockSpec((inner, half), lambda i: (i + first, 0))
+    specs[2] = pl.BlockSpec((inner, half), lambda i: (i + first, 0))
+    specs[3] = pl.BlockSpec((inner, half), lambda i: (i + first + before, 0))
     specs[4] = per_head(b_heads, first)
     specs[5] = pl.BlockSpec((HEAD_DIM, half), lambda i: (i + first, 0))
-    specs[6] = pl.BlockSpec((HEAD_DIM, half), lambda i: (i + first + skip, 0))
+    specs[6] = pl.BlockSpec((HEAD_DIM, half), lambda i: (i + first + deep, 0))
     return pl.pallas_call(
         attn_kernel,
         grid=(count,),
@@ -342,36 +359,53 @@
 
 
 def close_kernel(
-    core_ref, x_ref, mix_ref, gh_ref, c01, c2, j01, j2, wq_o, wq_p, wd_o, wd_p,
-    again_ref, mgain_ref,
-    mix_send, mix_keep, dx_send, dx_keep, vec_ref,
+    core_ref, x_ref, hid_a, hid_b, dp_a, dp_b, c01, c2, j01, j2,
+    wq_o, wd_o, wi_o, wo_o, got_a, got_b, again_ref, mgain_ref,
+    mix_send, mix_keep, dx_send, dx_keep,
+    vec_ref,
 ):
     del core_ref
     step = pl.program_id(0)
     sending = step < pl.num_programs(0) // 2
+    half = wi_o.shape[0]
+    inner = 3 * HEAD_DIM
+    at_q = 2 * half
+    at_d = at_q + wq_o.shape[0]
 
     @pl.when(step == 0)
     def _():
         vec_ref[...] = jnp.zeros_like(vec_ref)
 
     ctxt = jnp.concatenate([c01[0], c01[1], c2[0]], axis=0)
-    mix = mix_ref[...] + jnp.concatenate(
-        [dot_tn(ctxt, wd_o[...]), dot_tn(ctxt, wd_p[...])], axis=1
+    mix = jnp.concatenate(
+        [
+            dot_tn(ctxt, wd_o[...])
+            + dot_nn(hid_a[...], wo_o[:half, :]) + dot_nn(hid_b[...], wo_o[half:, :]),
+            dot_tn(ctxt, got_b[at_d:, :])
+            + dot_nn(hid_a[...], got_a[half:, :]) + dot_nn(hid_b[...], got_b[half:at_q, :]),
+        ],
+        axis=1,
     )
     grad_h = jnp.concatenate(
         [
             sum(
-                dot_nn(j, w[n * 3 * HEAD_DIM : (n + 1) * 3 * HEAD_DIM, :])
+                dot_nn(j, w[at + n * inner : at + (n + 1) * inner, :])
                 for n, j in enumerate((j01[0], j01[1], j2[0]))
             )
-            for w in (wq_o, wq_p)
+            for w, at in ((wq_o, 0), (got_b, at_q))
+        ],
+        axis=1,
+    )
+    grad_m = jnp.concatenate(
+        [
+            dot_nt(dp_a[...], wi_o[:, :half]) + dot_nt(dp_b[...], wi_o[:, half:]),
+            dot_nt(dp_a[...], got_a[:half, :]) + dot_nt(dp_b[...], got_b[:half, :]),
         ],
         axis=1,
     )
     normed, inv_std = normalize(x_ref[...])
     vec_ref[0:1, :] += jnp.sum(grad_h * normed, axis=0, keepdims=True)
     vec_ref[1:2, :] += jnp.sum(grad_h, axis=0, keepdims=True)
-    grad_m = gh_ref[...]
     vec_ref[2:3, :] += jnp.sum(grad_m * normed, axis=0, keepdims=True)
     vec_ref[3:4, :] += jnp.sum(grad_m, axis=0, keepdims=True)
     dx = norm_back(grad_h * again_ref[...] + grad_m * mgain_ref[...], normed, inv_std)
@@ -379,15 +413,21 @@
     @pl.when(sending)
     def _():
         mix_send[...] = mix.astype(BF16)
-        dx_send[...] = dx.astype(BF16)
+        dx_send[pl.ds(step * BLOCK, BLOCK), :] = dx.astype(BF16)
 
     @pl.when(jnp.logical_not(sending))
     def _():
         mix_keep[...] = mix.astype(BF16)
-        dx_keep[...] = dx.astype(BF16)
-
-
-def close_layer(core, x_seq, mix, gh, ctx, djs, *weights):
+        dx_keep[pl.ds((step - pl.num_programs(0) // 2) * BLOCK, BLOCK), :] = dx.astype(BF16)
+
+    @pl.when(step == pl.num_programs(0) - 1)
+    def _():
+        held = dx_send.shape[0] - EXTRA
+        dx_send[held:, :] = vec_ref[...].astype(BF16)
+        dx_keep[held:, :] = vec_ref[...].astype(BF16)
+
+
+def close_layer(core, x_seq, hidden, ctx, djs, *weights):
     rows, width = x_seq.shape
     held = rows // 2
     steps = held // BLOCK
@@ -396,6 +436,7 @@
         return jnp.where(i < steps, (1 - core_ref[0]) * steps + i, (core_ref[0] - 1) * steps + i)
 
     row_spec = pl.BlockSpec((BLOCK, width), lambda i, c: (block_of(i, c), 0))
+    half_spec = pl.BlockSpec((BLOCK, width // 2), lambda i, c: (block_of(i, c), 0))
     send_spec = pl.BlockSpec((BLOCK, width), lambda i, c: (jnp.minimum(i, steps - 1), 0))
     keep_spec = pl.BlockSpec((BLOCK, width), lambda i, c: (jnp.maximum(i - steps, 0), 0))
     ctx_specs = [
@@ -406,25 +447,16 @@
         pl.BlockSpec((a.shape[0], BLOCK, 3 * HEAD_DIM), lambda i, c: (0, block_of(i, c), 0))
         for a in djs
     ]
-    specs = [whole(a) for a in weights]
-    wide, half = weights[0].shape
-    deep = weights[2].shape[0]
-    specs[1] = pl.BlockSpec((wide, half), lambda *i: (0, 0))
-    specs[3] = pl.BlockSpec((deep, half), lambda *i: (wide // deep, 0))
-    outs = [
-        shape((held, width), BF16),
-        shape((held, width), BF16),
-        shape((held, width), BF16),
-        shape((held, width), BF16),
-        shape((8, width), F32),
-    ]
+    outs = [shape((held, width), BF16)] * 2 + [shape((held + EXTRA, width), BF16)] * 2
     return pl.pallas_call(
         close_kernel,
         grid_spec=pltpu.PrefetchScalarGridSpec(
             num_scalar_prefetch=1,
             grid=(rows // BLOCK,),
-            in_specs=[row_spec] * 3 + ctx_specs + dj_specs + specs,
-            out_specs=[send_spec, keep_spec, send_spec, keep_spec, whole(outs[4])],
+            in_specs=[row_spec] + [half_spec] * 4 + ctx_specs + dj_specs
+            + [whole(a) for a in weights],
+            out_specs=[send_spec, keep_spec, whole(outs[2]), whole(outs[3])],
+            scratch_shapes=[pltpu.VMEM((EXTRA, width), F32)],
         ),
         out_shape=outs,
         compiler_params=pltpu.CompilerParams(
@@ -432,7 +464,7 @@
         ),
         cost_estimate=brief(),
         name="close_layer",
-    )(core, x_seq, mix, gh, *ctx, *djs, *weights)
+    )(core, x_seq, *hidden, *ctx, *djs, *weights)
 
 
 def group_perm(n_row, n_col, target):
@@ -504,8 +536,7 @@
     inner = 3 * HEAD_DIM
     wq_t = w_qkv.T
     pack_a = jnp.concatenate([w_in[:, :half], w_out[:half]], axis=0)
-    pack_b = jnp.concatenate([w_in[:, half:], w_out[half:]], axis=0)
-    pack_c = jnp.concatenate([wq_t, w_dense], axis=0)
+    pack_b = jnp.concatenate([w_in[:, half:], w_out[half:], wq_t, w_dense], axis=0)
     norms = jnp.stack([ln_attn_gain, ln_attn_bias, ln_mlp_gain, ln_mlp_bias])
     core_at = core.reshape(1)
 
@@ -527,12 +558,11 @@
         )
 
     d_out_f = d_out.astype(F32)
-    d_sum = jnp.sum(d_out_f, axis=0)
     norms_got = swap_row(norms)
     near_x = lax.ppermute(block_input, GROUP, spread)
     segc = seg_seq[:, None]
-    go_in, cos_table, sin_up, sin_down, pack_a, pack_b, pack_c, segc, d_sum = barrier(
-        (d_out, cos_table, sin_up, sin_down, pack_a, pack_b, pack_c, segc, d_sum)
+    go_in, cos_table, sin_up, sin_down, pack_a, pack_b, segc = barrier(
+        (d_out, cos_table, sin_up, sin_down, pack_a, pack_b, segc)
     )
     near_go = lax.ppermute(go_in, GROUP, spread)
     near_x, norms, norms_got, pack_a = barrier((near_x, norms, norms_got, pack_a))
@@ -541,28 +571,26 @@
     far_go = lax.ppermute(near_go, GROUP, forward)
     x_mine = join(block_input, near_x, far_x)
     x_other = lax.ppermute(x_mine, GROUP, pair)
-    far_go, got_a, pack_b = barrier((far_go, got_a, pack_b))
+    far_go, got_a = barrier((far_go, got_a))
     go_mine = join(d_out, near_go, far_go)
     go_other = lax.ppermute(go_mine, GROUP, pair)
     got_b = swap_row(pack_b)
-    x_other, pack_c = barrier((x_other, pack_c))
-    got_c = swap_row(pack_c)
     norms = jnp.concatenate([norms, norms_got], axis=1)
 
-    mix, gh, x_seq, go_seq, h_seq, own_a, send_a, gb_a = mlp_first(
+    hid_a, dp_a, x_seq, go_seq, h_seq, own_a, send_a = mlp_first(
         core_at, x_mine, x_other, go_mine, go_other, w_in, w_out, got_a, b_in[None],
         norms[2:3], norms[3:4], norms[0:1], norms[1:2],
     )
     x_seq, send_a = barrier((x_seq, send_a))
     back_a = swap_row(send_a)
-    mix, gh, own_b, send_b, gb_b = mlp_second(
-        x_seq, go_seq, mix, gh, w_in, w_out, got_b, b_in[None], norms[2:3], norms[3:4]
-    )
-    h_seq, send_b, got_c = barrier((h_seq, send_b, got_c))
+    hid_b, dp_b, own_b, send_b = mlp_second(
+        x_seq, go_seq, w_in, w_out, got_b, b_in[None], norms[2:3], norms[3:4]
+    )
+    h_seq, send_b = barrier((h_seq, send_b))
     back_b = swap_row(send_b)
     width = wq_t.shape[0]
     heads_args = (
-        wq_t, got_c, b_qkv.reshape(heads, 1, inner), w_dense, got_c,
+        wq_t, got_b, b_qkv.reshape(heads, 1, inner), w_dense, got_b,
         cos_table, sin_up, sin_down, segc, seg_seq[None, :],
     )
 
@@ -570,35 +598,35 @@
         return (own.astype(F32) + got.astype(F32)).astype(BF16)
 
     heads01 = attn_head(0, heads - 1, h_seq, go_seq, *heads_args)
-    go_seq, heads01, back_a = barrier((go_seq, heads01, back_a))
+    go_seq, heads01, back_a, back_b = barrier((go_seq, heads01, back_a, back_b))
     back01 = swap_row(heads01[3])
     sum_a = payload_sum(own_a, back_a)
+    sum_b = payload_sum(own_b, back_b)
     if chain:
         in_a = dp_inward(sum_a)
+        in_b = dp_inward(sum_b)
     head2 = attn_head(heads - 1, 1, h_seq, go_seq, *heads_args)
-    x_seq, head2, back_b = barrier((x_seq, head2, back_b))
+    x_seq, head2, back01 = barrier((x_seq, head2, back01))
     back2 = swap_row(head2[3])
-    sum_b = payload_sum(own_b, back_b)
+    sum_c = payload_sum(heads01[2], back01).reshape(-1, half)
     if chain:
-        in_b = dp_inward(sum_b)
+        x_seq, in_a, sum_a = barrier((x_seq, in_a, sum_a))
+        pair_a, other_a = dp_middle(sum_a, in_a)
+        in_c = dp_inward(sum_c)
     done = [heads01, head2]
-    mix_s, mix_k, dx_s, dx_k, attn_vec = close_layer(
-        core_at, x_seq, mix, gh, [a[0] for a in done], [a[1] for a in done],
-        wq_t, got_c, w_dense, got_c, norms[0:1], norms[2:3],
+    mix_s, mix_k, dx_s, dx_k = close_layer(
+        core_at, x_seq, [hid_a, hid_b, dp_a, dp_b], [a[0] for a in done], [a[1] for a in done],
+        wq_t, w_dense, w_in, w_out, got_a, got_b, norms[0:1], norms[2:3],
     )
     if chain:
-        mix_s, dx_s, in_a, sum_a, back01 = barrier((mix_s, dx_s, in_a, sum_a, back01))
-        pair_a, other_a = dp_middle(sum_a, in_a)
+        mix_s, dx_s, in_b, sum_b, in_c, sum_c, pair_a, other_a = barrier(
+            (mix_s, dx_s, in_b, sum_b, in_c, sum_c, pair_a, other_a)
+        )
+        totals_a = dp_outward(pair_a, other_a)
+        pair_b, other_b = dp_middle(sum_b, in_b)
+        pair_c, other_c = dp_middle(sum_c, in_c)
     mix_got = lax.ppermute(mix_s, GROUP, pair)
     dx_got = lax.ppermute(dx_s, GROUP, pair)
-    sum_c = payload_sum(heads01[2], back01).reshape(-1, half)
-    if chain:
-        in_c = dp_inward(sum_c)
-    hid = b_in.shape[0]
-    wide = jnp.concatenate([gb_a[0], gb_b[0]] + [a[4].reshape(-1) for a in done])
-    mine = jnp.concatenate([attn_vec[:4, :half].reshape(-1), wide])
-    theirs = jnp.concatenate([attn_vec[:4, half:].reshape(-1), wide])
-    vec_got = swap_row(theirs)
     mix_got, dx_got, back2 = barrier((mix_got, dx_got, back2))
     sum_d = payload_sum(head2[2], back2).reshape(-1, half)
     if chain:
@@ -614,30 +642,28 @@
     def reduce_end(near, far, kept):
         return near.astype(F32) + jnp.where(home, kept, far).astype(F32)
 
+    held = block_input.shape[0]
+    norm_sums = dx_k[held : held + 4].astype(F32) + dx_got[held : held + 4].astype(F32)
+    rest = norm_sums[:, :half] + swap_row(norm_sums[:, half:])
+    rest = swap_sum(rest, "col", n_col, 2)
+    mix_got, dx_got, rest = barrier((mix_got, dx_got, rest))
     mix_parts = reduce_start(mix_got, mix_k)
-    dx_parts = reduce_start(dx_got, dx_k)
-    vecs = mine + vec_got
-    wide = vecs[4 * half :]
-    rest = jnp.concatenate([vecs[: 4 * half], d_sum])
-    rest = swap_sum(rest, "col", n_col, 1)
-    rest = swap_sum(rest, "col", n_col, 2)
-    vecs = jnp.concatenate([rest, wide])
+    dx_parts = reduce_start(dx_got[:held], dx_k[:held])
     if chain:
-        in_b, sum_b, other_a = barrier((in_b, sum_b, other_a))
-        pair_b, other_b = dp_middle(sum_b, in_b)
-        totals_a = dp_outward(pair_a, other_a)
-        in_c, sum_c, in_d, sum_d = barrier((in_c, sum_c, in_d, sum_d))
-        pair_c, other_c = dp_middle(sum_c, in_c)
+        rest = swap_sum(rest, "dp", 4, 1)
+    if chain:
+        in_d, sum_d, pair_b, other_b = barrier((in_d, sum_d, pair_b, other_b))
+        totals_b = dp_outward(pair_b, other_b)
         pair_d, other_d = dp_middle(sum_d, in_d)
-        mix_parts, dx_parts, vecs, other_b = barrier((mix_parts, dx_parts, vecs, other_b))
-        totals_b = dp_outward(pair_b, other_b)
-        vecs = swap_sum(vecs, "dp", 4, 1)
-        vecs, other_c, other_d, totals_a = barrier((vecs, other_c, other_d, totals_a))
+        mix_parts, dx_parts, pair_c, other_c, totals_a, rest = barrier(
+            (mix_parts, dx_parts, pair_c, other_c, totals_a, rest)
+        )
+        rest = swap_sum(rest, "dp", 4, 2)
         totals_c = dp_outward(pair_c, other_c)
         totals_d = dp_outward(pair_d, other_d)
-        vecs = swap_sum(vecs, "dp", 4, 2)
-    else:
-        vecs = lax.psum(vecs, "dp")
+    dx_total = reduce_end(*dx_parts)
+    if not chain:
+        rest = lax.psum(rest, "dp")
         totals_a, totals_b, totals_c, totals_d = (
             (lax.psum(v.astype(F32), "dp"),) for v in (sum_a, sum_b, sum_c, sum_d)
         )
@@ -648,7 +674,7 @@
     block_output = (
         block_input.astype(F32) + reduce_end(*mix_parts) + b_dense + b_out
     ).astype(BF16)
-    d_input = d_out_f + reduce_end(*dx_parts)
+    d_input = d_out_f + dx_total
     upper_rows = slice(0, half)
     lower_rows = slice(half, 2 * half)
     grad_w_in = jnp.concatenate(
@@ -657,16 +683,20 @@
     grad_w_out = jnp.concatenate(
         [finish(totals_a, lower_rows), finish(totals_b, lower_rows)], axis=0
     )
-    split = [finish(totals_c, slice(n * (inner + HEAD_DIM), (n + 1) * (inner + HEAD_DIM)))
-             for n in range(heads - 1)] + [finish(totals_d, slice(0, inner + HEAD_DIM))]
+    deep = inner + HEAD_DIM
+    step = deep + EXTRA
+    split = [finish(totals_c, slice(n * step, n * step + step)) for n in range(heads - 1)]
+    split = split + [finish(totals_d, slice(0, step))]
     grad_w_qkv = jnp.concatenate([a[:inner] for a in split], axis=0).T
-    grad_w_dense = jnp.concatenate([a[inner:] for a in split], axis=0)
-    rest = vecs[: 5 * half].reshape(5, half)
-    grad_b_in = vecs[5 * half : 5 * half + hid]
-    grad_b_qkv = vecs[5 * half + hid :]
+    grad_w_dense = jnp.concatenate([a[inner:deep] for a in split], axis=0)
+    grad_b_qkv = jnp.concatenate([a[deep, :inner] for a in split])
+    grad_b_in = jnp.concatenate(
+        [finish(totals_a, 2 * half), finish(totals_b, 2 * half)]
+    )
+    grad_b_out = finish(totals_a, 2 * half + 1)
     return (
         block_output, d_input, grad_w_qkv, grad_b_qkv, grad_w_in, grad_b_in,
-        grad_w_dense, rest[4], grad_w_out, rest[4], rest[0], rest[1], rest[2], rest[3],
+        grad_w_dense, grad_b_out, grad_w_out, grad_b_out, rest[0], rest[1], rest[2], rest[3],
     )
 
 

time: 210 us -> 207 us (0.986); the launches traced: 208 us -> 203 us
  waiting for transfers between devices: 50.3 us -> 56.5 us
  starting transfers between devices: 58.7 us -> 54.3 us
  other arithmetic: 20.3 us -> 17.9 us
  local copies, waits for them, and re-layouts: 15.4 us -> 13 us
    ppermute x9 -> x8, waiting for transfers between devices: 0.02 us -> 11.8 us  [swap_row(): return lax.ppermute(value, 'row', [(0, 1), (1, 0)])]
    pallas_call x1, Pallas kernels: 8.51 us -> 12.7 us  [close_layer(): pl.pallas_call(close_kernel, grid_spec=pltpu.PrefetchScalarGridSpec(num_s...]
    slice x13 -> x9, local copies, waits for them, and re-layouts: 5.41 us -> 1.38 us  [the longest x1 1.35 us: local(): w_in[:, half:]]
    pallas_call x1, Pallas kernels: 12.5 us -> 9.03 us  [mlp_second(): pl.pallas_call(mlp_second_kernel, grid=(rows // BLOCK,), in_specs=[row_sp...]
    ppermute x4 -> x3, starting transfers between devices: 5.99 us -> 2.64 us  [swap_sum(): lax.ppermute(value, axis, [(i, i ^ bit) for i in range(size)])]
    ppermute x4, waiting for transfers between devices: 3.34 us -> 0.01 us  [dp_inward(): return lax.ppermute(value, 'dp', [(0, 1), (3, 2)])]
    convert_element_type x3, other arithmetic: 3.63 us -> 0.43 us  [payload_sum(): return (own.astype(F32) + got.astype(F32)).astype(BF16)]
    pallas_call x1, Pallas kernels: 12.9 us -> 10.1 us  [mlp_first(): pl.pallas_call(mlp_first_kernel, grid_spec=pltpu.PrefetchScalarGridSpec(n...]
  transfers between devices with their start and end apart: 37 -> 35, of which waited for: 12 -> 13; matrix products, arithmetic and copies ran while one was open for 13% -> 10% of each run, Pallas kernels for 30% -> 30%
where the time goes in v3:
time: 207 us; the launch traced here: 203 us
  Pallas kernels  60.2 us (29%)
  waiting for transfers between devices  56.5 us (27%)
  starting transfers between devices  54.3 us (26%)
  other arithmetic  17.9 us (9%)
  local copies, waits for them, and re-layouts  13 us (6%)
    pallas_call x2, Pallas kernels, attn_head(): pl.pallas_call(attn_kernel, grid=(count,), in_specs=specs, out_specs=[per...  28.4 us
    ppermute x4, starting transfers between devices, dp_inward(): return lax.ppermute(value, 'dp', [(0, 1), (3, 2)])  15.3 us
    pallas_call x1, Pallas kernels, close_layer(): pl.pallas_call(close_kernel, grid_spec=pltpu.PrefetchScalarGridSpec(num_s...  12.7 us
    ppermute x8, starting transfers between devices, swap_row(): return lax.ppermute(value, 'row', [(0, 1), (1, 0)])  12.5 us
    ppermute x8, waiting for transfers between devices, swap_row(): return lax.ppermute(value, 'row', [(0, 1), (1, 0)])  11.8 us
    ppermute x4, waiting for transfers between devices, dp_outward(): return (total, lax.ppermute(total, 'dp', [(1, 0), (2, 3)]))  10.9 us
    pallas_call x1, Pallas kernels, mlp_first(): pl.pallas_call(mlp_first_kernel, grid_spec=pltpu.PrefetchScalarGridSpec(n...  10.1 us
    ppermute x2, waiting for transfers between devices, reduce_start(): lax.ppermute(jnp.where(home, low_sum[:, half:], low_sum[:, :half]), GROUP...  9.14 us
  transfers between devices with their start and end apart: 35, of which 13 were waited for; matrix products, arithmetic and copies ran while one was open for 10% of the time, Pallas kernels for 30%

profile of v3, /device:TPU:0, one launch (start us, length us, event | category | flops | bytes accessed | tf_op | source)
XLA Modules:
  0.0 203.4 jit_solution(2619902234287140351)
XLA Ops:
  3.5 3.0 %collective-permute-start.1 = (f32[4,384]{1,0:T(4,128)S(1)}, f32[4,384]{1,0:T(4,128)S(1)}, u32[]{:S(2)}, u32[]{:S(2)}) collective-permute-start(f32[4,384]{1,0:T(4,128)S(1)} %pad_maximum_fusion.5), channel_id=1, source_target_pairs={{0,4},{4,0},{1,5},{5,1},{2,6},{6,2},{3,7},{7,3},{8,12},{12,8},{9,1... | collective-permute-start | bytes 18440 | tf_op jit(solution)/shard_map/ppermute | solution.py:481
  6.5 1.5 collective-permute-start
  8.7 1.3 fusion.16
  10.1 1.1 pad_maximum_fusion
  11.2 3.2 %fusion = (f32[1024,128]{1,0:T(8,128)}, f32[1024,128]{1,0:T(8,128)}, f32[1024,128]{1,0:T(8,128)}) fusion(f32[128]{0:T(128)S(1)} %compare_select_fusion.2, f32[1024]{0:T(1024)S(1)} %dynamic-slice_convert_fusion, pred[128]{0:T(512)(128)(4,1)S(1)} %get-tuple-element.215, pred[128]{0:T(512)(128)(4,1)S(1)} %get-tuple-element.216), kind=kLoop, calls=%fused_computation.19 | loop fusion | flops 524288 | bytes 1577728 | tf_op jit(solution)/shard_map/jit(_where)/select_n | solution.py:553
  15.9 1.5 collective-permute-done
  17.4 4.4 %collective-permute-start.2 = (bf16[512,384]{1,0:T(8,128)(2,1)}, bf16[512,384]{1,0:T(8,128)(2,1)S(1)}, u32[]{:S(2)}, u32[]{:S(2)}) collective-permute-start(bf16[512,384]{1,0:T(8,128)(2,1)} %collective-permute-done), channel_id=1, source_target_pairs={{0,2},{1,3},{6,4},{7,5},{8,10},{9,11},{14,12},{15,13},{16,18},{17,... | collective-permute-start | bytes 1179656 | tf_op jit(solution)/shard_map/ppermute | solution.py:569
  21.8 2.0 collective-permute-start.8
  23.8 3.6 %collective-permute-done.4 = bf16[512,384]{1,0:T(8,128)(2,1)S(1)} collective-permute-done((bf16[512,384]{1,0:T(8,128)(2,1)S(1)}, bf16[512,384]{1,0:T(8,128)(2,1)S(1)}, u32[]{:S(2)}, u32[]{:S(2)}) %collective-permute-start.4) | collective-permute-done | bytes 393248 | tf_op jit(solution)/shard_map/ppermute | solution.py:567
  27.4 2.6 %collective-permute-start.5 = (bf16[512,384]{1,0:T(8,128)(2,1)S(1)}, bf16[512,384]{1,0:T(8,128)(2,1)S(1)}, u32[]{:S(2)}, u32[]{:S(2)}) collective-permute-start(bf16[512,384]{1,0:T(8,128)(2,1)S(1)} %collective-permute-done.4), channel_id=1, source_target_pairs={{0,2},{1,3},{6,4},{7,5},{8,10},{9,11},{14,12},{15,13},{16,18},{17,... | collective-permute-start | bytes 1179656 | tf_op jit(solution)/shard_map/ppermute | solution.py:571
  30.1 4.1 %collective-permute-done.2 = bf16[512,384]{1,0:T(8,128)(2,1)S(1)} collective-permute-done((bf16[512,384]{1,0:T(8,128)(2,1)}, bf16[512,384]{1,0:T(8,128)(2,1)S(1)}, u32[]{:S(2)}, u32[]{:S(2)}) %collective-permute-start.2) | collective-permute-done | bytes 393248 | tf_op jit(solution)/shard_map/ppermute | solution.py:569
  34.2 1.1 broadcast_select_fusion.5
  35.4 6.1 %collective-permute-done.5 = bf16[512,384]{1,0:T(8,128)(2,1)S(1)} collective-permute-done((bf16[512,384]{1,0:T(8,128)(2,1)S(1)}, bf16[512,384]{1,0:T(8,128)(2,1)S(1)}, u32[]{:S(2)}, u32[]{:S(2)}) %collective-permute-start.5) | collective-permute-done | bytes 393248 | tf_op jit(solution)/shard_map/ppermute | solution.py:571
  43.6 1.2 collective-permute-done.7.go_ref
  44.8 10.1 %mlp_first.1 = (bf16[1024,384]{1,0:T(8,128)(2,1)}, bf16[1024,384]{1,0:T(8,128)(2,1)}, bf16[1024,768]{1,0:T(8,128)(2,1)}, bf16[1024,768]{1,0:T(8,128)(2,1)}, bf16...) custom-call(s32[1]{0:T(128)} %bitcast.core_ref, bf16[512,768]{1,0:T(8,128)(2,1)} %copy-done.3, ...), custom_call_target="tpu_custom_call" | custom-call | flops 1024 | bytes 1024 | tf_op jit(solution)/shard_map/mlp_first/pallas_call | solution.py:185
  54.9 1.5 collective-permute-start.9
  56.4 8.9 %collective-permute-done.8.wi_p.wo_p.wp_ref.dp_ref.got_b = bf16[1536,384]{1,0:T(8,128)(2,1)S(1)} collective-permute-done((bf16[1536,384]{1,0:T(8,128)(2,1)}, bf16[1536,384]{1,0:T(8,128)(2,1)S(1)}, u32[]{:S(2)}, u32[]{:S(2)}) %collective-permute-start.8) | collective-permute-done | bytes 1179680 | tf_op jit(solution)/shard_map/ppermute | solution.py:481
  65.3 1.0 copy-done
  66.3 9.0 %mlp_second.1 = (bf16[1024,384]{1,0:T(8,128)(2,1)}, bf16[1024,384]{1,0:T(8,128)(2,1)}, bf16[784,384]{1,0:T(8,128)(2,1)}, bf16[784,384]{1,0:T(8,128)(2,1)}) custom-call(bf16[1024,768]{1,0:T(8,128)(2,1)} %get-tuple-element.134.x_ref, bf16[1024,768]{1,0:T(8,128)(2,1)} %get-tuple-element.125.go_ref, bf16[384,768]{1,0:T(8,128)(2,1)} %wi_o.5, ...), custom_call_target="tpu_custom_call" | custom-call | flops 1024 | bytes 1024 | tf_op jit(solution)/shard_map/mlp_second/pallas_call | solution.py:217
  76.1 1.0 copy.30.segc_ref
  77.2 17.9 %attn_head.2 = (bf16[2,64,1024]{2,1,0:T(8,128)(2,1)}, bf16[2,1024,192]{2,1,0:T(8,128)(2,1)}, bf16[2,272,384]{2,1,0:T(8,128)(2,1)}, bf16[2,272,384]{2,1,0:T(8,128)(2,1)}) custom-call(bf16[1024,768]{1,0:T(8,128)(2,1)} %get-tuple-element.114.h_ref, bf16[1024,768]{1,0:T(8,128)(2,1)} %get-tuple-element.125.go_ref, bf16[576,384]{1,0:T(8,128)(2,1)} %bitcast.12, ...), custom_call_target="tpu_custom_call" | custom-call | flops 1024 | bytes 1024 | tf_op jit(solution)/shard_map/attn_head/pallas_call | solution.py:338
  96.2 3.7 %collective-permute-start.12 = (bf16[784,384]{1,0:T(8,128)(2,1)S(1)}, bf16[784,384]{1,0:T(8,128)(2,1)S(1)}, u32[]{:S(2)}, u32[]{:S(2)}) collective-permute-start(bf16[784,384]{1,0:T(8,128)(2,1)S(1)} %add_convert_fusion.7), channel_id=1, source_target_pairs={{0,8},{24,16},{1,9},{25,17},{2,10},{26,18},{3,11},{27,19},{4,12},{... | collective-permute-start | bytes 1806344 | tf_op jit(solution)/shard_map/ppermute | solution.py:485
  99.8 2.1 %collective-permute-start.11 = (bf16[2,272,384]{2,1,0:T(8,128)(2,1)S(1)}, bf16[2,272,384]{2,1,0:T(8,128)(2,1)S(1)}, u32[]{:S(2)}, u32[]{:S(2)}) collective-permute-start(bf16[2,272,384]{2,1,0:T(8,128)(2,1)S(1)} %copy-done.31), channel_id=1, source_target_pairs={{0,4},{4,0},{1,5},{5,1},{2,6},{6,2},{3,7},{7,3},{8,12},{12,8},{9,1... | collective-permute-start | bytes 1253384 | tf_op jit(solution)/shard_map/ppermute | solution.py:481
  102.1 1.5 collective-permute-start.13
  103.6 10.5 %attn_head.3 = (bf16[1,64,1024]{2,1,0:T(8,128)(2,1)}, bf16[1,1024,192]{2,1,0:T(8,128)(2,1)}, bf16[1,272,384]{2,1,0:T(8,128)(2,1)}, bf16[1,272,384]{2,1,0:T(8,128)(2,1)}) custom-call(bf16[1024,768]{1,0:T(8,128)(2,1)} %get-tuple-element.114.h_ref, bf16[1024,768]{1,0:T(8,128)(2,1)} %get-tuple-element.125.go_ref, bf16[576,384]{1,0:T(8,128)(2,1)} %bitcast.13, ...), custom_call_target="tpu_custom_call" | custom-call | flops 1024 | bytes 1024 | tf_op jit(solution)/shard_map/attn_head/pallas_call | solution.py:338
  115.2 6.8 %collective-permute-start.14 = (bf16[544,384]{1,0:T(8,128)(2,1)S(1)}, bf16[544,384]{1,0:T(8,128)(2,1)S(1)}, u32[]{:S(2)}, u32[]{:S(2)}) collective-permute-start(bf16[544,384]{1,0:T(8,128)(2,1)S(1)} %bitcast.16), channel_id=1, source_target_pairs={{0,8},{24,16},{1,9},{25,17},{2,10},{26,18},{3,11},{27,19},{4,12},{... | collective-permute-start | bytes 1253384 | tf_op jit(solution)/shard_map/ppermute | solution.py:485
  122.0 12.7 %close_layer.1 = (bf16[512,768]{1,0:T(8,128)(2,1)}, bf16[512,768]{1,0:T(8,128)(2,1)}, bf16[528,768]{1,0:T(8,128)(2,1)}, bf16[528,768]{1,0:T(8,128)(2,1)}) custom-call(s32[1]{0:T(128)} %bitcast.core_ref, bf16[1024,768]{1,0:T(8,128)(2,1)} %get-tuple-element.134.x_ref, bf16[1024,384]{1,0:T(8,128)(2,1)} %get-tuple-element.135.hid_a, ...), custom_call_target="tpu_custom_call" | custom-call | flops 1024 | bytes 1024 | tf_op jit(solution)/shard_map/close_layer/pallas_call | solution.py:451
  136.3 2.0 collective-permute-start.18
  138.3 1.1 add_convert_fusion.9
  141.3 2.5 %collective-permute-done.18 = bf16[1,272,384]{2,1,0:T(8,128)(2,1)S(1)} collective-permute-done((bf16[1,272,384]{2,1,0:T(8,128)(2,1)S(1)}, bf16[1,272,384]{2,1,0:T(8,128)(2,1)S(1)}, u32[]{:S(2)}, u32[]{:S(2)}) %collective-permute-start.18) | collective-permute-done | bytes 208928 | tf_op jit(solution)/shard_map/ppermute | solution.py:481
  143.8 1.8 collective-permute-start.19
  145.7 1.3 collective-permute-start.26
  147.5 1.1 collective-permute-start.20
  148.6 3.3 %collective-permute-start.29 = (bf16[272,384]{1,0:T(8,128)(2,1)S(1)}, bf16[272,384]{1,0:T(8,128)(2,1)S(1)}, u32[]{:S(2)}, u32[]{:S(2)}) collective-permute-start(bf16[272,384]{1,0:T(8,128)(2,1)S(1)} %fusion.3), channel_id=1, source_target_pairs={{0,8},{24,16},{1,9},{25,17},{2,10},{26,18},{3,11},{27,19},{4,12},{... | collective-permute-start | bytes 626696 | tf_op jit(solution)/shard_map/ppermute | solution.py:485
  152.2 1.5 collective-permute-start.27
  154.1 8.1 %collective-permute-done.27 = f32[4,384]{1,0:T(4,128)S(1)} collective-permute-done((f32[4,384]{1,0:T(4,128)S(1)}, f32[4,384]{1,0:T(4,128)S(1)}, u32[]{:S(2)}, u32[]{:S(2)}) %collective-permute-start.27) | collective-permute-done | bytes 6176 | tf_op jit(solution)/shard_map/ppermute | solution.py:506
  163.6 4.2 %collective-permute-start.21 = (bf16[512,384]{1,0:T(8,128)(2,1)S(1)}, bf16[512,384]{1,0:T(8,128)(2,1)S(1)}, u32[]{:S(2)}, u32[]{:S(2)}) collective-permute-start(bf16[512,384]{1,0:T(8,128)(2,1)S(1)} %get-tuple-element.198), channel_id=1, source_target_pairs={{0,4},{1,5},{2,0},{3,1},{4,6},{5,7},{6,2},{7,3},{8,12},{9,13},{10,... | collective-permute-start | bytes 1179656 | tf_op jit(solution)/shard_map/ppermute | solution.py:637
  169.4 5.0 %collective-permute-done.23 = bf16[512,384]{1,0:T(8,128)(2,1)S(1)} collective-permute-done((bf16[512,384]{1,0:T(8,128)(2,1)S(1)}, bf16[512,384]{1,0:T(8,128)(2,1)S(1)}, u32[]{:S(2)}, u32[]{:S(2)}) %collective-permute-start.23) | collective-permute-done | bytes 393248 | tf_op jit(solution)/shard_map/ppermute | solution.py:637
  174.3 1.3 collective-permute-start.33
  175.6 4.2 %collective-permute-done.21 = bf16[512,384]{1,0:T(8,128)(2,1)S(1)} collective-permute-done((bf16[512,384]{1,0:T(8,128)(2,1)S(1)}, bf16[512,384]{1,0:T(8,128)(2,1)S(1)}, u32[]{:S(2)}, u32[]{:S(2)}) %collective-permute-start.21) | collective-permute-done | bytes 393248 | tf_op jit(solution)/shard_map/ppermute | solution.py:637
  180.0 1.1 add_add_fusion
  181.1 1.0 add_convert_fusion.11
  182.3 1.3 collective-permute-start.32
  183.6 1.3 collective-permute-start.28
  185.6 8.0 %collective-permute-done.32 = bf16[272,384]{1,0:T(8,128)(2,1)S(1)} collective-permute-done((bf16[272,384]{1,0:T(8,128)(2,1)S(1)}, bf16[272,384]{1,0:T(8,128)(2,1)S(1)}, u32[]{:S(2)}, u32[]{:S(2)}) %collective-permute-start.32) | collective-permute-done | bytes 208928 | tf_op jit(solution)/shard_map/ppermute | solution.py:495
  195.0 1.1 maximum_convert_fusion.1
  196.1 1.1 maximum_convert_fusion
  197.2 2.8 %collective-permute-done.28 = bf16[544,384]{1,0:T(8,128)(2,1)S(1)} collective-permute-done((bf16[544,384]{1,0:T(8,128)(2,1)S(1)}, bf16[544,384]{1,0:T(8,128)(2,1)S(1)}, u32[]{:S(2)}, u32[]{:S(2)}) %collective-permute-start.28) | collective-permute-done | bytes 417824 | tf_op jit(solution)/shard_map/ppermute | solution.py:495
  (166 shorter events, 23.3 us)
Async XLA Ops:
  2.7 7.3 %copy-start.1 = (bf16[384,576]{0,1:T(8,128)(2,1)S(1)}, bf16[384,576]{0,1:T(8,128)(2,1)}, u32[]{:S(2)}) copy-start(bf16[384,576]{0,1:T(8,128)(2,1)} %param.17) | copy-start | bytes 1327108
  2.7 7.3 %copy-start.5 = (bf16[192,384]{1,0:T(8,128)(2,1)S(1)}, bf16[192,384]{1,0:T(8,128)(2,1)}, u32[]{:S(2)}) copy-start(bf16[192,384]{1,0:T(8,128)(2,1)} %wd_o.1) | copy-start | bytes 442372
  3.5 12.4 %collective-permute-start.1 = (f32[4,384]{1,0:T(4,128)S(1)}, f32[4,384]{1,0:T(4,128)S(1)}, u32[]{:S(2)}, u32[]{:S(2)}) collective-permute-start(f32[4,384]{1,0:T(4,128)S(1)} %pad_maximum_fusion.5), channel_id=1, source_target_pairs={{0,4},{4,0},{1,5},{5,1},{2,6},{6,2},{3,7},{7,3},{8,12},{12,8},{9,1... | collective-permute-start | bytes 18440 | tf_op jit(solution)/shard_map/ppermute | solution.py:481
  6.5 10.9 %collective-permute-start = (bf16[512,384]{1,0:T(8,128)(2,1)}, bf16[512,384]{1,0:T(8,128)(2,1)}, u32[]{:S(2)}, u32[]{:S(2)}) collective-permute-start(bf16[512,384]{1,0:T(8,128)(2,1)} %param.16), channel_id=1, source_target_pairs={{0,2},{1,3},{2,6},{3,7},{4,0},{5,1},{6,4},{7,5},{8,10},{9,11},{10,... | collective-permute-start | bytes 1179656 | tf_op jit(solution)/shard_map/ppermute | solution.py:562
  11.2 23.0 %copy-start.9 = (bf16[512,384]{1,0:T(8,128)(2,1)S(1)}, bf16[512,384]{1,0:T(8,128)(2,1)}, u32[]{:S(2)}) copy-start(bf16[512,384]{1,0:T(8,128)(2,1)} %param.16) | copy-start | bytes 1179652
  15.3 60.8 %copy-start.24 = (s32[1024]{0:T(1024)}, s32[1024]{0:T(1024)S(1)}, u32[]{:S(2)}) copy-start(s32[1024]{0:T(1024)S(1)} %dynamic_slice.7) | copy-start | bytes 12292
  15.3 12.1 %collective-permute-start.4 = (bf16[512,384]{1,0:T(8,128)(2,1)S(1)}, bf16[512,384]{1,0:T(8,128)(2,1)S(1)}, u32[]{:S(2)}, u32[]{:S(2)}) collective-permute-start(bf16[512,384]{1,0:T(8,128)(2,1)S(1)} %copy-done.7), channel_id=1, source_target_pairs={{0,2},{1,3},{2,6},{3,7},{4,0},{5,1},{6,4},{7,5},{8,10},{9,11},{10,... | collective-permute-start | bytes 1179656 | tf_op jit(solution)/shard_map/ppermute | solution.py:567
  17.4 16.8 %collective-permute-start.2 = (bf16[512,384]{1,0:T(8,128)(2,1)}, bf16[512,384]{1,0:T(8,128)(2,1)S(1)}, u32[]{:S(2)}, u32[]{:S(2)}) collective-permute-start(bf16[512,384]{1,0:T(8,128)(2,1)} %collective-permute-done), channel_id=1, source_target_pairs={{0,2},{1,3},{6,4},{7,5},{8,10},{9,11},{14,12},{15,13},{16,18},{17,... | collective-permute-start | bytes 1179656 | tf_op jit(solution)/shard_map/ppermute | solution.py:569
  21.7 19.8 %collective-permute-start.6 = (bf16[768,384]{1,0:T(8,128)(2,1)}, bf16[768,384]{1,0:T(8,128)(2,1)S(1)}, u32[]{:S(2)}, u32[]{:S(2)}) collective-permute-start(bf16[768,384]{1,0:T(8,128)(2,1)} %pad_maximum_fusion.3), channel_id=1, source_target_pairs={{0,4},{4,0},{1,5},{5,1},{2,6},{6,2},{3,7},{7,3},{8,12},{12,8},{9,1... | collective-permute-start | bytes 1769480 | tf_op jit(solution)/shard_map/ppermute | solution.py:481
  21.8 43.5 %collective-permute-start.8 = (bf16[1536,384]{1,0:T(8,128)(2,1)}, bf16[1536,384]{1,0:T(8,128)(2,1)S(1)}, u32[]{:S(2)}, u32[]{:S(2)}) collective-permute-start(bf16[1536,384]{1,0:T(8,128)(2,1)} %pad_maximum_fusion), channel_id=1, source_target_pairs={{0,4},{4,0},{1,5},{5,1},{2,6},{6,2},{3,7},{7,3},{8,12},{12,8},{9,1... | collective-permute-start | bytes 3538952 | tf_op jit(solution)/shard_map/ppermute | solution.py:481
  27.4 14.2 %collective-permute-start.5 = (bf16[512,384]{1,0:T(8,128)(2,1)S(1)}, bf16[512,384]{1,0:T(8,128)(2,1)S(1)}, u32[]{:S(2)}, u32[]{:S(2)}) collective-permute-start(bf16[512,384]{1,0:T(8,128)(2,1)S(1)} %collective-permute-done.4), channel_id=1, source_target_pairs={{0,2},{1,3},{6,4},{7,5},{8,10},{9,11},{14,12},{15,13},{16,18},{17,... | collective-permute-start | bytes 1179656 | tf_op jit(solution)/shard_map/ppermute | solution.py:571
  35.3 6.4 %copy-start.3 = (bf16[512,768]{1,0:T(8,128)(2,1)}, bf16[512,768]{1,0:T(8,128)(2,1)S(1)}, u32[]{:S(2)}) copy-start(bf16[512,768]{1,0:T(8,128)(2,1)S(1)} %pad_maximum_fusion.1.xm_ref) | copy-start | bytes 2359300
  35.3 8.3 %collective-permute-start.3 = (bf16[512,768]{1,0:T(8,128)(2,1)S(1)}, bf16[512,768]{1,0:T(8,128)(2,1)}, u32[]{:S(2)}, u32[]{:S(2)}) collective-permute-start(bf16[512,768]{1,0:T(8,128)(2,1)S(1)} %pad_maximum_fusion.1.xm_ref), channel_id=1, source_target_pairs={{0,1},{1,0},{2,3},{3,2},{4,5},{5,4},{6,7},{7,6},{8,9},{9,8},{10,11... | collective-permute-start | bytes 2359304 | tf_op jit(solution)/shard_map/ppermute | solution.py:573
  42.4 2.4 %collective-permute-start.7 = (bf16[512,768]{1,0:T(8,128)(2,1)S(1)}, bf16[512,768]{1,0:T(8,128)(2,1)}, u32[]{:S(2)}, u32[]{:S(2)}) collective-permute-start(bf16[512,768]{1,0:T(8,128)(2,1)S(1)} %pad_maximum_fusion.2.gm_ref), channel_id=1, source_target_pairs={{0,1},{1,0},{2,3},{3,2},{4,5},{5,4},{6,7},{7,6},{8,9},{9,8},{10,11... | collective-permute-start | bytes 2359304 | tf_op jit(solution)/shard_map/ppermute | solution.py:576
  54.9 40.2 %collective-permute-start.9 = (bf16[784,384]{1,0:T(8,128)(2,1)}, bf16[784,384]{1,0:T(8,128)(2,1)S(1)}, u32[]{:S(2)}, u32[]{:S(2)}) collective-permute-start(bf16[784,384]{1,0:T(8,128)(2,1)} %get-tuple-element.123), channel_id=1, source_target_pairs={{0,4},{4,0},{1,5},{5,1},{2,6},{6,2},{3,7},{7,3},{8,12},{12,8},{9,1... | collective-permute-start | bytes 1806344 | tf_op jit(solution)/shard_map/ppermute | solution.py:481
  66.3 9.1 %copy-start.27 = (f32[576]{0:T(1024)S(1)}, f32[576]{0:T(1024)}, u32[]{:S(2)}) copy-start(f32[576]{0:T(1024)} %param.18) | copy-start | bytes 6916
  75.4 19.7 %collective-permute-start.10 = (bf16[784,384]{1,0:T(8,128)(2,1)}, bf16[784,384]{1,0:T(8,128)(2,1)S(1)}, u32[]{:S(2)}, u32[]{:S(2)}) collective-permute-start(bf16[784,384]{1,0:T(8,128)(2,1)} %get-tuple-element.124), channel_id=1, source_target_pairs={{0,4},{4,0},{1,5},{5,1},{2,6},{6,2},{3,7},{7,3},{8,12},{12,8},{9,1... | collective-permute-start | bytes 1806344 | tf_op jit(solution)/shard_map/ppermute | solution.py:481
  77.2 18.8 %copy-start.17 = (bf16[784,384]{1,0:T(8,128)(2,1)S(1)}, bf16[784,384]{1,0:T(8,128)(2,1)}, u32[]{:S(2)}) copy-start(bf16[784,384]{1,0:T(8,128)(2,1)} %get-tuple-element.132) | copy-start | bytes 1806340
  95.1 6.8 %copy-start.18 = (bf16[784,384]{1,0:T(8,128)(2,1)S(1)}, bf16[784,384]{1,0:T(8,128)(2,1)}, u32[]{:S(2)}) copy-start(bf16[784,384]{1,0:T(8,128)(2,1)} %get-tuple-element.146) | copy-start | bytes 1806340
  96.2 17.9 %collective-permute-start.12 = (bf16[784,384]{1,0:T(8,128)(2,1)S(1)}, bf16[784,384]{1,0:T(8,128)(2,1)S(1)}, u32[]{:S(2)}, u32[]{:S(2)}) collective-permute-start(bf16[784,384]{1,0:T(8,128)(2,1)S(1)} %add_convert_fusion.7), channel_id=1, source_target_pairs={{0,8},{24,16},{1,9},{25,17},{2,10},{26,18},{3,11},{27,19},{4,12},{... | collective-permute-start | bytes 1806344 | tf_op jit(solution)/shard_map/ppermute | solution.py:485
  99.8 14.2 %collective-permute-start.11 = (bf16[2,272,384]{2,1,0:T(8,128)(2,1)S(1)}, bf16[2,272,384]{2,1,0:T(8,128)(2,1)S(1)}, u32[]{:S(2)}, u32[]{:S(2)}) collective-permute-start(bf16[2,272,384]{2,1,0:T(8,128)(2,1)S(1)} %copy-done.31), channel_id=1, source_target_pairs={{0,4},{4,0},{1,5},{5,1},{2,6},{6,2},{3,7},{7,3},{8,12},{12,8},{9,1... | collective-permute-start | bytes 1253384 | tf_op jit(solution)/shard_map/ppermute | solution.py:481
  102.1 32.6 %collective-permute-start.13 = (bf16[784,384]{1,0:T(8,128)(2,1)S(1)}, bf16[784,384]{1,0:T(8,128)(2,1)S(1)}, u32[]{:S(2)}, u32[]{:S(2)}) collective-permute-start(bf16[784,384]{1,0:T(8,128)(2,1)S(1)} %add_convert_fusion.6), channel_id=1, source_target_pairs={{0,8},{24,16},{1,9},{25,17},{2,10},{26,18},{3,11},{27,19},{4,12},{... | collective-permute-start | bytes 1806344 | tf_op jit(solution)/shard_map/ppermute | solution.py:485
  114.3 20.5 %collective-permute-start.15 = (bf16[784,384]{1,0:T(8,128)(2,1)S(1)}, bf16[784,384]{1,0:T(8,128)(2,1)S(1)}, u32[]{:S(2)}, u32[]{:S(2)}) collective-permute-start(bf16[784,384]{1,0:T(8,128)(2,1)S(1)} %add_convert_fusion.5), channel_id=1, source_target_pairs={{8,16},{16,8},{9,17},{17,9},{10,18},{18,10},{11,19},{19,11},{12,20... | collective-permute-start | bytes 1806344 | tf_op jit(solution)/shard_map/ppermute | solution.py:490
  115.2 19.6 %collective-permute-start.14 = (bf16[544,384]{1,0:T(8,128)(2,1)S(1)}, bf16[544,384]{1,0:T(8,128)(2,1)S(1)}, u32[]{:S(2)}, u32[]{:S(2)}) collective-permute-start(bf16[544,384]{1,0:T(8,128)(2,1)S(1)} %bitcast.16), channel_id=1, source_target_pairs={{0,8},{24,16},{1,9},{25,17},{2,10},{26,18},{3,11},{27,19},{4,12},{... | collective-permute-start | bytes 1253384 | tf_op jit(solution)/shard_map/ppermute | solution.py:485
  122.0 14.2 %copy-start.32 = (bf16[1,272,384]{2,1,0:T(8,128)(2,1)S(1)}, bf16[1,272,384]{2,1,0:T(8,128)(2,1)}, u32[]{:S(2)}) copy-start(bf16[1,272,384]{2,1,0:T(8,128)(2,1)} %get-tuple-element.154) | copy-start | bytes 626692
  135.7 8.0 %collective-permute-start.17 = (bf16[528,768]{1,0:T(8,128)(2,1)}, bf16[528,768]{1,0:T(8,128)(2,1)S(1)}, u32[]{:S(2)}, u32[]{:S(2)}) collective-permute-start(bf16[528,768]{1,0:T(8,128)(2,1)} %get-tuple-element.153), channel_id=1, source_target_pairs={{0,1},{1,0},{2,3},{3,2},{4,5},{5,4},{6,7},{7,6},{8,9},{9,8},{10,11... | collective-permute-start | bytes 2433032 | tf_op jit(solution)/shard_map/ppermute | solution.py:629
  135.9 7.8 %collective-permute-start.16 = (bf16[512,768]{1,0:T(8,128)(2,1)}, bf16[512,768]{1,0:T(8,128)(2,1)S(1)}, u32[]{:S(2)}, u32[]{:S(2)}) collective-permute-start(bf16[512,768]{1,0:T(8,128)(2,1)} %get-tuple-element.152), channel_id=1, source_target_pairs={{0,1},{1,0},{2,3},{3,2},{4,5},{5,4},{6,7},{7,6},{8,9},{9,8},{10,11... | collective-permute-start | bytes 2359304 | tf_op jit(solution)/shard_map/ppermute | solution.py:628
  136.3 7.5 %collective-permute-start.18 = (bf16[1,272,384]{2,1,0:T(8,128)(2,1)S(1)}, bf16[1,272,384]{2,1,0:T(8,128)(2,1)S(1)}, u32[]{:S(2)}, u32[]{:S(2)}) collective-permute-start(bf16[1,272,384]{2,1,0:T(8,128)(2,1)S(1)} %copy-done.32), channel_id=1, source_target_pairs={{0,4},{4,0},{1,5},{5,1},{2,6},{6,2},{3,7},{7,3},{8,12},{12,8},{9,1... | collective-permute-start | bytes 626696 | tf_op jit(solution)/shard_map/ppermute | solution.py:481
  139.4 6.2 %copy-start.16 = (bf16[784,384]{1,0:T(8,128)(2,1)S(1)}, bf16[784,384]{1,0:T(8,128)(2,1)}, u32[]{:S(2)}) copy-start(bf16[784,384]{1,0:T(8,128)(2,1)} %copy-done.15) | copy-start | bytes 1806340
  139.4 28.4 %collective-permute-start.25 = (bf16[544,384]{1,0:T(8,128)(2,1)S(1)}, bf16[544,384]{1,0:T(8,128)(2,1)S(1)}, u32[]{:S(2)}, u32[]{:S(2)}) collective-permute-start(bf16[544,384]{1,0:T(8,128)(2,1)S(1)} %add_convert_fusion.9), channel_id=1, source_target_pairs={{8,16},{16,8},{9,17},{17,9},{10,18},{18,10},{11,19},{19,11},{12,20... | collective-permute-start | bytes 1253384 | tf_op jit(solution)/shard_map/ppermute | solution.py:490
  140.4 8.2 %copy-start.23 = (bf16[1,272,384]{2,1,0:T(8,128)(2,1)S(1)}, bf16[1,272,384]{2,1,0:T(8,128)(2,1)}, u32[]{:S(2)}) copy-start(bf16[1,272,384]{2,1,0:T(8,128)(2,1)} %get-tuple-element.173) | copy-start | bytes 626692
  140.4 22.4 %collective-permute-start.30 = (bf16[784,384]{1,0:T(8,128)(2,1)S(1)}, bf16[784,384]{1,0:T(8,128)(2,1)S(1)}, u32[]{:S(2)}, u32[]{:S(2)}) collective-permute-start(bf16[784,384]{1,0:T(8,128)(2,1)S(1)} %add_convert_fusion.3), channel_id=1, source_target_pairs={{8,16},{16,8},{9,17},{17,9},{10,18},{18,10},{11,19},{19,11},{12,20... | collective-permute-start | bytes 1806344 | tf_op jit(solution)/shard_map/ppermute | solution.py:490
  143.8 3.7 %collective-permute-start.19 = (f32[4,384]{1,0:T(4,128)S(1)}, f32[4,384]{1,0:T(4,128)S(1)}, u32[]{:S(2)}, u32[]{:S(2)}) collective-permute-start(f32[4,384]{1,0:T(4,128)S(1)} %slice.209), channel_id=1, source_target_pairs={{0,4},{4,0},{1,5},{5,1},{2,6},{6,2},{3,7},{7,3},{8,12},{12,8},{9,1... | collective-permute-start | bytes 18440 | tf_op jit(solution)/shard_map/ppermute | solution.py:481
  145.7 22.9 %collective-permute-start.26 = (bf16[784,384]{1,0:T(8,128)(2,1)S(1)}, bf16[784,384]{1,0:T(8,128)(2,1)S(1)}, u32[]{:S(2)}, u32[]{:S(2)}) collective-permute-start(bf16[784,384]{1,0:T(8,128)(2,1)S(1)} %add_convert_fusion.4), channel_id=1, source_target_pairs={{8,0},{16,24},{9,1},{17,25},{10,2},{18,26},{11,3},{19,27},{12,4},{... | collective-permute-start | bytes 1806344 | tf_op jit(solution)/shard_map/ppermute | solution.py:495
  147.5 4.5 %collective-permute-start.20 = (f32[4,384]{1,0:T(4,128)S(1)}, f32[4,384]{1,0:T(4,128)S(1)}, u32[]{:S(2)}, u32[]{:S(2)}) collective-permute-start(f32[4,384]{1,0:T(4,128)S(1)} %slice_add_fusion), channel_id=1, source_target_pairs={{0,2},{1,3},{2,0},{3,1},{4,6},{5,7},{6,4},{7,5},{8,10},{9,11},{10,... | collective-permute-start | bytes 18440 | tf_op jit(solution)/shard_map/ppermute | solution.py:506
  148.6 14.9 %collective-permute-start.29 = (bf16[272,384]{1,0:T(8,128)(2,1)S(1)}, bf16[272,384]{1,0:T(8,128)(2,1)S(1)}, u32[]{:S(2)}, u32[]{:S(2)}) collective-permute-start(bf16[272,384]{1,0:T(8,128)(2,1)S(1)} %fusion.3), channel_id=1, source_target_pairs={{0,8},{24,16},{1,9},{25,17},{2,10},{26,18},{3,11},{27,19},{4,12},{... | collective-permute-start | bytes 626696 | tf_op jit(solution)/shard_map/ppermute | solution.py:485
  152.2 10.1 %collective-permute-start.27 = (f32[4,384]{1,0:T(4,128)S(1)}, f32[4,384]{1,0:T(4,128)S(1)}, u32[]{:S(2)}, u32[]{:S(2)}) collective-permute-start(f32[4,384]{1,0:T(4,128)S(1)} %add.126), channel_id=1, source_target_pairs={{0,8},{8,0},{16,24},{24,16},{1,9},{9,1},{17,25},{25,17},{2,10},{10... | collective-permute-start | bytes 18440 | tf_op jit(solution)/shard_map/ppermute | solution.py:506
  162.3 12.1 %collective-permute-start.23 = (bf16[512,384]{1,0:T(8,128)(2,1)S(1)}, bf16[512,384]{1,0:T(8,128)(2,1)S(1)}, u32[]{:S(2)}, u32[]{:S(2)}) collective-permute-start(bf16[512,384]{1,0:T(8,128)(2,1)S(1)} %get-tuple-element.195), channel_id=1, source_target_pairs={{0,4},{1,5},{2,0},{3,1},{4,6},{5,7},{6,2},{7,3},{8,12},{9,13},{10,... | collective-permute-start | bytes 1179656 | tf_op jit(solution)/shard_map/ppermute | solution.py:637
  162.9 12.8 %collective-permute-start.24 = (bf16[512,384]{1,0:T(8,128)(2,1)S(1)}, bf16[512,384]{1,0:T(8,128)(2,1)S(1)}, u32[]{:S(2)}, u32[]{:S(2)}) collective-permute-start(bf16[512,384]{1,0:T(8,128)(2,1)S(1)} %get-tuple-element.196), channel_id=1, source_target_pairs={{2,4},{3,5},{4,2},{5,3},{10,12},{11,13},{12,10},{13,11},{18,20},{1... | collective-permute-start | bytes 1179656 | tf_op jit(solution)/shard_map/ppermute | solution.py:640
  163.6 16.3 %collective-permute-start.21 = (bf16[512,384]{1,0:T(8,128)(2,1)S(1)}, bf16[512,384]{1,0:T(8,128)(2,1)S(1)}, u32[]{:S(2)}, u32[]{:S(2)}) collective-permute-start(bf16[512,384]{1,0:T(8,128)(2,1)S(1)} %get-tuple-element.198), channel_id=1, source_target_pairs={{0,4},{1,5},{2,0},{3,1},{4,6},{5,7},{6,2},{7,3},{8,12},{9,13},{10,... | collective-permute-start | bytes 1179656 | tf_op jit(solution)/shard_map/ppermute | solution.py:637
  167.8 12.1 %collective-permute-start.22 = (bf16[512,384]{1,0:T(8,128)(2,1)S(1)}, bf16[512,384]{1,0:T(8,128)(2,1)S(1)}, u32[]{:S(2)}, u32[]{:S(2)}) collective-permute-start(bf16[512,384]{1,0:T(8,128)(2,1)S(1)} %get-tuple-element.199), channel_id=1, source_target_pairs={{2,4},{3,5},{4,2},{5,3},{10,12},{11,13},{12,10},{13,11},{18,20},{1... | collective-permute-start | bytes 1179656 | tf_op jit(solution)/shard_map/ppermute | solution.py:640
  168.5 11.4 %copy-start.8 = (bf16[512,384]{1,0:T(8,128)(2,1)S(1)}, bf16[512,384]{1,0:T(8,128)(2,1)}, u32[]{:S(2)}) copy-start(bf16[512,384]{1,0:T(8,128)(2,1)} %param.31) | copy-start | bytes 1179652
  168.7 13.6 %collective-permute-start.31 = (bf16[272,384]{1,0:T(8,128)(2,1)S(1)}, bf16[272,384]{1,0:T(8,128)(2,1)S(1)}, u32[]{:S(2)}, u32[]{:S(2)}) collective-permute-start(bf16[272,384]{1,0:T(8,128)(2,1)S(1)} %add_convert_fusion.13), channel_id=1, source_target_pairs={{8,16},{16,8},{9,17},{17,9},{10,18},{18,10},{11,19},{19,11},{12,20... | collective-permute-start | bytes 626696 | tf_op jit(solution)/shard_map/ppermute | solution.py:490
  174.3 19.4 %collective-permute-start.33 = (bf16[784,384]{1,0:T(8,128)(2,1)S(1)}, bf16[784,384]{1,0:T(8,128)(2,1)S(1)}, u32[]{:S(2)}, u32[]{:S(2)}) collective-permute-start(bf16[784,384]{1,0:T(8,128)(2,1)S(1)} %add_convert_fusion.2), channel_id=1, source_target_pairs={{8,0},{16,24},{9,1},{17,25},{10,2},{18,26},{11,3},{19,27},{12,4},{... | collective-permute-start | bytes 1806344 | tf_op jit(solution)/shard_map/ppermute | solution.py:495
  179.8 5.1 %collective-permute-start.34 = (f32[4,384]{1,0:T(4,128)S(1)}, f32[4,384]{1,0:T(4,128)S(1)}, u32[]{:S(2)}, u32[]{:S(2)}) collective-permute-start(f32[4,384]{1,0:T(4,128)S(1)} %add.131), channel_id=1, source_target_pairs={{0,16},{8,24},{16,0},{24,8},{1,17},{9,25},{17,1},{25,9},{2,18},{10... | collective-permute-start | bytes 18440 | tf_op jit(solution)/shard_map/ppermute | solution.py:506
  181.1 21.7 %copy-start.25 = (f32[384]{0:T(512)}, f32[384]{0:T(512)S(1)}, u32[]{:S(2)}) copy-start(f32[384]{0:T(512)S(1)} %fusion.9) | copy-start | bytes 4612
  182.3 11.3 %collective-permute-start.32 = (bf16[272,384]{1,0:T(8,128)(2,1)S(1)}, bf16[272,384]{1,0:T(8,128)(2,1)S(1)}, u32[]{:S(2)}, u32[]{:S(2)}) collective-permute-start(bf16[272,384]{1,0:T(8,128)(2,1)S(1)} %add_convert_fusion.12), channel_id=1, source_target_pairs={{8,0},{16,24},{9,1},{17,25},{10,2},{18,26},{11,3},{19,27},{12,4},{... | collective-permute-start | bytes 626696 | tf_op jit(solution)/shard_map/ppermute | solution.py:495
  183.6 16.4 %collective-permute-start.28 = (bf16[544,384]{1,0:T(8,128)(2,1)S(1)}, bf16[544,384]{1,0:T(8,128)(2,1)S(1)}, u32[]{:S(2)}, u32[]{:S(2)}) collective-permute-start(bf16[544,384]{1,0:T(8,128)(2,1)S(1)} %add_convert_fusion.8), channel_id=1, source_target_pairs={{8,0},{16,24},{9,1},{17,25},{10,2},{18,26},{11,3},{19,27},{12,4},{... | collective-permute-start | bytes 1253384 | tf_op jit(solution)/shard_map/ppermute | solution.py:495
  (22 other events, 49.2 us)

commit v4 on v3

--- a/solution.py
+++ b/solution.py
@@ -646,7 +646,6 @@
     norm_sums = dx_k[held : held + 4].astype(F32) + dx_got[held : held + 4].astype(F32)
     rest = norm_sums[:, :half] + swap_row(norm_sums[:, half:])
     rest = swap_sum(rest, "col", n_col, 2)
-    mix_got, dx_got, rest = barrier((mix_got, dx_got, rest))
     mix_parts = reduce_start(mix_got, mix_k)
     dx_parts = reduce_start(dx_got[:held], dx_k[:held])
     if chain:

time: 207 us -> 207 us (level); the launches traced: 203 us -> 206 us
  waiting for transfers between devices: 56.5 us -> 62.8 us
    ppermute x4, waiting for transfers between devices: 10.9 us -> 14.8 us  [dp_outward(): return (total, lax.ppermute(total, 'dp', [(1, 0), (2, 3)]))]
    ppermute x3, starting transfers between devices: 2.64 us -> 0.08 us  [swap_sum(): lax.ppermute(value, axis, [(i, i ^ bit) for i in range(size)])]
    unnamed x68 -> x56, local copies, waits for them, and re-layouts: 5.12 us -> 3.89 us
  transfers between devices with their start and end apart: 35 -> 35, of which waited for: 13 -> 12; matrix products, arithmetic and copies ran while one was open for 10% -> 8% of each run, Pallas kernels for 30% -> 29%
where the time goes in v4:
time: 207 us; the launch traced here: 206 us
  waiting for transfers between devices  62.8 us (30%)
  Pallas kernels  60.3 us (29%)
  starting transfers between devices  53 us (26%)
  other arithmetic  17 us (8%)
  local copies, waits for them, and re-layouts  11.6 us (6%)
    pallas_call x2, Pallas kernels, attn_head(): pl.pallas_call(attn_kernel, grid=(count,), in_specs=specs, out_specs=[per...  28.4 us
    ppermute x4, starting transfers between devices, dp_inward(): return lax.ppermute(value, 'dp', [(0, 1), (3, 2)])  16.6 us
    ppermute x4, waiting for transfers between devices, dp_outward(): return (total, lax.ppermute(total, 'dp', [(1, 0), (2, 3)]))  14.8 us
    pallas_call x1, Pallas kernels, close_layer(): pl.pallas_call(close_kernel, grid_spec=pltpu.PrefetchScalarGridSpec(num_s...  12.7 us
    ppermute x8, starting transfers between devices, swap_row(): return lax.ppermute(value, 'row', [(0, 1), (1, 0)])  12.6 us
    ppermute x8, waiting for transfers between devices, swap_row(): return lax.ppermute(value, 'row', [(0, 1), (1, 0)])  12.5 us
    pallas_call x1, Pallas kernels, mlp_first(): pl.pallas_call(mlp_first_kernel, grid_spec=pltpu.PrefetchScalarGridSpec(n...  10.2 us
    ppermute x2, waiting for transfers between devices, reduce_start(): lax.ppermute(jnp.where(home, low_sum[:, half:], low_sum[:, :half]), GROUP...  10.1 us
  transfers between devices with their start and end apart: 35, of which 12 were waited for; matrix products, arithmetic and copies ran while one was open for 8% of the time, Pallas kernels for 29%

profile of v4, /device:TPU:0, one launch (start us, length us, event | category | flops | bytes accessed | tf_op | source)
XLA Modules:
  0.0 206.1 jit_solution(15959299720102866465)
XLA Ops:
  3.5 3.0 %collective-permute-start.1 = (f32[4,384]{1,0:T(4,128)S(1)}, f32[4,384]{1,0:T(4,128)S(1)}, u32[]{:S(2)}, u32[]{:S(2)}) collective-permute-start(f32[4,384]{1,0:T(4,128)S(1)} %pad_maximum_fusion.5), channel_id=1, source_target_pairs={{0,4},{4,0},{1,5},{5,1},{2,6},{6,2},{3,7},{7,3},{8,12},{12,8},{9,1... | collective-permute-start | bytes 18440 | tf_op jit(solution)/shard_map/ppermute | solution.py:481
  6.5 1.5 collective-permute-start
  8.7 1.3 fusion.16
  10.1 1.1 pad_maximum_fusion
  11.2 3.2 %fusion = (f32[1024,128]{1,0:T(8,128)}, f32[1024,128]{1,0:T(8,128)}, f32[1024,128]{1,0:T(8,128)}) fusion(f32[128]{0:T(128)S(1)} %compare_select_fusion.2, f32[1024]{0:T(1024)S(1)} %dynamic-slice_convert_fusion, pred[128]{0:T(512)(128)(4,1)S(1)} %get-tuple-element.209, pred[128]{0:T(512)(128)(4,1)S(1)} %get-tuple-element.210), kind=kLoop, calls=%fused_computation.19 | loop fusion | flops 524288 | bytes 1577728 | tf_op jit(solution)/shard_map/jit(_where)/select_n | solution.py:553
  14.4 0.9 pad_maximum_fusion.3
  15.9 1.4 collective-permute-done
  17.4 4.3 %collective-permute-start.2 = (bf16[512,384]{1,0:T(8,128)(2,1)}, bf16[512,384]{1,0:T(8,128)(2,1)S(1)}, u32[]{:S(2)}, u32[]{:S(2)}) collective-permute-start(bf16[512,384]{1,0:T(8,128)(2,1)} %collective-permute-done), channel_id=1, source_target_pairs={{0,2},{1,3},{6,4},{7,5},{8,10},{9,11},{14,12},{15,13},{16,18},{17,... | collective-permute-start | bytes 1179656 | tf_op jit(solution)/shard_map/ppermute | solution.py:569
  21.8 2.0 collective-permute-start.8
  23.8 3.6 %collective-permute-done.4 = bf16[512,384]{1,0:T(8,128)(2,1)S(1)} collective-permute-done((bf16[512,384]{1,0:T(8,128)(2,1)S(1)}, bf16[512,384]{1,0:T(8,128)(2,1)S(1)}, u32[]{:S(2)}, u32[]{:S(2)}) %collective-permute-start.4) | collective-permute-done | bytes 393248 | tf_op jit(solution)/shard_map/ppermute | solution.py:567
  27.4 2.6 %collective-permute-start.5 = (bf16[512,384]{1,0:T(8,128)(2,1)S(1)}, bf16[512,384]{1,0:T(8,128)(2,1)S(1)}, u32[]{:S(2)}, u32[]{:S(2)}) collective-permute-start(bf16[512,384]{1,0:T(8,128)(2,1)S(1)} %collective-permute-done.4), channel_id=1, source_target_pairs={{0,2},{1,3},{6,4},{7,5},{8,10},{9,11},{14,12},{15,13},{16,18},{17,... | collective-permute-start | bytes 1179656 | tf_op jit(solution)/shard_map/ppermute | solution.py:571
  30.0 4.1 %collective-permute-done.2 = bf16[512,384]{1,0:T(8,128)(2,1)S(1)} collective-permute-done((bf16[512,384]{1,0:T(8,128)(2,1)}, bf16[512,384]{1,0:T(8,128)(2,1)S(1)}, u32[]{:S(2)}, u32[]{:S(2)}) %collective-permute-start.2) | collective-permute-done | bytes 393248 | tf_op jit(solution)/shard_map/ppermute | solution.py:569
  34.2 1.1 broadcast_select_fusion.5
  35.4 6.2 %collective-permute-done.5 = bf16[512,384]{1,0:T(8,128)(2,1)S(1)} collective-permute-done((bf16[512,384]{1,0:T(8,128)(2,1)S(1)}, bf16[512,384]{1,0:T(8,128)(2,1)S(1)}, u32[]{:S(2)}, u32[]{:S(2)}) %collective-permute-start.5) | collective-permute-done | bytes 393248 | tf_op jit(solution)/shard_map/ppermute | solution.py:571
  43.7 1.2 collective-permute-done.7.go_ref
  44.8 10.2 %mlp_first.1 = (bf16[1024,384]{1,0:T(8,128)(2,1)}, bf16[1024,384]{1,0:T(8,128)(2,1)}, bf16[1024,768]{1,0:T(8,128)(2,1)}, bf16[1024,768]{1,0:T(8,128)(2,1)}, bf16...) custom-call(s32[1]{0:T(128)} %bitcast.core_ref, bf16[512,768]{1,0:T(8,128)(2,1)} %copy-done.3, ...), custom_call_target="tpu_custom_call" | custom-call | flops 1024 | bytes 1024 | tf_op jit(solution)/shard_map/mlp_first/pallas_call | solution.py:185
  55.0 1.5 collective-permute-start.9
  56.5 8.8 %collective-permute-done.8.wi_p.wo_p.wp_ref.dp_ref.got_b = bf16[1536,384]{1,0:T(8,128)(2,1)S(1)} collective-permute-done((bf16[1536,384]{1,0:T(8,128)(2,1)}, bf16[1536,384]{1,0:T(8,128)(2,1)S(1)}, u32[]{:S(2)}, u32[]{:S(2)}) %collective-permute-start.8) | collective-permute-done | bytes 1179680 | tf_op jit(solution)/shard_map/ppermute | solution.py:481
  65.4 1.0 copy-done
  66.4 9.0 %mlp_second.1 = (bf16[1024,384]{1,0:T(8,128)(2,1)}, bf16[1024,384]{1,0:T(8,128)(2,1)}, bf16[784,384]{1,0:T(8,128)(2,1)}, bf16[784,384]{1,0:T(8,128)(2,1)}) custom-call(bf16[1024,768]{1,0:T(8,128)(2,1)} %get-tuple-element.131.x_ref, bf16[1024,768]{1,0:T(8,128)(2,1)} %get-tuple-element.122.go_ref, bf16[384,768]{1,0:T(8,128)(2,1)} %wi_o.5, ...), custom_call_target="tpu_custom_call" | custom-call | flops 1024 | bytes 1024 | tf_op jit(solution)/shard_map/mlp_second/pallas_call | solution.py:217
  76.2 1.0 copy.30.segc_ref
  77.2 17.9 %attn_head.2 = (bf16[2,64,1024]{2,1,0:T(8,128)(2,1)}, bf16[2,1024,192]{2,1,0:T(8,128)(2,1)}, bf16[2,272,384]{2,1,0:T(8,128)(2,1)}, bf16[2,272,384]{2,1,0:T(8,128)(2,1)}) custom-call(bf16[1024,768]{1,0:T(8,128)(2,1)} %get-tuple-element.111.h_ref, bf16[1024,768]{1,0:T(8,128)(2,1)} %get-tuple-element.122.go_ref, bf16[576,384]{1,0:T(8,128)(2,1)} %bitcast.12, ...), custom_call_target="tpu_custom_call" | custom-call | flops 1024 | bytes 1024 | tf_op jit(solution)/shard_map/attn_head/pallas_call | solution.py:338
  95.4 3.7 %collective-permute-start.12 = (bf16[784,384]{1,0:T(8,128)(2,1)S(1)}, bf16[784,384]{1,0:T(8,128)(2,1)S(1)}, u32[]{:S(2)}, u32[]{:S(2)}) collective-permute-start(bf16[784,384]{1,0:T(8,128)(2,1)S(1)} %add_convert_fusion.7), channel_id=1, source_target_pairs={{0,8},{24,16},{1,9},{25,17},{2,10},{26,18},{3,11},{27,19},{4,12},{... | collective-permute-start | bytes 1806344 | tf_op jit(solution)/shard_map/ppermute | solution.py:485
  99.0 2.1 %collective-permute-start.11 = (bf16[2,272,384]{2,1,0:T(8,128)(2,1)S(1)}, bf16[2,272,384]{2,1,0:T(8,128)(2,1)S(1)}, u32[]{:S(2)}, u32[]{:S(2)}) collective-permute-start(bf16[2,272,384]{2,1,0:T(8,128)(2,1)S(1)} %copy-done.26), channel_id=1, source_target_pairs={{0,4},{4,0},{1,5},{5,1},{2,6},{6,2},{3,7},{7,3},{8,12},{12,8},{9,1... | collective-permute-start | bytes 1253384 | tf_op jit(solution)/shard_map/ppermute | solution.py:481
  101.3 1.5 collective-permute-start.13
  102.8 10.5 %attn_head.3 = (bf16[1,64,1024]{2,1,0:T(8,128)(2,1)}, bf16[1,1024,192]{2,1,0:T(8,128)(2,1)}, bf16[1,272,384]{2,1,0:T(8,128)(2,1)}, bf16[1,272,384]{2,1,0:T(8,128)(2,1)}) custom-call(bf16[1024,768]{1,0:T(8,128)(2,1)} %get-tuple-element.111.h_ref, bf16[1024,768]{1,0:T(8,128)(2,1)} %get-tuple-element.122.go_ref, bf16[576,384]{1,0:T(8,128)(2,1)} %bitcast.13, ...), custom_call_target="tpu_custom_call" | custom-call | flops 1024 | bytes 1024 | tf_op jit(solution)/shard_map/attn_head/pallas_call | solution.py:338
  114.4 6.8 %collective-permute-start.14 = (bf16[544,384]{1,0:T(8,128)(2,1)S(1)}, bf16[544,384]{1,0:T(8,128)(2,1)S(1)}, u32[]{:S(2)}, u32[]{:S(2)}) collective-permute-start(bf16[544,384]{1,0:T(8,128)(2,1)S(1)} %bitcast.16), channel_id=1, source_target_pairs={{0,8},{24,16},{1,9},{25,17},{2,10},{26,18},{3,11},{27,19},{4,12},{... | collective-permute-start | bytes 1253384 | tf_op jit(solution)/shard_map/ppermute | solution.py:485
  121.2 12.7 %close_layer.1 = (bf16[512,768]{1,0:T(8,128)(2,1)}, bf16[512,768]{1,0:T(8,128)(2,1)}, bf16[528,768]{1,0:T(8,128)(2,1)}, bf16[528,768]{1,0:T(8,128)(2,1)}) custom-call(s32[1]{0:T(128)} %bitcast.core_ref, bf16[1024,768]{1,0:T(8,128)(2,1)} %get-tuple-element.131.x_ref, bf16[1024,384]{1,0:T(8,128)(2,1)} %get-tuple-element.132.hid_a, ...), custom_call_target="tpu_custom_call" | custom-call | flops 1024 | bytes 1024 | tf_op jit(solution)/shard_map/close_layer/pallas_call | solution.py:451
  134.8 2.0 collective-permute-start.18
  139.2 3.7 %collective-permute-done.18 = bf16[1,272,384]{2,1,0:T(8,128)(2,1)S(1)} collective-permute-done((bf16[1,272,384]{2,1,0:T(8,128)(2,1)}, bf16[1,272,384]{2,1,0:T(8,128)(2,1)S(1)}, u32[]{:S(2)}, u32[]{:S(2)}) %collective-permute-start.18) | collective-permute-done | bytes 208928 | tf_op jit(solution)/shard_map/ppermute | solution.py:481
  142.8 1.3 collective-permute-start.24
  144.4 1.8 collective-permute-start.25
  146.3 4.6 %collective-permute-start.29 = (bf16[272,384]{1,0:T(8,128)(2,1)S(1)}, bf16[272,384]{1,0:T(8,128)(2,1)S(1)}, u32[]{:S(2)}, u32[]{:S(2)}) collective-permute-start(bf16[272,384]{1,0:T(8,128)(2,1)S(1)} %fusion.3), channel_id=1, source_target_pairs={{0,8},{24,16},{1,9},{25,17},{2,10},{26,18},{3,11},{27,19},{4,12},{... | collective-permute-start | bytes 626696 | tf_op jit(solution)/shard_map/ppermute | solution.py:485
  151.3 3.5 %collective-permute-done.26 = f32[4,384]{1,0:T(4,128)S(1)} collective-permute-done((f32[4,384]{1,0:T(4,128)S(1)}, f32[4,384]{1,0:T(4,128)S(1)}, u32[]{:S(2)}, u32[]{:S(2)}) %collective-permute-start.26) | collective-permute-done | bytes 6176 | tf_op jit(solution)/shard_map/ppermute | solution.py:506
  154.9 5.3 %collective-permute-done.27 = f32[4,384]{1,0:T(4,128)S(1)} collective-permute-done((f32[4,384]{1,0:T(4,128)S(1)}, f32[4,384]{1,0:T(4,128)S(1)}, u32[]{:S(2)}, u32[]{:S(2)}) %collective-permute-start.27) | collective-permute-done | bytes 6176 | tf_op jit(solution)/shard_map/ppermute | solution.py:506
  160.2 1.6 collective-permute-start.19
  162.5 3.2 %collective-permute-start.21 = (bf16[512,384]{1,0:T(8,128)(2,1)S(1)}, bf16[512,384]{1,0:T(8,128)(2,1)S(1)}, u32[]{:S(2)}, u32[]{:S(2)}) collective-permute-start(bf16[512,384]{1,0:T(8,128)(2,1)S(1)} %get-tuple-element.189), channel_id=1, source_target_pairs={{0,4},{1,5},{2,0},{3,1},{4,6},{5,7},{6,2},{7,3},{8,12},{9,13},{10,... | collective-permute-start | bytes 1179656 | tf_op jit(solution)/shard_map/ppermute | solution.py:637
  167.3 5.0 %collective-permute-done.19 = bf16[512,384]{1,0:T(8,128)(2,1)S(1)} collective-permute-done((bf16[512,384]{1,0:T(8,128)(2,1)S(1)}, bf16[512,384]{1,0:T(8,128)(2,1)S(1)}, u32[]{:S(2)}, u32[]{:S(2)}) %collective-permute-start.19) | collective-permute-done | bytes 393248 | tf_op jit(solution)/shard_map/ppermute | solution.py:637
  172.3 1.3 collective-permute-start.33
  173.6 5.1 %collective-permute-done.21 = bf16[512,384]{1,0:T(8,128)(2,1)S(1)} collective-permute-done((bf16[512,384]{1,0:T(8,128)(2,1)S(1)}, bf16[512,384]{1,0:T(8,128)(2,1)S(1)}, u32[]{:S(2)}, u32[]{:S(2)}) %collective-permute-start.21) | collective-permute-done | bytes 393248 | tf_op jit(solution)/shard_map/ppermute | solution.py:637
  178.9 1.4 collective-permute-start.28
  180.3 1.1 add_add_fusion
  181.4 1.0 add_convert_fusion.11
  182.6 1.3 collective-permute-start.32
  184.6 14.8 %collective-permute-done.32 = bf16[272,384]{1,0:T(8,128)(2,1)S(1)} collective-permute-done((bf16[272,384]{1,0:T(8,128)(2,1)S(1)}, bf16[272,384]{1,0:T(8,128)(2,1)S(1)}, u32[]{:S(2)}, u32[]{:S(2)}) %collective-permute-start.32) | collective-permute-done | bytes 208928 | tf_op jit(solution)/shard_map/ppermute | solution.py:495
  201.0 1.1 maximum_convert_fusion.1
  202.1 1.1 maximum_convert_fusion
  203.8 1.0 maximum_bitcast_fusion
  (154 shorter events, 19.3 us)
Async XLA Ops:
  2.7 7.3 %copy-start.1 = (bf16[384,576]{0,1:T(8,128)(2,1)S(1)}, bf16[384,576]{0,1:T(8,128)(2,1)}, u32[]{:S(2)}) copy-start(bf16[384,576]{0,1:T(8,128)(2,1)} %param.17) | copy-start | bytes 1327108
  2.7 7.3 %copy-start.5 = (bf16[192,384]{1,0:T(8,128)(2,1)S(1)}, bf16[192,384]{1,0:T(8,128)(2,1)}, u32[]{:S(2)}) copy-start(bf16[192,384]{1,0:T(8,128)(2,1)} %wd_o.1) | copy-start | bytes 442372
  3.5 12.5 %collective-permute-start.1 = (f32[4,384]{1,0:T(4,128)S(1)}, f32[4,384]{1,0:T(4,128)S(1)}, u32[]{:S(2)}, u32[]{:S(2)}) collective-permute-start(f32[4,384]{1,0:T(4,128)S(1)} %pad_maximum_fusion.5), channel_id=1, source_target_pairs={{0,4},{4,0},{1,5},{5,1},{2,6},{6,2},{3,7},{7,3},{8,12},{12,8},{9,1... | collective-permute-start | bytes 18440 | tf_op jit(solution)/shard_map/ppermute | solution.py:481
  6.5 10.9 %collective-permute-start = (bf16[512,384]{1,0:T(8,128)(2,1)}, bf16[512,384]{1,0:T(8,128)(2,1)}, u32[]{:S(2)}, u32[]{:S(2)}) collective-permute-start(bf16[512,384]{1,0:T(8,128)(2,1)} %param.16), channel_id=1, source_target_pairs={{0,2},{1,3},{2,6},{3,7},{4,0},{5,1},{6,4},{7,5},{8,10},{9,11},{10,... | collective-permute-start | bytes 1179656 | tf_op jit(solution)/shard_map/ppermute | solution.py:562
  11.2 23.0 %copy-start.9 = (bf16[512,384]{1,0:T(8,128)(2,1)S(1)}, bf16[512,384]{1,0:T(8,128)(2,1)}, u32[]{:S(2)}) copy-start(bf16[512,384]{1,0:T(8,128)(2,1)} %param.16) | copy-start | bytes 1179652
  15.3 60.8 %copy-start.19 = (s32[1024]{0:T(1024)}, s32[1024]{0:T(1024)S(1)}, u32[]{:S(2)}) copy-start(s32[1024]{0:T(1024)S(1)} %dynamic_slice.7) | copy-start | bytes 12292
  15.3 12.1 %collective-permute-start.4 = (bf16[512,384]{1,0:T(8,128)(2,1)S(1)}, bf16[512,384]{1,0:T(8,128)(2,1)S(1)}, u32[]{:S(2)}, u32[]{:S(2)}) collective-permute-start(bf16[512,384]{1,0:T(8,128)(2,1)S(1)} %copy-done.7), channel_id=1, source_target_pairs={{0,2},{1,3},{2,6},{3,7},{4,0},{5,1},{6,4},{7,5},{8,10},{9,11},{10,... | collective-permute-start | bytes 1179656 | tf_op jit(solution)/shard_map/ppermute | solution.py:567
  17.4 16.8 %collective-permute-start.2 = (bf16[512,384]{1,0:T(8,128)(2,1)}, bf16[512,384]{1,0:T(8,128)(2,1)S(1)}, u32[]{:S(2)}, u32[]{:S(2)}) collective-permute-start(bf16[512,384]{1,0:T(8,128)(2,1)} %collective-permute-done), channel_id=1, source_target_pairs={{0,2},{1,3},{6,4},{7,5},{8,10},{9,11},{14,12},{15,13},{16,18},{17,... | collective-permute-start | bytes 1179656 | tf_op jit(solution)/shard_map/ppermute | solution.py:569
  21.7 19.9 %collective-permute-start.6 = (bf16[768,384]{1,0:T(8,128)(2,1)}, bf16[768,384]{1,0:T(8,128)(2,1)S(1)}, u32[]{:S(2)}, u32[]{:S(2)}) collective-permute-start(bf16[768,384]{1,0:T(8,128)(2,1)} %pad_maximum_fusion.3), channel_id=1, source_target_pairs={{0,4},{4,0},{1,5},{5,1},{2,6},{6,2},{3,7},{7,3},{8,12},{12,8},{9,1... | collective-permute-start | bytes 1769480 | tf_op jit(solution)/shard_map/ppermute | solution.py:481
  21.8 43.6 %collective-permute-start.8 = (bf16[1536,384]{1,0:T(8,128)(2,1)}, bf16[1536,384]{1,0:T(8,128)(2,1)S(1)}, u32[]{:S(2)}, u32[]{:S(2)}) collective-permute-start(bf16[1536,384]{1,0:T(8,128)(2,1)} %pad_maximum_fusion), channel_id=1, source_target_pairs={{0,4},{4,0},{1,5},{5,1},{2,6},{6,2},{3,7},{7,3},{8,12},{12,8},{9,1... | collective-permute-start | bytes 3538952 | tf_op jit(solution)/shard_map/ppermute | solution.py:481
  27.4 14.1 %collective-permute-start.5 = (bf16[512,384]{1,0:T(8,128)(2,1)S(1)}, bf16[512,384]{1,0:T(8,128)(2,1)S(1)}, u32[]{:S(2)}, u32[]{:S(2)}) collective-permute-start(bf16[512,384]{1,0:T(8,128)(2,1)S(1)} %collective-permute-done.4), channel_id=1, source_target_pairs={{0,2},{1,3},{6,4},{7,5},{8,10},{9,11},{14,12},{15,13},{16,18},{17,... | collective-permute-start | bytes 1179656 | tf_op jit(solution)/shard_map/ppermute | solution.py:571
  35.3 6.4 %copy-start.3 = (bf16[512,768]{1,0:T(8,128)(2,1)}, bf16[512,768]{1,0:T(8,128)(2,1)S(1)}, u32[]{:S(2)}) copy-start(bf16[512,768]{1,0:T(8,128)(2,1)S(1)} %pad_maximum_fusion.1.xm_ref) | copy-start | bytes 2359300
  35.3 8.3 %collective-permute-start.3 = (bf16[512,768]{1,0:T(8,128)(2,1)S(1)}, bf16[512,768]{1,0:T(8,128)(2,1)}, u32[]{:S(2)}, u32[]{:S(2)}) collective-permute-start(bf16[512,768]{1,0:T(8,128)(2,1)S(1)} %pad_maximum_fusion.1.xm_ref), channel_id=1, source_target_pairs={{0,1},{1,0},{2,3},{3,2},{4,5},{5,4},{6,7},{7,6},{8,9},{9,8},{10,11... | collective-permute-start | bytes 2359304 | tf_op jit(solution)/shard_map/ppermute | solution.py:573
  42.4 2.4 %collective-permute-start.7 = (bf16[512,768]{1,0:T(8,128)(2,1)S(1)}, bf16[512,768]{1,0:T(8,128)(2,1)}, u32[]{:S(2)}, u32[]{:S(2)}) collective-permute-start(bf16[512,768]{1,0:T(8,128)(2,1)S(1)} %pad_maximum_fusion.2.gm_ref), channel_id=1, source_target_pairs={{0,1},{1,0},{2,3},{3,2},{4,5},{5,4},{6,7},{7,6},{8,9},{9,8},{10,11... | collective-permute-start | bytes 2359304 | tf_op jit(solution)/shard_map/ppermute | solution.py:576
  55.0 40.2 %collective-permute-start.9 = (bf16[784,384]{1,0:T(8,128)(2,1)}, bf16[784,384]{1,0:T(8,128)(2,1)S(1)}, u32[]{:S(2)}, u32[]{:S(2)}) collective-permute-start(bf16[784,384]{1,0:T(8,128)(2,1)} %get-tuple-element.120), channel_id=1, source_target_pairs={{0,4},{4,0},{1,5},{5,1},{2,6},{6,2},{3,7},{7,3},{8,12},{12,8},{9,1... | collective-permute-start | bytes 1806344 | tf_op jit(solution)/shard_map/ppermute | solution.py:481
  66.4 9.1 %copy-start.22 = (f32[576]{0:T(1024)S(1)}, f32[576]{0:T(1024)}, u32[]{:S(2)}) copy-start(f32[576]{0:T(1024)} %param.18) | copy-start | bytes 6916
  75.4 19.8 %collective-permute-start.10 = (bf16[784,384]{1,0:T(8,128)(2,1)}, bf16[784,384]{1,0:T(8,128)(2,1)S(1)}, u32[]{:S(2)}, u32[]{:S(2)}) collective-permute-start(bf16[784,384]{1,0:T(8,128)(2,1)} %get-tuple-element.121), channel_id=1, source_target_pairs={{0,4},{4,0},{1,5},{5,1},{2,6},{6,2},{3,7},{7,3},{8,12},{12,8},{9,1... | collective-permute-start | bytes 1806344 | tf_op jit(solution)/shard_map/ppermute | solution.py:481
  77.2 18.0 %copy-start.15 = (bf16[784,384]{1,0:T(8,128)(2,1)S(1)}, bf16[784,384]{1,0:T(8,128)(2,1)}, u32[]{:S(2)}) copy-start(bf16[784,384]{1,0:T(8,128)(2,1)} %get-tuple-element.129) | copy-start | bytes 1806340
  95.1 6.0 %copy-start.16 = (bf16[784,384]{1,0:T(8,128)(2,1)S(1)}, bf16[784,384]{1,0:T(8,128)(2,1)}, u32[]{:S(2)}) copy-start(bf16[784,384]{1,0:T(8,128)(2,1)} %get-tuple-element.143) | copy-start | bytes 1806340
  95.4 17.9 %collective-permute-start.12 = (bf16[784,384]{1,0:T(8,128)(2,1)S(1)}, bf16[784,384]{1,0:T(8,128)(2,1)S(1)}, u32[]{:S(2)}, u32[]{:S(2)}) collective-permute-start(bf16[784,384]{1,0:T(8,128)(2,1)S(1)} %add_convert_fusion.7), channel_id=1, source_target_pairs={{0,8},{24,16},{1,9},{25,17},{2,10},{26,18},{3,11},{27,19},{4,12},{... | collective-permute-start | bytes 1806344 | tf_op jit(solution)/shard_map/ppermute | solution.py:485
  99.0 14.3 %collective-permute-start.11 = (bf16[2,272,384]{2,1,0:T(8,128)(2,1)S(1)}, bf16[2,272,384]{2,1,0:T(8,128)(2,1)S(1)}, u32[]{:S(2)}, u32[]{:S(2)}) collective-permute-start(bf16[2,272,384]{2,1,0:T(8,128)(2,1)S(1)} %copy-done.26), channel_id=1, source_target_pairs={{0,4},{4,0},{1,5},{5,1},{2,6},{6,2},{3,7},{7,3},{8,12},{12,8},{9,1... | collective-permute-start | bytes 1253384 | tf_op jit(solution)/shard_map/ppermute | solution.py:481
  101.3 32.6 %collective-permute-start.13 = (bf16[784,384]{1,0:T(8,128)(2,1)S(1)}, bf16[784,384]{1,0:T(8,128)(2,1)S(1)}, u32[]{:S(2)}, u32[]{:S(2)}) collective-permute-start(bf16[784,384]{1,0:T(8,128)(2,1)S(1)} %add_convert_fusion.6), channel_id=1, source_target_pairs={{0,8},{24,16},{1,9},{25,17},{2,10},{26,18},{3,11},{27,19},{4,12},{... | collective-permute-start | bytes 1806344 | tf_op jit(solution)/shard_map/ppermute | solution.py:485
  113.5 20.5 %collective-permute-start.15 = (bf16[784,384]{1,0:T(8,128)(2,1)S(1)}, bf16[784,384]{1,0:T(8,128)(2,1)S(1)}, u32[]{:S(2)}, u32[]{:S(2)}) collective-permute-start(bf16[784,384]{1,0:T(8,128)(2,1)S(1)} %add_convert_fusion.5), channel_id=1, source_target_pairs={{8,16},{16,8},{9,17},{17,9},{10,18},{18,10},{11,19},{19,11},{12,20... | collective-permute-start | bytes 1806344 | tf_op jit(solution)/shard_map/ppermute | solution.py:490
  114.4 19.5 %collective-permute-start.14 = (bf16[544,384]{1,0:T(8,128)(2,1)S(1)}, bf16[544,384]{1,0:T(8,128)(2,1)S(1)}, u32[]{:S(2)}, u32[]{:S(2)}) collective-permute-start(bf16[544,384]{1,0:T(8,128)(2,1)S(1)} %bitcast.16), channel_id=1, source_target_pairs={{0,8},{24,16},{1,9},{25,17},{2,10},{26,18},{3,11},{27,19},{4,12},{... | collective-permute-start | bytes 1253384 | tf_op jit(solution)/shard_map/ppermute | solution.py:485
  134.8 9.4 %collective-permute-start.17 = (bf16[528,768]{1,0:T(8,128)(2,1)}, bf16[528,768]{1,0:T(8,128)(2,1)S(1)}, u32[]{:S(2)}, u32[]{:S(2)}) collective-permute-start(bf16[528,768]{1,0:T(8,128)(2,1)} %get-tuple-element.150), channel_id=1, source_target_pairs={{0,1},{1,0},{2,3},{3,2},{4,5},{5,4},{6,7},{7,6},{8,9},{9,8},{10,11... | collective-permute-start | bytes 2433032 | tf_op jit(solution)/shard_map/ppermute | solution.py:629
  134.8 8.0 %collective-permute-start.18 = (bf16[1,272,384]{2,1,0:T(8,128)(2,1)}, bf16[1,272,384]{2,1,0:T(8,128)(2,1)S(1)}, u32[]{:S(2)}, u32[]{:S(2)}) collective-permute-start(bf16[1,272,384]{2,1,0:T(8,128)(2,1)} %get-tuple-element.151), channel_id=1, source_target_pairs={{0,4},{4,0},{1,5},{5,1},{2,6},{6,2},{3,7},{7,3},{8,12},{12,8},{9,1... | collective-permute-start | bytes 626696 | tf_op jit(solution)/shard_map/ppermute | solution.py:481
  136.8 7.3 %collective-permute-start.16 = (bf16[512,768]{1,0:T(8,128)(2,1)}, bf16[512,768]{1,0:T(8,128)(2,1)S(1)}, u32[]{:S(2)}, u32[]{:S(2)}) collective-permute-start(bf16[512,768]{1,0:T(8,128)(2,1)} %get-tuple-element.149), channel_id=1, source_target_pairs={{0,1},{1,0},{2,3},{3,2},{4,5},{5,4},{6,7},{7,6},{8,9},{9,8},{10,11... | collective-permute-start | bytes 2359304 | tf_op jit(solution)/shard_map/ppermute | solution.py:628
  137.1 28.6 %collective-permute-start.23 = (bf16[544,384]{1,0:T(8,128)(2,1)S(1)}, bf16[544,384]{1,0:T(8,128)(2,1)S(1)}, u32[]{:S(2)}, u32[]{:S(2)}) collective-permute-start(bf16[544,384]{1,0:T(8,128)(2,1)S(1)} %add_convert_fusion.9), channel_id=1, source_target_pairs={{8,16},{16,8},{9,17},{17,9},{10,18},{18,10},{11,19},{19,11},{12,20... | collective-permute-start | bytes 1253384 | tf_op jit(solution)/shard_map/ppermute | solution.py:490
  138.1 6.0 %copy-start.12 = (bf16[528,768]{1,0:T(8,128)(2,1)S(1)}, bf16[528,768]{1,0:T(8,128)(2,1)}, u32[]{:S(2)}) copy-start(bf16[528,768]{1,0:T(8,128)(2,1)} %get-tuple-element.153) | copy-start | bytes 2433028
  138.1 23.7 %collective-permute-start.30 = (bf16[784,384]{1,0:T(8,128)(2,1)S(1)}, bf16[784,384]{1,0:T(8,128)(2,1)S(1)}, u32[]{:S(2)}, u32[]{:S(2)}) collective-permute-start(bf16[784,384]{1,0:T(8,128)(2,1)S(1)} %add_convert_fusion.3), channel_id=1, source_target_pairs={{8,16},{16,8},{9,17},{17,9},{10,18},{18,10},{11,19},{19,11},{12,20... | collective-permute-start | bytes 1806344 | tf_op jit(solution)/shard_map/ppermute | solution.py:490
  139.1 7.1 %copy-start.18 = (bf16[1,272,384]{2,1,0:T(8,128)(2,1)S(1)}, bf16[1,272,384]{2,1,0:T(8,128)(2,1)}, u32[]{:S(2)}) copy-start(bf16[1,272,384]{2,1,0:T(8,128)(2,1)} %get-tuple-element.167) | copy-start | bytes 626692
  142.8 23.8 %collective-permute-start.24 = (bf16[784,384]{1,0:T(8,128)(2,1)S(1)}, bf16[784,384]{1,0:T(8,128)(2,1)S(1)}, u32[]{:S(2)}, u32[]{:S(2)}) collective-permute-start(bf16[784,384]{1,0:T(8,128)(2,1)S(1)} %add_convert_fusion.4), channel_id=1, source_target_pairs={{8,0},{16,24},{9,1},{17,25},{10,2},{18,26},{11,3},{19,27},{12,4},{... | collective-permute-start | bytes 1806344 | tf_op jit(solution)/shard_map/ppermute | solution.py:495
  144.1 6.7 %copy-start.11 = (bf16[512,768]{1,0:T(8,128)(2,1)S(1)}, bf16[512,768]{1,0:T(8,128)(2,1)}, u32[]{:S(2)}) copy-start(bf16[512,768]{1,0:T(8,128)(2,1)} %get-tuple-element.140) | copy-start | bytes 2359300
  144.4 6.7 %collective-permute-start.25 = (f32[4,384]{1,0:T(4,128)S(1)}, f32[4,384]{1,0:T(4,128)S(1)}, u32[]{:S(2)}, u32[]{:S(2)}) collective-permute-start(f32[4,384]{1,0:T(4,128)S(1)} %slice.213), channel_id=1, source_target_pairs={{0,4},{4,0},{1,5},{5,1},{2,6},{6,2},{3,7},{7,3},{8,12},{12,8},{9,1... | collective-permute-start | bytes 18440 | tf_op jit(solution)/shard_map/ppermute | solution.py:481
  146.3 16.2 %collective-permute-start.29 = (bf16[272,384]{1,0:T(8,128)(2,1)S(1)}, bf16[272,384]{1,0:T(8,128)(2,1)S(1)}, u32[]{:S(2)}, u32[]{:S(2)}) collective-permute-start(bf16[272,384]{1,0:T(8,128)(2,1)S(1)} %fusion.3), channel_id=1, source_target_pairs={{0,8},{24,16},{1,9},{25,17},{2,10},{26,18},{3,11},{27,19},{4,12},{... | collective-permute-start | bytes 626696 | tf_op jit(solution)/shard_map/ppermute | solution.py:485
  151.1 3.7 %collective-permute-start.26 = (f32[4,384]{1,0:T(4,128)S(1)}, f32[4,384]{1,0:T(4,128)S(1)}, u32[]{:S(2)}, u32[]{:S(2)}) collective-permute-start(f32[4,384]{1,0:T(4,128)S(1)} %slice_add_fusion), channel_id=1, source_target_pairs={{0,2},{1,3},{2,0},{3,1},{4,6},{5,7},{6,4},{7,5},{8,10},{9,11},{10,... | collective-permute-start | bytes 18440 | tf_op jit(solution)/shard_map/ppermute | solution.py:506
  154.8 5.4 %collective-permute-start.27 = (f32[4,384]{1,0:T(4,128)S(1)}, f32[4,384]{1,0:T(4,128)S(1)}, u32[]{:S(2)}, u32[]{:S(2)}) collective-permute-start(f32[4,384]{1,0:T(4,128)S(1)} %add.130), channel_id=1, source_target_pairs={{0,8},{8,0},{16,24},{24,16},{1,9},{9,1},{17,25},{25,17},{2,10},{10... | collective-permute-start | bytes 18440 | tf_op jit(solution)/shard_map/ppermute | solution.py:506
  160.2 12.1 %collective-permute-start.19 = (bf16[512,384]{1,0:T(8,128)(2,1)S(1)}, bf16[512,384]{1,0:T(8,128)(2,1)S(1)}, u32[]{:S(2)}, u32[]{:S(2)}) collective-permute-start(bf16[512,384]{1,0:T(8,128)(2,1)S(1)} %get-tuple-element.192), channel_id=1, source_target_pairs={{0,4},{1,5},{2,0},{3,1},{4,6},{5,7},{6,2},{7,3},{8,12},{9,13},{10,... | collective-permute-start | bytes 1179656 | tf_op jit(solution)/shard_map/ppermute | solution.py:637
  161.8 11.8 %collective-permute-start.20 = (bf16[512,384]{1,0:T(8,128)(2,1)S(1)}, bf16[512,384]{1,0:T(8,128)(2,1)S(1)}, u32[]{:S(2)}, u32[]{:S(2)}) collective-permute-start(bf16[512,384]{1,0:T(8,128)(2,1)S(1)} %get-tuple-element.193), channel_id=1, source_target_pairs={{2,4},{3,5},{4,2},{5,3},{10,12},{11,13},{12,10},{13,11},{18,20},{1... | collective-permute-start | bytes 1179656 | tf_op jit(solution)/shard_map/ppermute | solution.py:640
  162.5 16.2 %collective-permute-start.21 = (bf16[512,384]{1,0:T(8,128)(2,1)S(1)}, bf16[512,384]{1,0:T(8,128)(2,1)S(1)}, u32[]{:S(2)}, u32[]{:S(2)}) collective-permute-start(bf16[512,384]{1,0:T(8,128)(2,1)S(1)} %get-tuple-element.189), channel_id=1, source_target_pairs={{0,4},{1,5},{2,0},{3,1},{4,6},{5,7},{6,2},{7,3},{8,12},{9,13},{10,... | collective-permute-start | bytes 1179656 | tf_op jit(solution)/shard_map/ppermute | solution.py:637
  165.7 13.0 %collective-permute-start.22 = (bf16[512,384]{1,0:T(8,128)(2,1)S(1)}, bf16[512,384]{1,0:T(8,128)(2,1)S(1)}, u32[]{:S(2)}, u32[]{:S(2)}) collective-permute-start(bf16[512,384]{1,0:T(8,128)(2,1)S(1)} %get-tuple-element.190), channel_id=1, source_target_pairs={{2,4},{3,5},{4,2},{5,3},{10,12},{11,13},{12,10},{13,11},{18,20},{1... | collective-permute-start | bytes 1179656 | tf_op jit(solution)/shard_map/ppermute | solution.py:640
  166.4 13.9 %copy-start.8 = (bf16[512,384]{1,0:T(8,128)(2,1)S(1)}, bf16[512,384]{1,0:T(8,128)(2,1)}, u32[]{:S(2)}) copy-start(bf16[512,384]{1,0:T(8,128)(2,1)} %param.31) | copy-start | bytes 1179652
  166.6 15.9 %collective-permute-start.31 = (bf16[272,384]{1,0:T(8,128)(2,1)S(1)}, bf16[272,384]{1,0:T(8,128)(2,1)S(1)}, u32[]{:S(2)}, u32[]{:S(2)}) collective-permute-start(bf16[272,384]{1,0:T(8,128)(2,1)S(1)} %add_convert_fusion.13), channel_id=1, source_target_pairs={{8,16},{16,8},{9,17},{17,9},{10,18},{18,10},{11,19},{19,11},{12,20... | collective-permute-start | bytes 626696 | tf_op jit(solution)/shard_map/ppermute | solution.py:490
  172.3 28.0 %collective-permute-start.33 = (bf16[784,384]{1,0:T(8,128)(2,1)S(1)}, bf16[784,384]{1,0:T(8,128)(2,1)S(1)}, u32[]{:S(2)}, u32[]{:S(2)}) collective-permute-start(bf16[784,384]{1,0:T(8,128)(2,1)S(1)} %add_convert_fusion.2), channel_id=1, source_target_pairs={{8,0},{16,24},{9,1},{17,25},{10,2},{18,26},{11,3},{19,27},{12,4},{... | collective-permute-start | bytes 1806344 | tf_op jit(solution)/shard_map/ppermute | solution.py:495
  178.7 5.2 %collective-permute-start.34 = (f32[4,384]{1,0:T(4,128)S(1)}, f32[4,384]{1,0:T(4,128)S(1)}, u32[]{:S(2)}, u32[]{:S(2)}) collective-permute-start(f32[4,384]{1,0:T(4,128)S(1)} %add.131), channel_id=1, source_target_pairs={{0,16},{8,24},{16,0},{24,8},{1,17},{9,25},{17,1},{25,9},{2,18},{10... | collective-permute-start | bytes 18440 | tf_op jit(solution)/shard_map/ppermute | solution.py:506
  178.9 20.6 %collective-permute-start.28 = (bf16[544,384]{1,0:T(8,128)(2,1)S(1)}, bf16[544,384]{1,0:T(8,128)(2,1)S(1)}, u32[]{:S(2)}, u32[]{:S(2)}) collective-permute-start(bf16[544,384]{1,0:T(8,128)(2,1)S(1)} %add_convert_fusion.8), channel_id=1, source_target_pairs={{8,0},{16,24},{9,1},{17,25},{10,2},{18,26},{11,3},{19,27},{12,4},{... | collective-permute-start | bytes 1253384 | tf_op jit(solution)/shard_map/ppermute | solution.py:495
  181.4 24.1 %copy-start.20 = (f32[384]{0:T(512)}, f32[384]{0:T(512)S(1)}, u32[]{:S(2)}) copy-start(f32[384]{0:T(512)S(1)} %fusion.9) | copy-start | bytes 4612
  182.6 16.7 %collective-permute-start.32 = (bf16[272,384]{1,0:T(8,128)(2,1)S(1)}, bf16[272,384]{1,0:T(8,128)(2,1)S(1)}, u32[]{:S(2)}, u32[]{:S(2)}) collective-permute-start(bf16[272,384]{1,0:T(8,128)(2,1)S(1)} %add_convert_fusion.12), channel_id=1, source_target_pairs={{8,0},{16,24},{9,1},{17,25},{10,2},{18,26},{11,3},{19,27},{12,4},{... | collective-permute-start | bytes 626696 | tf_op jit(solution)/shard_map/ppermute | solution.py:495
  (16 other events, 32.7 us)
